TPU v7x, 32 devices: a whole 2x2x4 slice. The times are simulated.
32 devices in a mesh: seq: 4 (over z), row: 2 (over core), col: 4 (over y, x).
Axes of the slice: x: 2, y: 2, z: 4, core: 2. Of those that a mesh axis runs over, the one named last changes fastest.
Arguments:
- query_input: bfloat16 [2048, 3072], P(('seq', 'row'), 'col'), may hold values from -6 to 6
- key_input: bfloat16 [2048, 3072], P(('seq', 'row'), 'col'), may hold values from -6 to 6
- value_input: bfloat16 [2048, 3072], P(('seq', 'row'), 'col'), may hold values from -6 to 6
- norm_gain: float32 [3072], P('col'), may hold values from 0.1 to 1.9
- out_weight: bfloat16 [3072, 6144], P(('seq', 'row'), 'col'), may hold values from -0.109375 to 0.109375
- out_grad: bfloat16 [2048, 6144], P(('seq', 'row'), 'col'), may hold values from -6 to 6
Outputs:
- projected: bfloat16 [2048, 6144], P(('seq', 'row'), 'col')
- query_grad: bfloat16 [2048, 3072], P(('seq', 'row'), 'col')
- key_grad: bfloat16 [2048, 3072], P(('seq', 'row'), 'col')
- value_grad: bfloat16 [2048, 3072], P(('seq', 'row'), 'col')
All inputs are finite; a program needn't handle non-finite values.
Results may differ from a plain program's by a relative error of at most 0.0049.
Values may be sent and summed in bfloat16 or wider, within the bound.
No kernel may reach another device: no remote copies, remote signals or barrier semaphores. Data moves between devices by JAX's collectives and lax.ppermute only.
A program may use at most 128 MiB of HBM per device.

v0:
```python
import jax
import jax.numpy as jnp
from jax import lax
from jax.sharding import PartitionSpec as P

DH = 128
HG = 6


norm_eps = 1e-05


def carried_in(part, axis, combine, identity, reverse):
    count = lax.axis_size(axis)
    place = lax.axis_index(axis)
    ahead = count - 1 - place if reverse else place
    gathered = lax.all_gather(part, axis)
    state = jnp.zeros_like(part) + jnp.asarray(identity, part.dtype)

    def one(hop, state):
        source = count - 1 - hop if reverse else hop
        return combine(state, lax.dynamic_index_in_dim(gathered, source, 0, False))

    return lax.fori_loop(0, ahead, one, state)


def add_states(earlier, latter):
    return earlier + latter


def chain_states(own_state, backward):
    empty_state = jnp.zeros_like(own_state)
    return carried_in(own_state, ("seq", "row"), add_states, empty_state, backward)


def per_device(query_input, key_input, value_input, norm_gain, out_weight, out_grad):
    highest = lax.Precision.HIGHEST
    score_scale = DH ** (-0.5)
    tok_rows = query_input.shape[0]
    width_loc = query_input.shape[1]
    heads_loc = width_loc // DH
    groups_loc = heads_loc // HG
    query_heads = query_input.reshape(tok_rows, heads_loc, DH)
    key_heads = key_input.reshape(tok_rows, heads_loc, DH)
    value_heads = value_input.reshape(tok_rows, heads_loc, DH)
    query_float = query_heads.astype(jnp.float32)
    key_float = key_heads.astype(jnp.float32)
    value_float = value_heads.astype(jnp.float32)
    row_ids = lax.broadcasted_iota(jnp.int32, (tok_rows, tok_rows), 0)
    col_ids = lax.broadcasted_iota(jnp.int32, (tok_rows, tok_rows), 1)
    causal = (row_ids >= col_ids).astype(jnp.float32)
    own_kv = jnp.einsum("tha,thb->hab", key_heads, value_heads, preferred_element_type=jnp.float32)
    prefix = chain_states(own_kv, False)
    key_scores = (
        jnp.einsum("thd,shd->hts", query_heads, key_heads, preferred_element_type=jnp.float32)
        * causal
    )
    attend = jnp.einsum("hts,shd->thd", key_scores, value_float, precision=highest)
    attend = attend + jnp.einsum("thd,hde->the", query_float, prefix, precision=highest)
    attend = (attend * score_scale).reshape(tok_rows, groups_loc, HG * DH)
    inv_rms = lax.rsqrt(jnp.mean(attend * attend, axis=-1, keepdims=True) + norm_eps)
    normed = attend * inv_rms
    gain_groups = norm_gain.reshape(groups_loc, HG * DH)
    normalized = (normed * gain_groups).astype(jnp.bfloat16).reshape(tok_rows, width_loc)
    weight_panel = lax.all_gather(out_weight, ("seq", "row"), axis=0, tiled=True)
    projected = jnp.dot(
        lax.all_gather(normalized, "col", axis=1, tiled=True),
        weight_panel,
        preferred_element_type=jnp.float32,
    )
    grad_parts = lax.dot_general(
        out_grad, weight_panel, (((1,), (1,)), ((), ())), preferred_element_type=jnp.float32
    )
    grad_norm = lax.psum_scatter(grad_parts, "col", scatter_dimension=1, tiled=True)
    scaled = grad_norm.reshape(tok_rows, groups_loc, HG * DH) * gain_groups
    grad_attend = inv_rms * (scaled - normed * jnp.mean(scaled * normed, axis=-1, keepdims=True))
    grad_heads = grad_attend.reshape(tok_rows, heads_loc, DH)
    own_qg = jnp.einsum("tha,thb->hab", query_float, grad_heads, precision=highest)
    suffix = chain_states(own_qg, True)
    value_scores = jnp.einsum("thd,shd->hts", grad_heads, value_float, precision=highest) * causal
    query_part = jnp.einsum("hts,shd->thd", value_scores, key_float, precision=highest)
    query_part = query_part + jnp.einsum("the,hde->thd", grad_heads, prefix, precision=highest)
    key_part = jnp.einsum("hts,thd->shd", value_scores, query_float, precision=highest)
    key_part = key_part + jnp.einsum("shb,hab->sha", value_float, suffix, precision=highest)
    value_part = jnp.einsum("hts,the->she", key_scores, grad_heads, precision=highest)
    value_part = value_part + jnp.einsum("sha,hab->shb", key_float, suffix, precision=highest)
    query_grad = (query_part * score_scale).reshape(tok_rows, width_loc).astype(jnp.bfloat16)
    key_grad = (key_part * score_scale).reshape(tok_rows, width_loc).astype(jnp.bfloat16)
    value_grad = (value_part * score_scale).reshape(tok_rows, width_loc).astype(jnp.bfloat16)
    return (projected.astype(jnp.bfloat16), query_grad, key_grad, value_grad)


def solution(mesh):
    in_specs = (
        P(("seq", "row"), "col"),
        P(("seq", "row"), "col"),
        P(("seq", "row"), "col"),
        P("col"),
        P(("seq", "row"), "col"),
        P(("seq", "row"), "col"),
    )
    out_specs = (
        P(("seq", "row"), "col"),
        P(("seq", "row"), "col"),
        P(("seq", "row"), "col"),
        P(("seq", "row"), "col"),
    )
    return jax.shard_map(
        per_device, mesh=mesh, in_specs=in_specs, out_specs=out_specs, check_vma=False
    )
```

profile of v0, /device:TPU:0, one launch (start us, length us, event | category | flops | bytes accessed | tf_op | source)
XLA Modules:
  0.0 280.8 jit_solution(1814047832965972491)
XLA Ops:
  7.2 0.0 copy-start
  7.2 0.0 copy-start.12
  7.2 0.0 all-gather.9.cloned.1.call-start
  7.2 0.7 all-gather.9.cloned.1.call-update
  7.9 0.0 all-gather.11.cloned.1.call-start
  8.0 1.2 copy.55
  9.1 0.0 copy-done.12
  9.2 0.0 copy-start.2
  9.2 0.2 copy.58
  9.3 0.0 copy-start.6
  9.3 1.0 fusion.11
  10.4 0.0 all-gather.11.cloned.1.call-update
  10.4 0.0 reduce-scatter.2.cloned.1.call-start
  10.4 92.7 %all-gather.9.cloned.1.call-done = bf16[3072,1536]{1,0:T(8,128)(2,1)} async-done(((bf16[384,1536]{1,0:T(8,128)(2,1)}), bf16[3072,1536]{1,0:T(8,128)(2,1)}) %all-gather.9.cloned.1.call-update) | async-done | bytes 9437200 | tf_op jit(solution)/shard_map/all_gather | solution.py:65
  103.1 8.0 %fusion.12 = f32[256,3072]{1,0:T(8,128)} fusion(bf16[256,1536]{1,0:T(8,128)(2,1)S(1)} %copy-done, bf16[3072,1536]{1,0:T(8,128)(2,1)} %all-gather.9.cloned.1.call-done), kind=kOutput, calls=%fused_computation.32 | convolution fusion | flops 2415919104 | bytes 13369344 | tf_op jit(solution)/shard_map/dot_general | solution.py:71
  111.1 0.0 reduce-scatter.2.cloned.1.call-update
  111.1 0.0 all-gather.7.cloned.1.call-start
  111.2 0.9 copy-done.13
  112.1 0.2 copy.54
  112.3 0.8 copy-done.11
  113.1 0.4 convolution_multiply_fusion.1
  113.5 1.9 convolution_bitcast_fusion.5
  115.4 26.7 %all-gather.11.cloned.1.call-done = f32[48,128,128]{2,1,0:T(8,128)} async-done(((f32[6,128,128]{2,1,0:T(8,128)}), f32[48,128,128]{2,1,0:T(8,128)}) %all-gather.11.cloned.1.call-update) | async-done | bytes 3145744 | tf_op jit(solution)/shard_map/all_gather | solution.py:17
  142.2 0.0 copy-start.14
  142.2 2.6 multiply_reduce_fusion.1
  144.8 1.4 copy.62
  146.2 41.8 %reduce-scatter.2.cloned.1.call-done = f32[256,768]{1,0:T(8,128)} async-done(((f32[256,3072]{1,0:T(8,128)}), f32[256,768]{1,0:T(8,128)}) %reduce-scatter.2.cloned.1.call-update) | async-done | bytes 786448 | tf_op jit(solution)/shard_map/reduce_scatter | solution.py:74
  188.0 1.4 multiply_reduce_fusion
  189.4 0.0 copy-done.8
  189.4 1.2 subtract_multiply_fusion
  190.7 0.0 all-gather.7.cloned.1.call-update
  190.7 0.2 all-gather.13.cloned.1.call-start
  190.9 1.4 copy.63
  192.3 2.2 convolution_bitcast_fusion.6
  194.6 1.9 copy.68
  196.5 0.0 all-gather.13.cloned.1.call-update
  196.5 0.0 copy-start.3
  196.5 2.0 convolution_multiply_fusion
  198.5 0.0 copy-done.3
  198.5 0.0 copy-start.1
  198.5 1.0 convolution_bitcast_fusion.4
  199.6 1.6 fusion.9
  201.1 1.9 copy.72
  203.0 3.1 %convolution_bitcast_fusion.3 = f32[256,6,128]{0,2,1:T(8,128)} fusion(f32[6,256,256]{2,1,0:T(8,128)} %copy-done.1, bf16[256,6,128]{0,2,1:T(8,128)(2,1)} %bitcast.89), kind=kOutput, calls=%fused_computation.16 | convolution fusion | flops 603979776 | bytes 2752512 | tf_op jit(solution)/shard_map/hts,thd->shd/dot_general | solution.py:83
  206.1 2.0 fusion.13
  208.0 13.8 %all-gather.7.cloned.1.call-done = bf16[256,3072]{1,0:T(8,128)(2,1)} async-done(((bf16[256,768]{1,0:T(8,128)(2,1)}), bf16[256,3072]{1,0:T(8,128)(2,1)}) %all-gather.7.cloned.1.call-update) | async-done | bytes 1572880 | tf_op jit(solution)/shard_map/all_gather | solution.py:67
  221.8 7.6 %convolution_convert_fusion = bf16[256,1536]{1,0:T(8,128)(2,1)} fusion(bf16[256,3072]{1,0:T(8,128)(2,1)} %all-gather.7.cloned.1.call-done, bf16[3072,1536]{1,0:T(8,128)(2,1)} %all-gather.9.cloned.1.call-done), kind=kOutput, calls=%fused_computation.2 | convolution fusion | flops 2416312320 | bytes 11796480 | tf_op jit(solution)/shard_map/dot_general | solution.py:66
  229.5 32.2 %all-gather.13.cloned.1.call-done = f32[48,128,128]{2,1,0:T(8,128)} async-done(((f32[6,128,128]{2,1,0:T(8,128)}), f32[48,128,128]{2,1,0:T(8,128)}) %all-gather.13.cloned.1.call-update) | async-done | bytes 3145744 | tf_op jit(solution)/shard_map/all_gather | solution.py:17
  261.6 0.0 copy-start.4
  261.7 0.0 copy-start.10
  261.7 7.9 %while.23 = (s32[]{:T(128)}, f32[6,128,128]{2,1,0:T(8,128)S(1)}, s32[]{:T(128)}, f32[8,6,128,128]{3,2,1,0:T(8,128)}, s32[]{:T(128)}, /*index=5*/s32[]{:T(128)}, s32[]{:T(128)}, s32[]{:T(128)}) while((s32[]{:T(128)}, f32[6,128,128]{2,1,0:T(8,128)S(1)}, s32[]{:T(128)}, f32[8,6,128,128]{3,2,1,0:T(8,128)}, s32[]{:T(128)}, /*index=5*/s32[]{:T(128)}, ...), condition=%wide.region_6.7_spmd, body=%wide.region_5.6_spmd.sunk | while | flops 98310 | bytes 1179783 | solution.py:24
  261.7 1.2 bitcast_add_fusion.5
  262.9 1.1 bitcast_add_fusion.5
  264.0 1.1 bitcast_add_fusion.5
  265.1 1.1 bitcast_add_fusion.5
  266.3 1.1 bitcast_add_fusion.5
  267.4 1.1 bitcast_add_fusion.5
  268.5 1.1 bitcast_add_fusion.5
  269.6 0.0 copy-start.7
  269.7 1.3 fusion.7
  270.9 1.9 copy.74
  272.8 0.0 copy-done.9
  272.9 0.5 fusion.8
  273.3 0.9 copy.73
  (20 shorter events, 0.1 us)
Async XLA Ops:
  7.2 96.0 %copy-start = (bf16[256,1536]{1,0:T(8,128)(2,1)S(1)}, bf16[256,1536]{1,0:T(8,128)(2,1)}, u32[]{:S(2)}) copy-start(bf16[256,1536]{1,0:T(8,128)(2,1)} %param.15) | copy-start | bytes 2359300
  7.2 2.0 copy-start.12
  7.2 95.9 %all-gather.9.cloned.1.call-start = ((), (), s32[]{:S(2)}) async-start(), calls=%async_computation.2 | async-start | bytes 10616832 | tf_op jit(solution)/shard_map/all_gather | solution.py:65
  7.9 134.2 %all-gather.11.cloned.1.call-start = ((), (), s32[]{:S(2)}) async-start(), calls=%async_computation.4 | async-start | bytes 3538944 | tf_op jit(solution)/shard_map/all_gather | solution.py:17
  9.2 103.2 %copy-start.2 = (bf16[256,768]{0,1:T(8,128)(2,1)}, bf16[256,768]{0,1:T(8,128)(2,1)S(1)}, u32[]{:S(2)}) copy-start(bf16[256,768]{0,1:T(8,128)(2,1)S(1)} %copy.55) | copy-start | bytes 1179652
  9.3 104.2 %copy-start.6 = (bf16[256,768]{0,1:T(8,128)(2,1)}, bf16[256,768]{0,1:T(8,128)(2,1)S(1)}, u32[]{:S(2)}) copy-start(bf16[256,768]{0,1:T(8,128)(2,1)S(1)} %copy.58) | copy-start | bytes 1179652
  10.4 177.6 %reduce-scatter.2.cloned.1.call-start = ((), (), s32[]{:S(2)}) async-start(), calls=%async_computation.3 | async-start | bytes 3932160 | tf_op jit(solution)/shard_map/reduce_scatter | solution.py:74
  111.1 1.0 copy-start.13
  111.1 110.7 %all-gather.7.cloned.1.call-start = ((), (), s32[]{:S(2)}) async-start(), calls=%async_computation.1 | async-start | bytes 1966080 | tf_op jit(solution)/shard_map/all_gather | solution.py:67
  112.3 29.9 %copy-start.5 = (bf16[256,768]{0,1:T(8,128)(2,1)}, bf16[256,768]{0,1:T(8,128)(2,1)S(1)}, u32[]{:S(2)}) copy-start(bf16[256,768]{0,1:T(8,128)(2,1)S(1)} %copy.54) | copy-start | bytes 1179652
  112.3 0.8 copy-start.11
  142.2 45.8 %copy-start.14 = (f32[768]{0:T(1024)S(1)}, f32[768]{0:T(1024)}, u32[]{:S(2)}) copy-start(f32[768]{0:T(1024)} %param.13) | copy-start | bytes 9220
  188.0 1.4 copy-start.8
  190.7 70.9 %all-gather.13.cloned.1.call-start = ((), (), s32[]{:S(2)}) async-start(), calls=%async_computation.5 | async-start | bytes 3538944 | tf_op jit(solution)/shard_map/all_gather | solution.py:17
  196.5 2.0 copy-start.3
  198.5 2.6 copy-start.1
  261.6 8.0 %copy-start.4 = (bf16[256,768]{0,1:T(8,128)(2,1)S(1)}, bf16[256,768]{0,1:T(8,128)(2,1)}, u32[]{:S(2)}) copy-start(bf16[256,768]{0,1:T(8,128)(2,1)} %copy-done.2) | copy-start | bytes 1179652
  261.7 8.0 %copy-start.10 = (f32[6,128,256]{2,1,0:T(8,128)S(1)}, f32[6,128,256]{2,1,0:T(8,128)}, u32[]{:S(2)}) copy-start(f32[6,128,256]{2,1,0:T(8,128)} %fusion.13) | copy-start | bytes 2359300
  269.6 3.2 %copy-start.7 = (bf16[256,768]{0,1:T(8,128)(2,1)S(1)}, bf16[256,768]{0,1:T(8,128)(2,1)}, u32[]{:S(2)}) copy-start(bf16[256,768]{0,1:T(8,128)(2,1)} %copy-done.6) | copy-start | bytes 1179652
  269.6 3.2 %copy-start.9 = (f32[256,6,128]{0,2,1:T(8,128)S(1)}, f32[256,6,128]{0,2,1:T(8,128)}, u32[]{:S(2)}) copy-start(f32[256,6,128]{0,2,1:T(8,128)} %convolution_bitcast_fusion.3) | copy-start | bytes 2359300
Sparse Core Ops, SparseCore 0:
  9.7 93.4 all-gather.8
  105.3 36.7 all-gather.10
  145.1 42.8 reduce-scatter.1
  190.8 30.9 all-gather.6
  223.3 38.2 all-gather.12
where the time goes:
time: 282 us; the launch traced here: 281 us
  waiting for transfers between devices  208 us (74%)
  matrix products  35.1 us (12%)
  between operations  14.1 us (5%)
  local copies, waits for them, and re-layouts  12.8 us (5%)
  other arithmetic  10.5 us (4%)
    all_gather x1, waiting for transfers between devices, per_device(): lax.all_gather(out_weight, ('seq', 'row'), axis=0, tiled=True)  92.7 us
    all_gather x2, waiting for transfers between devices, carried_in(): gathered = lax.all_gather(part, axis)  58.9 us
    reduce_scatter x1, waiting for transfers between devices, per_device(): lax.psum_scatter(grad_parts, 'col', scatter_dimension=1, tiled=True)  41.8 us
    all_gather x1, waiting for transfers between devices, per_device(): lax.all_gather(normalized, 'col', axis=1, tiled=True)  13.8 us
    unnamed x36, local copies, waits for them, and re-layouts  8 us
    dot_general x1, matrix products, per_device(): lax.dot_general(out_grad, weight_panel, (((1,), (1,)), ((), ())), preferr...  7.95 us
    add x7, other arithmetic, add_states(): return earlier + latter  7.75 us
    dot_general x1, matrix products, per_device(): jnp.dot(lax.all_gather(normalized, 'col', axis=1, tiled=True), weight_pan...  7.64 us
  transfers between devices with their start and end apart: 5, of which 5 were waited for; matrix products, arithmetic and copies ran while one was open for 15% of the time, Pallas kernels for 0%

commit v1 on v0

v1 whole, which is shorter than its diff:
```python
import jax
import jax.numpy as jnp
from jax import lax
from jax.sharding import PartitionSpec as P

DH = 128
HG = 6
CHUNK_HEADS = (1, 1, 1)

norm_eps = 1e-05
bf16 = jnp.bfloat16
f32 = jnp.float32


def carried_in(part, axis, reverse):
    count = lax.axis_size(axis)
    place = lax.axis_index(axis)
    gathered = lax.all_gather(part, axis)
    order = jnp.arange(count)
    keep = (order > place) if reverse else (order < place)
    return jnp.tensordot(keep.astype(f32), gathered, 1, precision=lax.Precision.HIGHEST)


def general(query_input, key_input, value_input, norm_gain, out_weight, out_grad):
    highest = lax.Precision.HIGHEST
    score_scale = DH ** (-0.5)
    tok_rows = query_input.shape[0]
    width_loc = query_input.shape[1]
    heads_loc = width_loc // DH
    groups_loc = heads_loc // HG
    query_heads = query_input.reshape(tok_rows, heads_loc, DH)
    key_heads = key_input.reshape(tok_rows, heads_loc, DH)
    value_heads = value_input.reshape(tok_rows, heads_loc, DH)
    query_float = query_heads.astype(f32)
    key_float = key_heads.astype(f32)
    value_float = value_heads.astype(f32)
    row_ids = lax.broadcasted_iota(jnp.int32, (tok_rows, tok_rows), 0)
    col_ids = lax.broadcasted_iota(jnp.int32, (tok_rows, tok_rows), 1)
    causal = (row_ids >= col_ids).astype(f32)
    own_kv = jnp.einsum("tha,thb->hab", key_heads, value_heads, preferred_element_type=f32)
    prefix = carried_in(own_kv, ("seq", "row"), False)
    key_scores = (
        jnp.einsum("thd,shd->hts", query_heads, key_heads, preferred_element_type=f32) * causal
    )
    attend = jnp.einsum("hts,shd->thd", key_scores, value_float, precision=highest)
    attend = attend + jnp.einsum("thd,hde->the", query_float, prefix, precision=highest)
    attend = (attend * score_scale).reshape(tok_rows, groups_loc, HG * DH)
    inv_rms = lax.rsqrt(jnp.mean(attend * attend, axis=-1, keepdims=True) + norm_eps)
    normed = attend * inv_rms
    gain_groups = norm_gain.reshape(groups_loc, HG * DH)
    normalized = (normed * gain_groups).astype(bf16).reshape(tok_rows, width_loc)
    weight_panel = lax.all_gather(out_weight, ("seq", "row"), axis=0, tiled=True)
    projected = jnp.dot(
        lax.all_gather(normalized, "col", axis=1, tiled=True),
        weight_panel,
        preferred_element_type=f32,
    )
    grad_parts = lax.dot_general(
        out_grad, weight_panel, (((1,), (1,)), ((), ())), preferred_element_type=f32
    )
    grad_norm = lax.psum_scatter(grad_parts, "col", scatter_dimension=1, tiled=True)
    scaled = grad_norm.reshape(tok_rows, groups_loc, HG * DH) * gain_groups
    grad_attend = inv_rms * (scaled - normed * jnp.mean(scaled * normed, axis=-1, keepdims=True))
    grad_heads = grad_attend.reshape(tok_rows, heads_loc, DH)
    own_qg = jnp.einsum("tha,thb->hab", query_float, grad_heads, precision=highest)
    suffix = carried_in(own_qg, ("seq", "row"), True)
    value_scores = jnp.einsum("thd,shd->hts", grad_heads, value_float, precision=highest) * causal
    query_part = jnp.einsum("hts,shd->thd", value_scores, key_float, precision=highest)
    query_part = query_part + jnp.einsum("the,hde->thd", grad_heads, prefix, precision=highest)
    key_part = jnp.einsum("hts,thd->shd", value_scores, query_float, precision=highest)
    key_part = key_part + jnp.einsum("shb,hab->sha", value_float, suffix, precision=highest)
    value_part = jnp.einsum("hts,the->she", key_scores, grad_heads, precision=highest)
    value_part = value_part + jnp.einsum("sha,hab->shb", key_float, suffix, precision=highest)
    query_grad = (query_part * score_scale).reshape(tok_rows, width_loc).astype(bf16)
    key_grad = (key_part * score_scale).reshape(tok_rows, width_loc).astype(bf16)
    value_grad = (value_part * score_scale).reshape(tok_rows, width_loc).astype(bf16)
    return (projected.astype(bf16), query_grad, key_grad, value_grad)


def row_swap(x):
    return lax.ppermute(x, "row", [(0, 1), (1, 0)])


def col_flip(x, bits):
    return lax.ppermute(x, "col", [(i, i ^ bits) for i in range(lax.axis_size("col"))])


def seq_shift(x, step):
    count = lax.axis_size("seq")
    return lax.ppermute(x, "seq", [(i, i + step) for i in range(count) if 0 <= i + step < count])


def seq_rotate(x):
    count = lax.axis_size("seq")
    return lax.ppermute(x, "seq", [(i, (i + 1) % count) for i in range(count)])


def sum_of_shifts(state, sign):
    sent = state.astype(bf16)
    total = jnp.zeros(state.shape, f32)
    for hop in range(1, lax.axis_size("seq")):
        total = total + seq_shift(sent, sign * hop).astype(f32)
    return total


def dot(spec, a, b):
    return jnp.einsum(spec, a.astype(bf16), b.astype(bf16), preferred_element_type=f32)


def head_split(query_input, key_input, value_input, norm_gain, out_weight, out_grad):
    score_scale = DH ** (-0.5)
    tok = query_input.shape[0]
    width = query_input.shape[1]
    half = width // 2
    heads = half // DH
    n_seq = lax.axis_size("seq")
    n_col = lax.axis_size("col")
    z = lax.axis_index("seq")
    r = lax.axis_index("row")
    c = lax.axis_index("col")

    held = []
    start = 0
    for count in CHUNK_HEADS:
        rows = count * DH
        blocks = [out_weight[start : start + rows]]
        for _ in range(n_seq - 1):
            blocks.append(seq_rotate(blocks[-1]))
        held.append(blocks)
        start += rows

    def halves_swapped(x):
        return jnp.concatenate([x[tok:], x[:tok]])

    def mine(x):
        return lax.dynamic_slice_in_dim(x, r * half, half, 1)

    def other(x):
        return lax.dynamic_slice_in_dim(x, (1 - r) * half, half, 1)

    qkv = (query_input, key_input, value_input)
    got = row_swap(jnp.stack([other(x) for x in qkv]))
    q, k, v = [
        jnp.concatenate([mine(x), got[i]], 0).reshape(2 * tok, heads, DH) for i, x in enumerate(qkv)
    ]
    grads = jnp.concatenate([out_grad, row_swap(out_grad)], 0)
    gain = lax.dynamic_slice_in_dim(norm_gain, r * half, half, 0)

    place = lax.broadcasted_iota(jnp.int32, (2 * tok, 1), 0)
    place = jnp.where(place < tok, place + r * tok, place - tok + (1 - r) * tok)
    causal = place >= place.reshape(1, 2 * tok)

    own_kv = dot("tha,thb->hab", k, v)
    prefix = sum_of_shifts(own_kv, 1)
    key_scores = jnp.where(causal, dot("thd,shd->hts", q, k), 0.0).astype(bf16)
    attend = dot("hts,shd->thd", key_scores, v) + dot("thd,hde->the", q, prefix)
    attend = attend.reshape(2 * tok, half) * score_scale
    squares = jnp.sum(attend * attend, axis=-1)
    squares = squares + halves_swapped(row_swap(squares))
    inv_rms = lax.rsqrt(squares * (1.0 / width) + norm_eps)[:, None]
    normed = attend * inv_rms
    normalized = (normed * gain).astype(bf16)

    pieces = []
    start = 0
    for count, blocks in zip(CHUNK_HEADS, held):
        parts = [
            lax.dot_general(grads, w, (((1,), (1,)), ((), ())), preferred_element_type=f32)
            for w in blocks
        ]

        def group(g):
            out = parts[0]
            for s in range(1, n_seq):
                out = jnp.where((z - g) % n_seq == s, parts[s], out)
            return out

        piece = group(c)
        for bits in range(1, n_col):
            piece = piece + col_flip(group(c ^ bits).astype(bf16), bits).astype(f32)
        pieces.append(piece)
        start += count
    grad_norm = jnp.concatenate(pieces, 1)

    feats = [normalized] + [col_flip(normalized, bits) for bits in range(1, n_col)]

    def features(g):
        out = feats[0]
        for bits in range(1, n_col):
            out = jnp.where(c ^ g == bits, feats[bits], out)
        return out

    partial = 0.0
    for s in range(n_seq):
        weight = jnp.concatenate([blocks[s] for blocks in held], 0)
        partial = partial + jnp.dot(
            features((z - s) % n_seq), weight, preferred_element_type=f32
        )
    projected = (partial[:tok] + row_swap(partial[tok:])).astype(bf16)

    scaled = grad_norm * gain
    inner = jnp.sum(scaled * normed, axis=-1)
    inner = (inner + halves_swapped(row_swap(inner)))[:, None] * (1.0 / width)
    grad_attend = inv_rms * (scaled - normed * inner)
    g = grad_attend.reshape(2 * tok, heads, DH).astype(bf16)

    suffix = sum_of_shifts(dot("tha,thb->hab", q, g), -1)
    value_scores = jnp.where(causal, dot("thd,shd->hts", g, v), 0.0).astype(bf16)
    query_part = dot("hts,shd->thd", value_scores, k) + dot("the,hde->thd", g, prefix)
    key_part = dot("hts,thd->shd", value_scores, q) + dot("shb,hab->sha", v, suffix)
    value_part = dot("hts,the->she", key_scores, g) + dot("sha,hab->shb", k, suffix)

    def settle(parts):
        whole = [(x * score_scale).reshape(2 * tok, half).astype(bf16) for x in parts]
        back = row_swap(jnp.stack([x[tok:] for x in whole]))
        return [
            jnp.where(
                r == 0,
                jnp.concatenate([x[:tok], y], 1),
                jnp.concatenate([y, x[:tok]], 1),
            )
            for x, y in zip(whole, back)
        ]

    (query_grad,) = settle([query_part])
    key_grad, value_grad = settle([key_part, value_part])
    return (projected, query_grad, key_grad, value_grad)


def solution(mesh):
    sizes = dict(mesh.shape)

    def per_device(query_input, key_input, value_input, norm_gain, out_weight, out_grad):
        width = query_input.shape[1]
        fits = (
            sizes["row"] == 2
            and sizes["seq"] == sizes["col"] == 4
            and width == HG * DH
            and 2 * out_weight.shape[0] == width
        )
        plan = head_split if fits else general
        return plan(query_input, key_input, value_input, norm_gain, out_weight, out_grad)

    in_specs = (
        P(("seq", "row"), "col"),
        P(("seq", "row"), "col"),
        P(("seq", "row"), "col"),
        P("col"),
        P(("seq", "row"), "col"),
        P(("seq", "row"), "col"),
    )
    out_specs = (
        P(("seq", "row"), "col"),
        P(("seq", "row"), "col"),
        P(("seq", "row"), "col"),
        P(("seq", "row"), "col"),
    )
    return jax.shard_map(
        per_device, mesh=mesh, in_specs=in_specs, out_specs=out_specs, check_vma=False
    )
```

time: 282 us -> 143 us (0.51)
  waiting for transfers between devices: 208 us -> 54.3 us
  starting transfers between devices: 0.38 us -> 45.4 us
  matrix products: 35.1 us -> 21.4 us
  between operations: 14.1 us -> 1.46 us
    all_gather x4 -> x0, waiting for transfers between devices: 165 us -> none  [the longest x1 92.7 us: per_device(): lax.all_gather(out_weight, ('seq', 'row'), axis=0, tiled=True)]
    ppermute x0 -> x34, waiting for transfers between devices: none -> 54.3 us  [the longest x9 26.3 us: seq_rotate(): return lax.ppermute(x, 'seq', [(i, (i + 1) % count) for i in range(count)])]
    ppermute x0 -> x34, starting transfers between devices: none -> 45.4 us  [the longest x6 16.2 us: seq_shift(): lax.ppermute(x, 'seq', [(i, i + step) for i in range(count) if 0 <= i + s...]
    reduce_scatter x1 -> x0, waiting for transfers between devices: 41.8 us -> none  [per_device(): lax.psum_scatter(grad_parts, 'col', scatter_dimension=1, tiled=True)]
    dot_general x14 -> x28, matrix products: 35.1 us -> 21.4 us  [the longest x12 10.7 us: head_split(): lax.dot_general(grads, w, (((1,), (1,)), ((), ())), preferred_element_typ...]
    add x7 -> x0, other arithmetic: 7.75 us -> none  [add_states(): return earlier + latter]
    slice x0 -> x14, local copies, waits for them, and re-layouts: none -> 4.87 us  [the longest x1 2.36 us: head_split(): blocks = [out_weight[start:start + rows]]]
    unnamed x36 -> x61, local copies, waits for them, and re-layouts: 8 us -> 4.59 us
  transfers between devices with their start and end apart: 5 -> 34, of which waited for: 5 -> 14; matrix products, arithmetic and copies ran while one was open for 15% -> 23% of each run, Pallas kernels for 0% -> 0%
where the time goes in v1:
time: 143 us
  waiting for transfers between devices  54.3 us (38%)
  starting transfers between devices  45.4 us (32%)
  matrix products  21.4 us (15%)
  local copies, waits for them, and re-layouts  12.2 us (9%)
  other arithmetic  7.9 us (6%)
  between operations  1.46 us (1%)
    ppermute x9, waiting for transfers between devices, seq_rotate(): return lax.ppermute(x, 'seq', [(i, (i + 1) % count) for i in range(count)])  26.3 us
    ppermute x6, waiting for transfers between devices, seq_shift(): lax.ppermute(x, 'seq', [(i, i + step) for i in range(count) if 0 <= i + s...  21.1 us
    ppermute x6, starting transfers between devices, seq_shift(): lax.ppermute(x, 'seq', [(i, i + step) for i in range(count) if 0 <= i + s...  16.2 us
    ppermute x12, starting transfers between devices, col_flip(): lax.ppermute(x, 'col', [(i, i ^ bits) for i in range(lax.axis_size('col'))])  15.3 us
    ppermute x9, starting transfers between devices, seq_rotate(): return lax.ppermute(x, 'seq', [(i, (i + 1) % count) for i in range(count)])  12.5 us
    dot_general x12, matrix products, head_split(): lax.dot_general(grads, w, (((1,), (1,)), ((), ())), preferred_element_typ...  10.7 us
    ppermute x12, waiting for transfers between devices, col_flip(): lax.ppermute(x, 'col', [(i, i ^ bits) for i in range(lax.axis_size('col'))])  6.12 us
    dot_general x4, matrix products, head_split(): jnp.dot(features((z - s) % n_seq), weight, preferred_element_type=f32)  5.62 us
  transfers between devices with their start and end apart: 34, of which 14 were waited for; matrix products, arithmetic and copies ran while one was open for 23% of the time, Pallas kernels for 0%

profile of v1, /device:TPU:0, one launch (start us, length us, event | category | flops | bytes accessed | tf_op | source)
XLA Modules:
  0.0 142.7 jit_solution(17227417624050734354)
XLA Ops:
  0.7 2.4 %fusion.75 = (bf16[128,1536]{1,0:T(8,128)(2,1)}, bf16[128,1536]{1,0:T(8,128)(2,1)}, bf16[128,1536]{1,0:T(8,128)(2,1)}) fusion(bf16[384,1536]{1,0:T(8,128)(2,1)} %param.10), kind=kLoop, calls=%fused_computation.128 | loop fusion | bytes 2359296 | tf_op jit(solution)/shard_map/slice | solution.py:126
  3.0 3.0 %collective-permute-start.8 = (bf16[128,1536]{1,0:T(8,128)(2,1)}, bf16[128,1536]{1,0:T(8,128)(2,1)}, u32[]{:S(2)}, u32[]{:S(2)}) collective-permute-start(bf16[128,1536]{1,0:T(8,128)(2,1)} %get-tuple-element.6), channel_id=1, source_target_pairs={{0,8},{8,16},{16,24},{24,0},{1,9},{9,17},{17,25},{25,1},{2,10},{10... | collective-permute-start | bytes 1179656 | tf_op jit(solution)/shard_map/ppermute | solution.py:95
  6.0 1.6 %collective-permute-start.9 = (bf16[128,1536]{1,0:T(8,128)(2,1)}, bf16[128,1536]{1,0:T(8,128)(2,1)}, u32[]{:S(2)}, u32[]{:S(2)}) collective-permute-start(bf16[128,1536]{1,0:T(8,128)(2,1)} %get-tuple-element.8), channel_id=1, source_target_pairs={{0,8},{8,16},{16,24},{24,0},{1,9},{9,17},{17,25},{25,1},{2,10},{10... | collective-permute-start | bytes 1179656 | tf_op jit(solution)/shard_map/ppermute | solution.py:95
  7.6 1.6 %collective-permute-start.10 = (bf16[128,1536]{1,0:T(8,128)(2,1)}, bf16[128,1536]{1,0:T(8,128)(2,1)}, u32[]{:S(2)}, u32[]{:S(2)}) collective-permute-start(bf16[128,1536]{1,0:T(8,128)(2,1)} %get-tuple-element.7), channel_id=1, source_target_pairs={{0,8},{8,16},{16,24},{24,0},{1,9},{9,17},{17,25},{25,1},{2,10},{10... | collective-permute-start | bytes 1179656 | tf_op jit(solution)/shard_map/ppermute | solution.py:95
  9.4 0.9 pad_maximum_fusion
  11.3 1.0 broadcast_compare_fusion
  12.2 1.2 constant_dynamic-update-slice_fusion.1
  14.3 2.0 %collective-permute-start.1 = (bf16[3,128,128]{2,1,0:T(8,128)(2,1)S(1)}, bf16[3,128,128]{2,1,0:T(8,128)(2,1)S(1)}, u32[]{:S(2)}, u32[]{:S(2)}) collective-permute-start(bf16[3,128,128]{2,1,0:T(8,128)(2,1)S(1)} %convolution_convert_fusion.1), channel_id=1, source_target_pairs={{0,8},{8,16},{16,24},{1,9},{9,17},{17,25},{2,10},{10,18},{18,26},{... | collective-permute-start | bytes 294920 | tf_op jit(solution)/shard_map/ppermute | solution.py:90
  16.3 4.7 %collective-permute-start.2 = (bf16[3,128,128]{2,1,0:T(8,128)(2,1)S(1)}, bf16[3,128,128]{2,1,0:T(8,128)(2,1)S(1)}, u32[]{:S(2)}, u32[]{:S(2)}) collective-permute-start(bf16[3,128,128]{2,1,0:T(8,128)(2,1)S(1)} %convolution_convert_fusion.1), channel_id=1, source_target_pairs={{0,16},{8,24},{1,17},{9,25},{2,18},{10,26},{3,19},{11,27},{4,20},{... | collective-permute-start | bytes 294920 | tf_op jit(solution)/shard_map/ppermute | solution.py:90
  21.3 0.6 select_convert_fusion.1
  21.9 12.7 %collective-permute-done.1 = bf16[3,128,128]{2,1,0:T(8,128)(2,1)S(1)} collective-permute-done((bf16[3,128,128]{2,1,0:T(8,128)(2,1)S(1)}, bf16[3,128,128]{2,1,0:T(8,128)(2,1)S(1)}, u32[]{:S(2)}, u32[]{:S(2)}) %collective-permute-start.1) | collective-permute-done | bytes 98336 | tf_op jit(solution)/shard_map/ppermute | solution.py:90
  34.6 5.7 %collective-permute-start.3 = (bf16[3,128,128]{2,1,0:T(8,128)(2,1)S(1)}, bf16[3,128,128]{2,1,0:T(8,128)(2,1)S(1)}, u32[]{:S(2)}, u32[]{:S(2)}) collective-permute-start(bf16[3,128,128]{2,1,0:T(8,128)(2,1)S(1)} %convolution_convert_fusion.1), channel_id=1, source_target_pairs={{0,24},{1,25},{2,26},{3,27},{4,28},{5,29},{6,30},{7,31}} | collective-permute-start | bytes 294920 | tf_op jit(solution)/shard_map/ppermute | solution.py:90
  40.4 0.6 fusion.67
  41.2 1.4 collective-permute-done.3
  42.6 0.6 copy-done.21
  44.0 5.1 %collective-permute-start.13 = (bf16[128,1536]{1,0:T(8,128)(2,1)}, bf16[128,1536]{1,0:T(8,128)(2,1)S(1)}, u32[]{:S(2)}, u32[]{:S(2)}) collective-permute-start(bf16[128,1536]{1,0:T(8,128)(2,1)} %collective-permute-done.10), channel_id=1, source_target_pairs={{0,8},{8,16},{16,24},{24,0},{1,9},{9,17},{17,25},{25,1},{2,10},{10... | collective-permute-start | bytes 1179656 | tf_op jit(solution)/shard_map/ppermute | solution.py:95
  49.3 2.5 %collective-permute-start.5 = (bf16[512,384]{0,1:T(8,128)(2,1)S(1)}, bf16[512,384]{0,1:T(8,128)(2,1)S(1)}, u32[]{:S(2)}, u32[]{:S(2)}) collective-permute-start(bf16[512,384]{0,1:T(8,128)(2,1)S(1)} %fusion.31), channel_id=1, source_target_pairs={{0,3},{1,2},{2,1},{3,0},{4,7},{5,6},{6,5},{7,4},{8,11},{9,10},{10,... | collective-permute-start | bytes 1179656 | tf_op jit(solution)/shard_map/ppermute | solution.py:85
  52.3 1.2 constant_dynamic-update-slice_fusion
  53.5 0.6 fusion.72
  54.2 0.6 fusion.70
  54.8 0.6 fusion.68
  55.5 1.6 %fusion.83 = f32[512,128]{0,1:T(8,128)S(1)} fusion(bf16[512,1536]{1,0:T(8,128)(2,1)S(1)} %constant_dynamic-update-slice_fusion, bf16[128,1536]{1,0:T(8,128)(2,1)} %collective-permute-done.8), kind=kOutput, calls=%fused_computation.136 | convolution fusion | flops 201326592 | bytes 2228224 | tf_op jit(solution)/shard_map/dot_general | solution.py:168
  57.1 1.6 %fusion.85 = f32[512,128]{0,1:T(8,128)S(1)} fusion(bf16[512,1536]{1,0:T(8,128)(2,1)S(1)} %constant_dynamic-update-slice_fusion, bf16[128,1536]{1,0:T(8,128)(2,1)} %collective-permute-done.9), kind=kOutput, calls=%fused_computation.138 | convolution fusion | flops 201326592 | bytes 2228224 | tf_op jit(solution)/shard_map/dot_general | solution.py:168
  58.7 1.6 %fusion.87 = f32[512,128]{0,1:T(8,128)S(1)} fusion(bf16[512,1536]{1,0:T(8,128)(2,1)S(1)} %constant_dynamic-update-slice_fusion, bf16[128,1536]{1,0:T(8,128)(2,1)} %collective-permute-done.10), kind=kOutput, calls=%fused_computation.140 | convolution fusion | flops 201326592 | bytes 2228224 | tf_op jit(solution)/shard_map/dot_general | solution.py:168
  61.0 0.6 fusion.82
  61.6 5.0 %collective-permute-done.12 = bf16[128,1536]{1,0:T(8,128)(2,1)S(1)} collective-permute-done((bf16[128,1536]{1,0:T(8,128)(2,1)}, bf16[128,1536]{1,0:T(8,128)(2,1)S(1)}, u32[]{:S(2)}, u32[]{:S(2)}) %collective-permute-start.12) | collective-permute-done | bytes 393248 | tf_op jit(solution)/shard_map/ppermute | solution.py:95
  66.6 0.6 fusion.84
  67.2 7.8 %collective-permute-done.13 = bf16[128,1536]{1,0:T(8,128)(2,1)S(1)} collective-permute-done((bf16[128,1536]{1,0:T(8,128)(2,1)}, bf16[128,1536]{1,0:T(8,128)(2,1)S(1)}, u32[]{:S(2)}, u32[]{:S(2)}) %collective-permute-start.13) | collective-permute-done | bytes 393248 | tf_op jit(solution)/shard_map/ppermute | solution.py:95
  75.0 0.6 fusion.86
  75.7 1.0 collective-permute-start.16
  76.6 2.3 %fusion.12 = f32[512,1536]{1,0:T(8,128)S(1)} fusion(bf16[128,1536]{1,0:T(8,128)(2,1)} %collective-permute-done.10, bf16[128,1536]{1,0:T(8,128)(2,1)} %collective-permute-done.9, bf16[128,1536]{1,0:T(8,128)(2,1)} %collective-permute-done.8, bf16[512,384]{0,1:T(8,128)(2,1)S(1)} %collective-permute-done.5, bf16[512,384]{0,1:T(8,128)(2,1)S(1)} %collective-permute-done.6, ...), kind=kOutput, calls=%fused_computation.20 | convolution fusion | flops 608108544 | bytes 5898243 | tf_op jit(solution)/shard_map/dot_general | solution.py:196
  78.9 1.1 fusion.18
  80.0 3.4 %collective-permute-done.14 = bf16[128,1536]{1,0:T(8,128)(2,1)S(1)} collective-permute-done((bf16[128,1536]{1,0:T(8,128)(2,1)S(1)}, bf16[128,1536]{1,0:T(8,128)(2,1)S(1)}, u32[]{:S(2)}, u32[]{:S(2)}) %collective-permute-start.14) | collective-permute-done | bytes 393248 | tf_op jit(solution)/shard_map/ppermute | solution.py:95
  83.4 0.6 select_convert_fusion.10
  84.1 1.6 %collective-permute-start.19 = (bf16[512,128]{0,1:T(8,128)(2,1)S(1)}, bf16[512,128]{0,1:T(8,128)(2,1)S(1)}, u32[]{:S(2)}, u32[]{:S(2)}) collective-permute-start(bf16[512,128]{0,1:T(8,128)(2,1)S(1)} %get-tuple-element.9), channel_id=1, source_target_pairs={{0,1},{1,0},{2,3},{3,2},{4,5},{5,4},{6,7},{7,6},{8,9},{9,8},{10,11... | collective-permute-start | bytes 393224 | tf_op jit(solution)/shard_map/ppermute | solution.py:85
  85.7 1.5 %collective-permute-start.20 = (bf16[512,128]{0,1:T(8,128)(2,1)S(1)}, bf16[512,128]{0,1:T(8,128)(2,1)S(1)}, u32[]{:S(2)}, u32[]{:S(2)}) collective-permute-start(bf16[512,128]{0,1:T(8,128)(2,1)S(1)} %get-tuple-element.11), channel_id=1, source_target_pairs={{0,2},{1,3},{2,0},{3,1},{4,6},{5,7},{6,4},{7,5},{8,10},{9,11},{10,... | collective-permute-start | bytes 393224 | tf_op jit(solution)/shard_map/ppermute | solution.py:85
  87.7 4.2 %collective-permute-done.15 = bf16[128,1536]{1,0:T(8,128)(2,1)S(1)} collective-permute-done((bf16[128,1536]{1,0:T(8,128)(2,1)S(1)}, bf16[128,1536]{1,0:T(8,128)(2,1)S(1)}, u32[]{:S(2)}, u32[]{:S(2)}) %collective-permute-start.15) | collective-permute-done | bytes 393248 | tf_op jit(solution)/shard_map/ppermute | solution.py:95
  91.9 0.7 select_convert_fusion.7
  92.5 1.5 %collective-permute-start.22 = (bf16[512,128]{0,1:T(8,128)(2,1)S(1)}, bf16[512,128]{0,1:T(8,128)(2,1)S(1)}, u32[]{:S(2)}, u32[]{:S(2)}) collective-permute-start(bf16[512,128]{0,1:T(8,128)(2,1)S(1)} %get-tuple-element.12), channel_id=1, source_target_pairs={{0,1},{1,0},{2,3},{3,2},{4,5},{5,4},{6,7},{7,6},{8,9},{9,8},{10,11... | collective-permute-start | bytes 393224 | tf_op jit(solution)/shard_map/ppermute | solution.py:85
  94.1 5.9 %collective-permute-done.16 = bf16[128,1536]{1,0:T(8,128)(2,1)S(1)} collective-permute-done((bf16[128,1536]{1,0:T(8,128)(2,1)S(1)}, bf16[128,1536]{1,0:T(8,128)(2,1)S(1)}, u32[]{:S(2)}, u32[]{:S(2)}) %collective-permute-start.16) | collective-permute-done | bytes 393248 | tf_op jit(solution)/shard_map/ppermute | solution.py:95
  100.0 1.5 %collective-permute-start.23 = (bf16[512,128]{0,1:T(8,128)(2,1)S(1)}, bf16[512,128]{0,1:T(8,128)(2,1)S(1)}, u32[]{:S(2)}, u32[]{:S(2)}) collective-permute-start(bf16[512,128]{0,1:T(8,128)(2,1)S(1)} %get-tuple-element.14), channel_id=1, source_target_pairs={{0,2},{1,3},{2,0},{3,1},{4,6},{5,7},{6,4},{7,5},{8,10},{9,11},{10,... | collective-permute-start | bytes 393224 | tf_op jit(solution)/shard_map/ppermute | solution.py:85
  101.5 1.1 fusion.24
  102.6 0.7 select_convert_fusion.4
  103.3 1.5 %collective-permute-start.24 = (bf16[512,128]{0,1:T(8,128)(2,1)S(1)}, bf16[512,128]{0,1:T(8,128)(2,1)S(1)}, u32[]{:S(2)}, u32[]{:S(2)}) collective-permute-start(bf16[512,128]{0,1:T(8,128)(2,1)S(1)} %get-tuple-element.13), channel_id=1, source_target_pairs={{0,3},{1,2},{2,1},{3,0},{4,7},{5,6},{6,5},{7,4},{8,11},{9,10},{10,... | collective-permute-start | bytes 393224 | tf_op jit(solution)/shard_map/ppermute | solution.py:85
  105.3 1.5 %collective-permute-start.26 = (bf16[512,128]{0,1:T(8,128)(2,1)S(1)}, bf16[512,128]{0,1:T(8,128)(2,1)S(1)}, u32[]{:S(2)}, u32[]{:S(2)}) collective-permute-start(bf16[512,128]{0,1:T(8,128)(2,1)S(1)} %get-tuple-element.17), channel_id=1, source_target_pairs={{0,2},{1,3},{2,0},{3,1},{4,6},{5,7},{6,4},{7,5},{8,10},{9,11},{10,... | collective-permute-start | bytes 393224 | tf_op jit(solution)/shard_map/ppermute | solution.py:85
  107.0 1.5 %collective-permute-start.27 = (bf16[512,128]{0,1:T(8,128)(2,1)S(1)}, bf16[512,128]{0,1:T(8,128)(2,1)S(1)}, u32[]{:S(2)}, u32[]{:S(2)}) collective-permute-start(bf16[512,128]{0,1:T(8,128)(2,1)S(1)} %get-tuple-element.16), channel_id=1, source_target_pairs={{0,3},{1,2},{2,1},{3,0},{4,7},{5,6},{6,5},{7,4},{8,11},{9,10},{10,... | collective-permute-start | bytes 393224 | tf_op jit(solution)/shard_map/ppermute | solution.py:85
  108.5 2.2 %collective-permute-done.24 = bf16[512,128]{0,1:T(8,128)(2,1)S(1)} collective-permute-done((bf16[512,128]{0,1:T(8,128)(2,1)S(1)}, bf16[512,128]{0,1:T(8,128)(2,1)S(1)}, u32[]{:S(2)}, u32[]{:S(2)}) %collective-permute-start.24) | collective-permute-done | bytes 131104 | tf_op jit(solution)/shard_map/ppermute | solution.py:85
  110.9 1.6 %collective-permute-done.25 = bf16[512,128]{0,1:T(8,128)(2,1)S(1)} collective-permute-done((bf16[512,128]{0,1:T(8,128)(2,1)S(1)}, bf16[512,128]{0,1:T(8,128)(2,1)S(1)}, u32[]{:S(2)}, u32[]{:S(2)}) %collective-permute-start.25) | collective-permute-done | bytes 131104 | tf_op jit(solution)/shard_map/ppermute | solution.py:85
  112.4 1.0 collective-permute-done.26
  113.4 1.4 collective-permute-done.27
  115.2 1.2 fusion.1
  116.4 1.4 %slice.95 = f32[256,1536]{1,0:T(8,128)} slice(f32[512,1536]{1,0:T(8,128)S(1)} %fusion.1), slice={[256:512], [0:1536]} | slice | bytes 3145728 | tf_op jit(solution)/shard_map/slice | solution.py:199
  117.8 0.7 copy-done
  119.7 0.7 select_convert_fusion
  121.0 1.3 collective-permute-start.30
  122.3 1.3 collective-permute-start.31
  123.6 1.3 collective-permute-start.32
  126.3 0.7 fusion.65
  128.1 6.4 %collective-permute-done.31 = bf16[3,128,128]{2,1,0:T(8,128)(2,1)S(1)} collective-permute-done((bf16[3,128,128]{2,1,0:T(8,128)(2,1)S(1)}, bf16[3,128,128]{2,1,0:T(8,128)(2,1)S(1)}, u32[]{:S(2)}, u32[]{:S(2)}) %collective-permute-start.31) | collective-permute-done | bytes 98336 | tf_op jit(solution)/shard_map/ppermute | solution.py:90
  136.9 0.7 collective-permute-done.29
  137.6 0.8 maximum_select_fusion
  138.5 0.8 maximum_select_fusion.2
  139.4 0.8 maximum_select_fusion.1
  140.2 2.5 %fusion.2 = bf16[256,1536]{1,0:T(8,128)(2,1)} fusion(f32[256,1536]{1,0:T(8,128)} %collective-permute-done.17, f32[512,1536]{1,0:T(8,128)S(1)} %copy-done.1), kind=kLoop, calls=%fused_computation.6 | loop fusion | flops 786432 | bytes 3932160 | tf_op jit(solution)/shard_map/convert_element_type | solution.py:199
  (137 shorter events, 12.6 us)
Async XLA Ops:
  0.6 8.6 %copy-start.23 = (bf16[256,768]{1,0:T(8,128)(2,1)S(1)}, bf16[256,768]{1,0:T(8,128)(2,1)}, u32[]{:S(2)}) copy-start(bf16[256,768]{1,0:T(8,128)(2,1)} %param.8) | copy-start | bytes 1179652
  0.6 8.6 %copy-start.25 = (bf16[256,768]{1,0:T(8,128)(2,1)S(1)}, bf16[256,768]{1,0:T(8,128)(2,1)}, u32[]{:S(2)}) copy-start(bf16[256,768]{1,0:T(8,128)(2,1)} %param.6) | copy-start | bytes 1179652
  0.7 8.6 %copy-start.24 = (bf16[256,768]{1,0:T(8,128)(2,1)S(1)}, bf16[256,768]{1,0:T(8,128)(2,1)}, u32[]{:S(2)}) copy-start(bf16[256,768]{1,0:T(8,128)(2,1)} %param.7) | copy-start | bytes 1179652
  3.0 40.7 %collective-permute-start.8 = (bf16[128,1536]{1,0:T(8,128)(2,1)}, bf16[128,1536]{1,0:T(8,128)(2,1)}, u32[]{:S(2)}, u32[]{:S(2)}) collective-permute-start(bf16[128,1536]{1,0:T(8,128)(2,1)} %get-tuple-element.6), channel_id=1, source_target_pairs={{0,8},{8,16},{16,24},{24,0},{1,9},{9,17},{17,25},{25,1},{2,10},{10... | collective-permute-start | bytes 1179656 | tf_op jit(solution)/shard_map/ppermute | solution.py:95
  6.0 37.8 %collective-permute-start.9 = (bf16[128,1536]{1,0:T(8,128)(2,1)}, bf16[128,1536]{1,0:T(8,128)(2,1)}, u32[]{:S(2)}, u32[]{:S(2)}) collective-permute-start(bf16[128,1536]{1,0:T(8,128)(2,1)} %get-tuple-element.8), channel_id=1, source_target_pairs={{0,8},{8,16},{16,24},{24,0},{1,9},{9,17},{17,25},{25,1},{2,10},{10... | collective-permute-start | bytes 1179656 | tf_op jit(solution)/shard_map/ppermute | solution.py:95
  7.6 36.4 %collective-permute-start.10 = (bf16[128,1536]{1,0:T(8,128)(2,1)}, bf16[128,1536]{1,0:T(8,128)(2,1)}, u32[]{:S(2)}, u32[]{:S(2)}) collective-permute-start(bf16[128,1536]{1,0:T(8,128)(2,1)} %get-tuple-element.7), channel_id=1, source_target_pairs={{0,8},{8,16},{16,24},{24,0},{1,9},{9,17},{17,25},{25,1},{2,10},{10... | collective-permute-start | bytes 1179656 | tf_op jit(solution)/shard_map/ppermute | solution.py:95
  9.3 1.0 copy-start.28
  10.3 3.1 %collective-permute-start = (bf16[3,256,384]{2,1,0:T(8,128)(2,1)}, bf16[3,256,384]{2,1,0:T(8,128)(2,1)S(1)}, u32[]{:S(2)}, u32[]{:S(2)}) collective-permute-start(bf16[3,256,384]{2,1,0:T(8,128)(2,1)} %pad_maximum_fusion), channel_id=1, source_target_pairs={{0,4},{4,0},{1,5},{5,1},{2,6},{6,2},{3,7},{7,3},{8,12},{12,8},{9,1... | collective-permute-start | bytes 1769480 | tf_op jit(solution)/shard_map/ppermute | solution.py:81
  10.7 31.8 %copy-start.9 = (bf16[256,3,128]{2,0,1:T(8,128)(2,1)}, bf16[256,3,128]{2,0,1:T(8,128)(2,1)S(1)}, u32[]{:S(2)}) copy-start(bf16[256,3,128]{2,0,1:T(8,128)(2,1)S(1)} %copy.36) | copy-start | bytes 589828
  11.1 10.2 %copy-start.5 = (bf16[256,3,128]{2,0,1:T(8,128)(2,1)}, bf16[256,3,128]{2,0,1:T(8,128)(2,1)S(1)}, u32[]{:S(2)}) copy-start(bf16[256,3,128]{2,0,1:T(8,128)(2,1)S(1)} %copy.40) | copy-start | bytes 589828
  11.2 29.2 %copy-start.7 = (bf16[256,384]{0,1:T(8,128)(2,1)}, bf16[256,384]{0,1:T(8,128)(2,1)S(1)}, u32[]{:S(2)}) copy-start(bf16[256,384]{0,1:T(8,128)(2,1)S(1)} %copy.32) | copy-start | bytes 589828
  13.6 7.6 %copy-start.26 = (pred[512,512]{1,0:T(8,128)(4,1)S(1)}, pred[512,512]{1,0:T(8,128)(4,1)}, u32[]{:S(2)}) copy-start(pred[512,512]{1,0:T(8,128)(4,1)} %broadcast_compare_fusion) | copy-start | bytes 786436
  13.8 8.1 %copy-start.11 = (bf16[256,3,128]{2,0,1:T(8,128)(2,1)}, bf16[256,3,128]{2,0,1:T(8,128)(2,1)S(1)}, u32[]{:S(2)}) copy-start(bf16[256,3,128]{2,0,1:T(8,128)(2,1)S(1)} %copy.41) | copy-start | bytes 589828
  14.0 26.4 %copy-start.13 = (bf16[1,256,384]{1,2,0:T(8,128)(2,1)}, bf16[1,256,384]{1,2,0:T(8,128)(2,1)S(1)}, u32[]{:S(2)}) copy-start(bf16[1,256,384]{1,2,0:T(8,128)(2,1)S(1)} %copy.33) | copy-start | bytes 589828
  14.3 20.3 %collective-permute-start.1 = (bf16[3,128,128]{2,1,0:T(8,128)(2,1)S(1)}, bf16[3,128,128]{2,1,0:T(8,128)(2,1)S(1)}, u32[]{:S(2)}, u32[]{:S(2)}) collective-permute-start(bf16[3,128,128]{2,1,0:T(8,128)(2,1)S(1)} %convolution_convert_fusion.1), channel_id=1, source_target_pairs={{0,8},{8,16},{16,24},{1,9},{9,17},{17,25},{2,10},{10,18},{18,26},{... | collective-permute-start | bytes 294920 | tf_op jit(solution)/shard_map/ppermute | solution.py:90
  16.3 24.8 %collective-permute-start.2 = (bf16[3,128,128]{2,1,0:T(8,128)(2,1)S(1)}, bf16[3,128,128]{2,1,0:T(8,128)(2,1)S(1)}, u32[]{:S(2)}, u32[]{:S(2)}) collective-permute-start(bf16[3,128,128]{2,1,0:T(8,128)(2,1)S(1)} %convolution_convert_fusion.1), channel_id=1, source_target_pairs={{0,16},{8,24},{1,17},{9,25},{2,18},{10,26},{3,19},{11,27},{4,20},{... | collective-permute-start | bytes 294920 | tf_op jit(solution)/shard_map/ppermute | solution.py:90
  21.3 21.3 %copy-start.15 = (bf16[256,3,128]{2,0,1:T(8,128)(2,1)}, bf16[256,3,128]{2,0,1:T(8,128)(2,1)S(1)}, u32[]{:S(2)}) copy-start(bf16[256,3,128]{2,0,1:T(8,128)(2,1)S(1)} %copy.37) | copy-start | bytes 589828
  21.9 21.7 %copy-start.3 = (bf16[3,512,512]{2,1,0:T(8,128)(2,1)}, bf16[3,512,512]{2,1,0:T(8,128)(2,1)S(1)}, u32[]{:S(2)}) copy-start(bf16[3,512,512]{2,1,0:T(8,128)(2,1)S(1)} %select_convert_fusion.1) | copy-start | bytes 4718596
  34.6 7.9 %copy-start.17 = (bf16[3,128,128]{2,1,0:T(8,128)(2,1)}, bf16[3,128,128]{2,1,0:T(8,128)(2,1)S(1)}, u32[]{:S(2)}) copy-start(bf16[3,128,128]{2,1,0:T(8,128)(2,1)S(1)} %collective-permute-done.1) | copy-start | bytes 294916
  34.6 7.9 %collective-permute-start.3 = (bf16[3,128,128]{2,1,0:T(8,128)(2,1)S(1)}, bf16[3,128,128]{2,1,0:T(8,128)(2,1)S(1)}, u32[]{:S(2)}, u32[]{:S(2)}) collective-permute-start(bf16[3,128,128]{2,1,0:T(8,128)(2,1)S(1)} %convolution_convert_fusion.1), channel_id=1, source_target_pairs={{0,24},{1,25},{2,26},{3,27},{4,28},{5,29},{6,30},{7,31}} | collective-permute-start | bytes 294920 | tf_op jit(solution)/shard_map/ppermute | solution.py:90
  41.1 1.5 %copy-start.19 = (bf16[3,128,128]{2,1,0:T(8,128)(2,1)}, bf16[3,128,128]{2,1,0:T(8,128)(2,1)S(1)}, u32[]{:S(2)}) copy-start(bf16[3,128,128]{2,1,0:T(8,128)(2,1)S(1)} %collective-permute-done.2) | copy-start | bytes 294916
  41.1 10.8 %collective-permute-start.18 = (bf16[256,1536]{1,0:T(8,128)(2,1)}, bf16[256,1536]{1,0:T(8,128)(2,1)}, u32[]{:S(2)}, u32[]{:S(2)}) collective-permute-start(bf16[256,1536]{1,0:T(8,128)(2,1)} %param.11), channel_id=1, source_target_pairs={{0,4},{4,0},{1,5},{5,1},{2,6},{6,2},{3,7},{7,3},{8,12},{12,8},{9,1... | collective-permute-start | bytes 2359304 | tf_op jit(solution)/shard_map/ppermute | solution.py:81
  42.6 0.6 copy-start.21
  43.6 9.9 %copy-start.2 = (bf16[384,1536]{1,0:T(8,128)(2,1)S(1)}, bf16[384,1536]{1,0:T(8,128)(2,1)}, u32[]{:S(2)}) copy-start(bf16[384,1536]{1,0:T(8,128)(2,1)} %param.10) | copy-start | bytes 3538948
  43.6 5.6 %collective-permute-start.4 = (f32[512]{0:T(512)S(1)}, f32[512]{0:T(512)S(1)}, u32[]{:S(2)}, u32[]{:S(2)}) collective-permute-start(f32[512]{0:T(512)S(1)} %get-tuple-element.39), channel_id=1, source_target_pairs={{0,4},{4,0},{1,5},{5,1},{2,6},{6,2},{3,7},{7,3},{8,12},{12,8},{9,1... | collective-permute-start | bytes 6152 | tf_op jit(solution)/shard_map/ppermute | solution.py:81
  43.7 16.6 %collective-permute-start.11 = (bf16[128,1536]{1,0:T(8,128)(2,1)}, bf16[128,1536]{1,0:T(8,128)(2,1)S(1)}, u32[]{:S(2)}, u32[]{:S(2)}) collective-permute-start(bf16[128,1536]{1,0:T(8,128)(2,1)} %collective-permute-done.8), channel_id=1, source_target_pairs={{0,8},{8,16},{16,24},{24,0},{1,9},{9,17},{17,25},{25,1},{2,10},{10... | collective-permute-start | bytes 1179656 | tf_op jit(solution)/shard_map/ppermute | solution.py:95
  43.8 22.8 %collective-permute-start.12 = (bf16[128,1536]{1,0:T(8,128)(2,1)}, bf16[128,1536]{1,0:T(8,128)(2,1)S(1)}, u32[]{:S(2)}, u32[]{:S(2)}) collective-permute-start(bf16[128,1536]{1,0:T(8,128)(2,1)} %collective-permute-done.9), channel_id=1, source_target_pairs={{0,8},{8,16},{16,24},{24,0},{1,9},{9,17},{17,25},{25,1},{2,10},{10... | collective-permute-start | bytes 1179656 | tf_op jit(solution)/shard_map/ppermute | solution.py:95
  44.0 31.0 %collective-permute-start.13 = (bf16[128,1536]{1,0:T(8,128)(2,1)}, bf16[128,1536]{1,0:T(8,128)(2,1)S(1)}, u32[]{:S(2)}, u32[]{:S(2)}) collective-permute-start(bf16[128,1536]{1,0:T(8,128)(2,1)} %collective-permute-done.10), channel_id=1, source_target_pairs={{0,8},{8,16},{16,24},{24,0},{1,9},{9,17},{17,25},{25,1},{2,10},{10... | collective-permute-start | bytes 1179656 | tf_op jit(solution)/shard_map/ppermute | solution.py:95
  49.3 26.4 %collective-permute-start.5 = (bf16[512,384]{0,1:T(8,128)(2,1)S(1)}, bf16[512,384]{0,1:T(8,128)(2,1)S(1)}, u32[]{:S(2)}, u32[]{:S(2)}) collective-permute-start(bf16[512,384]{0,1:T(8,128)(2,1)S(1)} %fusion.31), channel_id=1, source_target_pairs={{0,3},{1,2},{2,1},{3,0},{4,7},{5,6},{6,5},{7,4},{8,11},{9,10},{10,... | collective-permute-start | bytes 1179656 | tf_op jit(solution)/shard_map/ppermute | solution.py:85
  51.8 24.8 %collective-permute-start.6 = (bf16[512,384]{0,1:T(8,128)(2,1)S(1)}, bf16[512,384]{0,1:T(8,128)(2,1)S(1)}, u32[]{:S(2)}, u32[]{:S(2)}) collective-permute-start(bf16[512,384]{0,1:T(8,128)(2,1)S(1)} %fusion.31), channel_id=1, source_target_pairs={{0,2},{1,3},{2,0},{3,1},{4,6},{5,7},{6,4},{7,5},{8,10},{9,11},{10,... | collective-permute-start | bytes 1179656 | tf_op jit(solution)/shard_map/ppermute | solution.py:85
  60.4 16.3 %collective-permute-start.7 = (bf16[512,384]{0,1:T(8,128)(2,1)S(1)}, bf16[512,384]{0,1:T(8,128)(2,1)S(1)}, u32[]{:S(2)}, u32[]{:S(2)}) collective-permute-start(bf16[512,384]{0,1:T(8,128)(2,1)S(1)} %fusion.31), channel_id=1, source_target_pairs={{0,1},{1,0},{2,3},{3,2},{4,5},{5,4},{6,7},{7,6},{8,9},{9,8},{10,11... | collective-permute-start | bytes 1179656 | tf_op jit(solution)/shard_map/ppermute | solution.py:85
  66.6 16.9 %collective-permute-start.14 = (bf16[128,1536]{1,0:T(8,128)(2,1)S(1)}, bf16[128,1536]{1,0:T(8,128)(2,1)S(1)}, u32[]{:S(2)}, u32[]{:S(2)}) collective-permute-start(bf16[128,1536]{1,0:T(8,128)(2,1)S(1)} %collective-permute-done.11), channel_id=1, source_target_pairs={{0,8},{8,16},{16,24},{24,0},{1,9},{9,17},{17,25},{25,1},{2,10},{10... | collective-permute-start | bytes 1179656 | tf_op jit(solution)/shard_map/ppermute | solution.py:95
  75.0 16.9 %collective-permute-start.15 = (bf16[128,1536]{1,0:T(8,128)(2,1)S(1)}, bf16[128,1536]{1,0:T(8,128)(2,1)S(1)}, u32[]{:S(2)}, u32[]{:S(2)}) collective-permute-start(bf16[128,1536]{1,0:T(8,128)(2,1)S(1)} %collective-permute-done.12), channel_id=1, source_target_pairs={{0,8},{8,16},{16,24},{24,0},{1,9},{9,17},{17,25},{25,1},{2,10},{10... | collective-permute-start | bytes 1179656 | tf_op jit(solution)/shard_map/ppermute | solution.py:95
  75.7 24.3 %collective-permute-start.16 = (bf16[128,1536]{1,0:T(8,128)(2,1)S(1)}, bf16[128,1536]{1,0:T(8,128)(2,1)S(1)}, u32[]{:S(2)}, u32[]{:S(2)}) collective-permute-start(bf16[128,1536]{1,0:T(8,128)(2,1)S(1)} %collective-permute-done.13), channel_id=1, source_target_pairs={{0,8},{8,16},{16,24},{24,0},{1,9},{9,17},{17,25},{25,1},{2,10},{10... | collective-permute-start | bytes 1179656 | tf_op jit(solution)/shard_map/ppermute | solution.py:95
  84.1 19.2 %collective-permute-start.19 = (bf16[512,128]{0,1:T(8,128)(2,1)S(1)}, bf16[512,128]{0,1:T(8,128)(2,1)S(1)}, u32[]{:S(2)}, u32[]{:S(2)}) collective-permute-start(bf16[512,128]{0,1:T(8,128)(2,1)S(1)} %get-tuple-element.9), channel_id=1, source_target_pairs={{0,1},{1,0},{2,3},{3,2},{4,5},{5,4},{6,7},{7,6},{8,9},{9,8},{10,11... | collective-permute-start | bytes 393224 | tf_op jit(solution)/shard_map/ppermute | solution.py:85
  85.7 19.1 %collective-permute-start.20 = (bf16[512,128]{0,1:T(8,128)(2,1)S(1)}, bf16[512,128]{0,1:T(8,128)(2,1)S(1)}, u32[]{:S(2)}, u32[]{:S(2)}) collective-permute-start(bf16[512,128]{0,1:T(8,128)(2,1)S(1)} %get-tuple-element.11), channel_id=1, source_target_pairs={{0,2},{1,3},{2,0},{3,1},{4,6},{5,7},{6,4},{7,5},{8,10},{9,11},{10,... | collective-permute-start | bytes 393224 | tf_op jit(solution)/shard_map/ppermute | solution.py:85
  87.2 18.1 %collective-permute-start.21 = (bf16[512,128]{0,1:T(8,128)(2,1)S(1)}, bf16[512,128]{0,1:T(8,128)(2,1)S(1)}, u32[]{:S(2)}, u32[]{:S(2)}) collective-permute-start(bf16[512,128]{0,1:T(8,128)(2,1)S(1)} %get-tuple-element.10), channel_id=1, source_target_pairs={{0,3},{1,2},{2,1},{3,0},{4,7},{5,6},{6,5},{7,4},{8,11},{9,10},{10,... | collective-permute-start | bytes 393224 | tf_op jit(solution)/shard_map/ppermute | solution.py:85
  92.5 14.5 %collective-permute-start.22 = (bf16[512,128]{0,1:T(8,128)(2,1)S(1)}, bf16[512,128]{0,1:T(8,128)(2,1)S(1)}, u32[]{:S(2)}, u32[]{:S(2)}) collective-permute-start(bf16[512,128]{0,1:T(8,128)(2,1)S(1)} %get-tuple-element.12), channel_id=1, source_target_pairs={{0,1},{1,0},{2,3},{3,2},{4,5},{5,4},{6,7},{7,6},{8,9},{9,8},{10,11... | collective-permute-start | bytes 393224 | tf_op jit(solution)/shard_map/ppermute | solution.py:85
  100.0 8.5 %collective-permute-start.23 = (bf16[512,128]{0,1:T(8,128)(2,1)S(1)}, bf16[512,128]{0,1:T(8,128)(2,1)S(1)}, u32[]{:S(2)}, u32[]{:S(2)}) collective-permute-start(bf16[512,128]{0,1:T(8,128)(2,1)S(1)} %get-tuple-element.14), channel_id=1, source_target_pairs={{0,2},{1,3},{2,0},{3,1},{4,6},{5,7},{6,4},{7,5},{8,10},{9,11},{10,... | collective-permute-start | bytes 393224 | tf_op jit(solution)/shard_map/ppermute | solution.py:85
  103.3 7.4 %collective-permute-start.24 = (bf16[512,128]{0,1:T(8,128)(2,1)S(1)}, bf16[512,128]{0,1:T(8,128)(2,1)S(1)}, u32[]{:S(2)}, u32[]{:S(2)}) collective-permute-start(bf16[512,128]{0,1:T(8,128)(2,1)S(1)} %get-tuple-element.13), channel_id=1, source_target_pairs={{0,3},{1,2},{2,1},{3,0},{4,7},{5,6},{6,5},{7,4},{8,11},{9,10},{10,... | collective-permute-start | bytes 393224 | tf_op jit(solution)/shard_map/ppermute | solution.py:85
  104.8 7.6 %collective-permute-start.25 = (bf16[512,128]{0,1:T(8,128)(2,1)S(1)}, bf16[512,128]{0,1:T(8,128)(2,1)S(1)}, u32[]{:S(2)}, u32[]{:S(2)}) collective-permute-start(bf16[512,128]{0,1:T(8,128)(2,1)S(1)} %get-tuple-element.15), channel_id=1, source_target_pairs={{0,1},{1,0},{2,3},{3,2},{4,5},{5,4},{6,7},{7,6},{8,9},{9,8},{10,11... | collective-permute-start | bytes 393224 | tf_op jit(solution)/shard_map/ppermute | solution.py:85
  105.3 8.1 %collective-permute-start.26 = (bf16[512,128]{0,1:T(8,128)(2,1)S(1)}, bf16[512,128]{0,1:T(8,128)(2,1)S(1)}, u32[]{:S(2)}, u32[]{:S(2)}) collective-permute-start(bf16[512,128]{0,1:T(8,128)(2,1)S(1)} %get-tuple-element.17), channel_id=1, source_target_pairs={{0,2},{1,3},{2,0},{3,1},{4,6},{5,7},{6,4},{7,5},{8,10},{9,11},{10,... | collective-permute-start | bytes 393224 | tf_op jit(solution)/shard_map/ppermute | solution.py:85
  107.0 7.8 %collective-permute-start.27 = (bf16[512,128]{0,1:T(8,128)(2,1)S(1)}, bf16[512,128]{0,1:T(8,128)(2,1)S(1)}, u32[]{:S(2)}, u32[]{:S(2)}) collective-permute-start(bf16[512,128]{0,1:T(8,128)(2,1)S(1)} %get-tuple-element.16), channel_id=1, source_target_pairs={{0,3},{1,2},{2,1},{3,0},{4,7},{5,6},{6,5},{7,4},{8,11},{9,10},{10,... | collective-permute-start | bytes 393224 | tf_op jit(solution)/shard_map/ppermute | solution.py:85
  115.1 3.9 %collective-permute-start.28 = (f32[512]{0:T(512)S(1)}, f32[512]{0:T(512)S(1)}, u32[]{:S(2)}, u32[]{:S(2)}) collective-permute-start(f32[512]{0:T(512)S(1)} %multiply_reduce_fusion), channel_id=1, source_target_pairs={{0,4},{4,0},{1,5},{5,1},{2,6},{6,2},{3,7},{7,3},{8,12},{12,8},{9,1... | collective-permute-start | bytes 6152 | tf_op jit(solution)/shard_map/ppermute | solution.py:81
  116.4 2.2 %copy-start = (f32[512,1536]{1,0:T(8,128)}, f32[512,1536]{1,0:T(8,128)S(1)}, u32[]{:S(2)}) copy-start(f32[512,1536]{1,0:T(8,128)S(1)} %fusion.1) | copy-start | bytes 9437188
  118.5 0.9 copy-start.8
  118.5 1.0 copy-start.14
  118.5 1.1 copy-start.27
  118.5 21.7 %collective-permute-start.17 = (f32[256,1536]{1,0:T(8,128)}, f32[256,1536]{1,0:T(8,128)}, u32[]{:S(2)}, u32[]{:S(2)}) collective-permute-start(f32[256,1536]{1,0:T(8,128)} %slice.95), channel_id=1, source_target_pairs={{0,4},{4,0},{1,5},{5,1},{2,6},{6,2},{3,7},{7,3},{8,12},{12,8},{9,1... | collective-permute-start | bytes 4718600 | tf_op jit(solution)/shard_map/ppermute | solution.py:81
  119.7 0.9 copy-start.10
  119.7 1.0 copy-start.16
  119.7 5.2 %copy-start.4 = (bf16[3,512,512]{2,1,0:T(8,128)(2,1)S(1)}, bf16[3,512,512]{2,1,0:T(8,128)(2,1)}, u32[]{:S(2)}) copy-start(bf16[3,512,512]{2,1,0:T(8,128)(2,1)} %copy-done.3) | copy-start | bytes 4718596
  121.0 7.1 %collective-permute-start.30 = (bf16[3,128,128]{2,1,0:T(8,128)(2,1)S(1)}, bf16[3,128,128]{2,1,0:T(8,128)(2,1)S(1)}, u32[]{:S(2)}, u32[]{:S(2)}) collective-permute-start(bf16[3,128,128]{2,1,0:T(8,128)(2,1)S(1)} %convolution_convert_fusion), channel_id=1, source_target_pairs={{8,0},{16,8},{24,16},{9,1},{17,9},{25,17},{10,2},{18,10},{26,18},{... | collective-permute-start | bytes 294920 | tf_op jit(solution)/shard_map/ppermute | solution.py:90
  122.3 12.2 %collective-permute-start.31 = (bf16[3,128,128]{2,1,0:T(8,128)(2,1)S(1)}, bf16[3,128,128]{2,1,0:T(8,128)(2,1)S(1)}, u32[]{:S(2)}, u32[]{:S(2)}) collective-permute-start(bf16[3,128,128]{2,1,0:T(8,128)(2,1)S(1)} %convolution_convert_fusion), channel_id=1, source_target_pairs={{16,0},{24,8},{17,1},{25,9},{18,2},{26,10},{19,3},{27,11},{20,4},{... | collective-permute-start | bytes 294920 | tf_op jit(solution)/shard_map/ppermute | solution.py:90
  123.6 10.9 %collective-permute-start.32 = (bf16[3,128,128]{2,1,0:T(8,128)(2,1)S(1)}, bf16[3,128,128]{2,1,0:T(8,128)(2,1)S(1)}, u32[]{:S(2)}, u32[]{:S(2)}) collective-permute-start(bf16[3,128,128]{2,1,0:T(8,128)(2,1)S(1)} %convolution_convert_fusion), channel_id=1, source_target_pairs={{24,0},{25,1},{26,2},{27,3},{28,4},{29,5},{30,6},{31,7}} | collective-permute-start | bytes 294920 | tf_op jit(solution)/shard_map/ppermute | solution.py:90
  125.3 0.9 copy-start.6
  125.3 1.0 copy-start.12
  126.3 0.9 copy-start.18
  126.3 0.9 copy-start.20
  126.3 1.0 copy-start.22
  135.6 2.9 %collective-permute-start.33 = (bf16[2,256,384]{2,1,0:T(8,128)(2,1)S(1)}, bf16[2,256,384]{2,1,0:T(8,128)(2,1)S(1)}, u32[]{:S(2)}, u32[]{:S(2)}) collective-permute-start(bf16[2,256,384]{2,1,0:T(8,128)(2,1)S(1)} %pad_maximum_fusion.4), channel_id=1, source_target_pairs={{0,4},{4,0},{1,5},{5,1},{2,6},{6,2},{3,7},{7,3},{8,12},{12,8},{9,1... | collective-permute-start | bytes 1179656 | tf_op jit(solution)/shard_map/ppermute | solution.py:81
  135.8 1.8 %collective-permute-start.29 = (bf16[1,256,384]{2,1,0:T(8,128)(2,1)S(1)}, bf16[1,256,384]{2,1,0:T(8,128)(2,1)S(1)}, u32[]{:S(2)}, u32[]{:S(2)}) collective-permute-start(bf16[1,256,384]{2,1,0:T(8,128)(2,1)S(1)} %copy.49), channel_id=1, source_target_pairs={{0,4},{4,0},{1,5},{5,1},{2,6},{6,2},{3,7},{7,3},{8,12},{12,8},{9,1... | collective-permute-start | bytes 589832 | tf_op jit(solution)/shard_map/ppermute | solution.py:81
  137.6 2.6 %copy-start.1 = (f32[512,1536]{1,0:T(8,128)S(1)}, f32[512,1536]{1,0:T(8,128)}, u32[]{:S(2)}) copy-start(f32[512,1536]{1,0:T(8,128)} %copy-done) | copy-start | bytes 9437188

commit v2 on v1

--- a/solution.py
+++ b/solution.py
@@ -1,6 +1,8 @@
 import jax
 import jax.numpy as jnp
 from jax import lax
+from jax.experimental import pallas as pl
+from jax.experimental.pallas import tpu as pltpu
 from jax.sharding import PartitionSpec as P
 
 DH = 128
@@ -95,16 +97,83 @@
     return lax.ppermute(x, "seq", [(i, (i + 1) % count) for i in range(count)])
 
 
-def sum_of_shifts(state, sign):
+def shifts(state, sign):
     sent = state.astype(bf16)
-    total = jnp.zeros(state.shape, f32)
-    for hop in range(1, lax.axis_size("seq")):
-        total = total + seq_shift(sent, sign * hop).astype(f32)
+    return [seq_shift(sent, sign * hop) for hop in range(1, lax.axis_size("seq"))]
+
+
+def sum_of(parts):
+    total = parts[0].astype(f32)
+    for part in parts[1:]:
+        total = total + part.astype(f32)
     return total
 
 
 def dot(spec, a, b):
     return jnp.einsum(spec, a.astype(bf16), b.astype(bf16), preferred_element_type=f32)
+
+
+class Fetch:
+    def __init__(self, value):
+        self.value = value
+
+
+def block_of(shape):
+    return pl.BlockSpec(tuple(shape), lambda: (0,) * len(shape))
+
+
+def call(body, name, outs, place, ins, after=(), store=False):
+    whole = pl.BlockSpec(memory_space=pltpu.VMEM)
+    in_specs = [block_of(x.value.shape) if isinstance(x, Fetch) else whole for x in ins]
+    ins = [x.value if isinstance(x, Fetch) else x for x in ins]
+    anywhere = pl.BlockSpec(memory_space=pl.ANY)
+    n_in, n_after = len(ins), len(after)
+
+    def kernel(place_ref, *refs):
+        body(place_ref, *refs[:n_in], *refs[n_in + n_after :])
+
+    return pl.pallas_call(
+        kernel,
+        name=name,
+        out_shape=[jax.ShapeDtypeStruct(shape, dtype) for shape, dtype in outs],
+        in_specs=[pl.BlockSpec(memory_space=pltpu.SMEM)] + in_specs + [anywhere] * n_after,
+        out_specs=[block_of(shape) if store else whole for shape, _ in outs],
+        cost_estimate=pl.CostEstimate(flops=1, bytes_accessed=1, transcendentals=0),
+        compiler_params=pltpu.CompilerParams(vmem_limit_bytes=40 * 2**20),
+    )(place, *ins, *after)
+
+
+def mm(a, b, ca, cb):
+    return lax.dot_general(a, b, (((ca,), (cb,)), ((), ())), preferred_element_type=f32)
+
+
+def half_of(ref, which, half):
+    return ref[:, pl.ds(pl.multiple_of(which * half, DH), half)]
+
+
+def head_of(ref, got, which, half, h):
+    own = ref[:, pl.ds(pl.multiple_of(which * half + h * DH, DH), DH)]
+    return jnp.concatenate([own, got[:, h * DH : (h + 1) * DH]], 0)
+
+
+def swapped(x):
+    tok = x.shape[0] // 2
+    return jnp.concatenate([x[tok:], x[:tok]], 0)
+
+
+def causal_mask(r, tok):
+    def spot(axis):
+        i = lax.broadcasted_iota(jnp.int32, (2 * tok, 2 * tok), axis)
+        return jnp.where(i < tok, i + r * tok, i - r * tok)
+
+    return spot(0) >= spot(1)
+
+
+def total_of(parts, h):
+    total = parts[0][h].astype(f32)
+    for part in parts[1:]:
+        total = total + part[h].astype(f32)
+    return total.astype(bf16)
 
 
 def head_split(query_input, key_input, value_input, norm_gain, out_weight, out_grad):
@@ -151,7 +220,8 @@
     causal = place >= place.reshape(1, 2 * tok)
 
     own_kv = dot("tha,thb->hab", k, v)
-    prefix = sum_of_shifts(own_kv, 1)
+    prefix_parts = shifts(own_kv, 1)
+    prefix = sum_of(prefix_parts)
     key_scores = jnp.where(causal, dot("thd,shd->hts", q, k), 0.0).astype(bf16)
     attend = dot("hts,shd->thd", key_scores, v) + dot("thd,hde->the", q, prefix)
     attend = attend.reshape(2 * tok, half) * score_scale
@@ -180,7 +250,6 @@
             piece = piece + col_flip(group(c ^ bits).astype(bf16), bits).astype(f32)
         pieces.append(piece)
         start += count
-    grad_norm = jnp.concatenate(pieces, 1)
 
     feats = [normalized] + [col_flip(normalized, bits) for bits in range(1, n_col)]
 
@@ -196,34 +265,124 @@
         partial = partial + jnp.dot(
             features((z - s) % n_seq), weight, preferred_element_type=f32
         )
-    projected = (partial[:tok] + row_swap(partial[tok:])).astype(bf16)
-
-    scaled = grad_norm * gain
-    inner = jnp.sum(scaled * normed, axis=-1)
-    inner = (inner + halves_swapped(row_swap(inner)))[:, None] * (1.0 / width)
-    grad_attend = inv_rms * (scaled - normed * inner)
-    g = grad_attend.reshape(2 * tok, heads, DH).astype(bf16)
-
-    suffix = sum_of_shifts(dot("tha,thb->hab", q, g), -1)
-    value_scores = jnp.where(causal, dot("thd,shd->hts", g, v), 0.0).astype(bf16)
-    query_part = dot("hts,shd->thd", value_scores, k) + dot("the,hde->thd", g, prefix)
-    key_part = dot("hts,thd->shd", value_scores, q) + dot("shb,hab->sha", v, suffix)
-    value_part = dot("hts,the->she", key_scores, g) + dot("sha,hab->shb", k, suffix)
-
-    def settle(parts):
-        whole = [(x * score_scale).reshape(2 * tok, half).astype(bf16) for x in parts]
-        back = row_swap(jnp.stack([x[tok:] for x in whole]))
-        return [
-            jnp.where(
-                r == 0,
-                jnp.concatenate([x[:tok], y], 1),
-                jnp.concatenate([y, x[:tok]], 1),
-            )
-            for x, y in zip(whole, back)
-        ]
-
-    (query_grad,) = settle([query_part])
-    key_grad, value_grad = settle([key_part, value_part])
+    scale = score_scale
+    both = 2 * tok
+    outs_loc = out_weight.shape[1]
+    place = jnp.stack([z, r, c]).astype(jnp.int32)
+
+    def scale_grad(s, *refs):
+        grads, (gain, attend, inv_rms, scaled, inner) = refs[:heads], refs[heads:]
+        total = 0.0
+        for h in range(heads):
+            cols = slice(h * DH, (h + 1) * DH)
+            grad = grads[h][...] * gain[:, cols]
+            scaled[:, cols] = grad
+            normed = attend[:, cols] * inv_rms[...]
+            total = total + jnp.sum(grad * normed, axis=1, keepdims=True)
+        inner[...] = total
+
+    scaled, inner = call(
+        scale_grad,
+        "scale_grad",
+        [((both, half), f32), ((both, 1), f32)],
+        place,
+        [*pieces, gain.reshape(1, half), attend, inv_rms],
+    )
+
+    def back_state(s, scaled, inner, inner_got, attend, inv_rms, q, got, grad, state):
+        mean = (inner[...] + swapped(inner_got[...])) * (1.0 / width)
+        inv = inv_rms[...]
+        value = (inv * (scaled[...] - attend[...] * inv * mean)).astype(bf16)
+        grad[...] = value
+        for h in range(heads):
+            queries = head_of(q, got.at[0], s[1], half, h)
+            state[h] = mm(queries, value[:, h * DH : (h + 1) * DH], 0, 0).astype(bf16)
+
+    grad, state = call(
+        back_state,
+        "back_state",
+        [((both, half), bf16), ((heads, DH, DH), bf16)],
+        place,
+        [scaled, inner, row_swap(inner), attend, inv_rms, query_input, got],
+    )
+    suffix = shifts(state, -1)
+
+    def local_grads(s, q, k, v, got, grad, *refs):
+        *prefix, dq_own, dq_other, own, other = refs
+        mask = causal_mask(s[1], tok)
+        for h in range(heads):
+            cols = slice(h * DH, (h + 1) * DH)
+            queries = head_of(q, got.at[0], s[1], half, h)
+            keys = head_of(k, got.at[1], s[1], half, h)
+            vals = head_of(v, got.at[2], s[1], half, h)
+            grads = grad[:, cols]
+            key_scores = jnp.where(mask, mm(queries, keys, 1, 1), 0.0).astype(bf16)
+            value_scores = jnp.where(mask, mm(grads, vals, 1, 1), 0.0).astype(bf16)
+            dq = mm(value_scores, keys, 1, 0) + mm(grads, total_of(prefix, h), 1, 1)
+            dq = (dq * scale).astype(bf16)
+            dq_own[:, cols] = dq[:tok]
+            dq_other[:, cols] = dq[tok:]
+            dk = mm(value_scores, queries, 0, 0)
+            dv = mm(key_scores, grads, 0, 0)
+            for i, x in enumerate((dk, dv)):
+                own[i, :, cols] = x[:tok]
+                other[i, :, cols] = x[tok:]
+
+    dq_own, dq_other, kv_own, kv_other = call(
+        local_grads,
+        "local_grads",
+        [((tok, half), bf16)] * 2 + [((2, tok, half), f32)] * 2,
+        place,
+        [query_input, key_input, value_input, got, grad, *prefix_parts],
+    )
+    kv_got = row_swap(kv_other)
+
+    def finish_early(s, own, other, dq_own, dq_other, out, dq, token):
+        token[...] = jnp.zeros_like(token)
+        out[...] = (own[:tok] + other[...]).astype(bf16)
+        dq[:, pl.ds(pl.multiple_of(s[1] * half, DH), half)] = dq_own[...]
+        dq[:, pl.ds(pl.multiple_of((1 - s[1]) * half, DH), half)] = dq_other[...]
+
+    projected, query_grad, token = call(
+        finish_early,
+        "finish_early",
+        [((tok, outs_loc), bf16), ((tok, width), bf16), ((8, DH), f32)],
+        place,
+        [partial, row_swap(partial[tok:]), dq_own, row_swap(dq_other)],
+        store=True,
+    )
+
+    def sum_later(s, *refs):
+        *parts, _, total = refs
+        for h in range(heads):
+            total[h] = total_of(parts, h)
+
+    (later,) = call(
+        sum_later,
+        "sum_later",
+        [((heads, DH, DH), bf16)],
+        place,
+        [*suffix, token],
+    )
+
+    def far_grads(s, k, v, kv_own, kv_got, later, later_got, key_grad, value_grad):
+        for local, state, which in ((kv_own, later, s[1]), (kv_got, later_got, 1 - s[1])):
+            for h in range(heads):
+                cols = slice(h * DH, (h + 1) * DH)
+                place_cols = pl.ds(pl.multiple_of(which * half + h * DH, DH), DH)
+                dk = local[0, :, cols] + mm(v[:, place_cols], state[h], 1, 1)
+                dv = local[1, :, cols] + mm(k[:, place_cols], state[h], 1, 0)
+                key_grad[:, place_cols] = (dk * scale).astype(bf16)
+                value_grad[:, place_cols] = (dv * scale).astype(bf16)
+
+    key_grad, value_grad = call(
+        far_grads,
+        "far_grads",
+        [((tok, width), bf16)] * 2,
+        place,
+        [key_input, value_input, kv_own, kv_got, later, row_swap(later)],
+        store=True,
+    )
     return (projected, query_grad, key_grad, value_grad)
 
 

time: 143 us -> 135 us (0.944)
  waiting for transfers between devices: 54.3 us -> 33.9 us
  Pallas kernels: 0 us -> 9.38 us
  starting transfers between devices: 45.4 us -> 50.3 us
  matrix products: 21.4 us -> 25.1 us
  other arithmetic: 7.9 us -> 4.77 us
  local copies, waits for them, and re-layouts: 12.2 us -> 9.95 us
    ppermute x9, waiting for transfers between devices: 26.3 us -> 14.3 us  [seq_rotate(): return lax.ppermute(x, 'seq', [(i, (i + 1) % count) for i in range(count)])]
    ppermute x6, waiting for transfers between devices: 21.1 us -> 9.56 us  [seq_shift(): lax.ppermute(x, 'seq', [(i, i + step) for i in range(count) if 0 <= i + s...]
    pallas_call x0 -> x6, Pallas kernels: none -> 9.38 us  [call(): pl.pallas_call(kernel, name=name, out_shape=[jax.ShapeDtypeStruct(shape,...]
    ppermute x9, starting transfers between devices: 12.5 us -> 21.3 us  [seq_rotate(): return lax.ppermute(x, 'seq', [(i, (i + 1) % count) for i in range(count)])]
    ppermute x6, starting transfers between devices: 16.2 us -> 11.8 us  [seq_shift(): lax.ppermute(x, 'seq', [(i, i + step) for i in range(count) if 0 <= i + s...]
    convert_element_type x2 -> x0, other arithmetic: 2.68 us -> none  [the longest x1 2.51 us: head_split(): projected = (partial[:tok] + row_swap(partial[tok:])).astype(bf16)]
    select_n x3 -> x0, other arithmetic: 2.51 us -> none  [settle(): jnp.where(r == 0, jnp.concatenate([x[:tok], y], 1), jnp.concatenate([y, x...]
    unnamed x61 -> x25, local copies, waits for them, and re-layouts: 4.59 us -> 2.1 us
  transfers between devices with their start and end apart: 34 -> 35, of which waited for: 14 -> 10; matrix products, arithmetic and copies ran while one was open for 23% -> 27% of each run, Pallas kernels for 0% -> 6%
where the time goes in v2:
time: 135 us
  starting transfers between devices  50.3 us (37%)
  waiting for transfers between devices  33.9 us (25%)
  matrix products  25.1 us (19%)
  local copies, waits for them, and re-layouts  9.95 us (7%)
  Pallas kernels  9.38 us (7%)
  other arithmetic  4.77 us (4%)
    ppermute x9, starting transfers between devices, seq_rotate(): return lax.ppermute(x, 'seq', [(i, (i + 1) % count) for i in range(count)])  21.3 us
    ppermute x12, starting transfers between devices, col_flip(): lax.ppermute(x, 'col', [(i, i ^ bits) for i in range(lax.axis_size('col'))])  16.4 us
    ppermute x9, waiting for transfers between devices, seq_rotate(): return lax.ppermute(x, 'seq', [(i, (i + 1) % count) for i in range(count)])  14.3 us
    ppermute x6, starting transfers between devices, seq_shift(): lax.ppermute(x, 'seq', [(i, i + step) for i in range(count) if 0 <= i + s...  11.8 us
    dot_general x12, matrix products, head_split(): lax.dot_general(grads, w, (((1,), (1,)), ((), ())), preferred_element_typ...  11.7 us
    ppermute x6, waiting for transfers between devices, seq_shift(): lax.ppermute(x, 'seq', [(i, i + step) for i in range(count) if 0 <= i + s...  9.56 us
    pallas_call x6, Pallas kernels, call(): pl.pallas_call(kernel, name=name, out_shape=[jax.ShapeDtypeStruct(shape,...  9.38 us
    ppermute x12, waiting for transfers between devices, col_flip(): lax.ppermute(x, 'col', [(i, i ^ bits) for i in range(lax.axis_size('col'))])  7.22 us
  transfers between devices with their start and end apart: 35, of which 10 were waited for; matrix products, arithmetic and copies ran while one was open for 27% of the time, Pallas kernels for 6%

profile of v2, /device:TPU:0, one launch (start us, length us, event | category | flops | bytes accessed | tf_op | source)
XLA Modules:
  0.0 134.7 jit_solution(17487132449168498174)
XLA Ops:
  0.7 2.4 %fusion.67 = (bf16[128,1536]{1,0:T(8,128)(2,1)}, bf16[128,1536]{1,0:T(8,128)(2,1)}, bf16[128,1536]{1,0:T(8,128)(2,1)}) fusion(bf16[384,1536]{1,0:T(8,128)(2,1)} %param.10), kind=kLoop, calls=%fused_computation.104 | loop fusion | bytes 2359296 | tf_op jit(solution)/shard_map/slice | solution.py:195
  3.0 3.0 %collective-permute-start.10 = (bf16[128,1536]{1,0:T(8,128)(2,1)}, bf16[128,1536]{1,0:T(8,128)(2,1)S(1)}, u32[]{:S(2)}, u32[]{:S(2)}) collective-permute-start(bf16[128,1536]{1,0:T(8,128)(2,1)} %get-tuple-element.31), channel_id=1, source_target_pairs={{0,8},{8,16},{16,24},{24,0},{1,9},{9,17},{17,25},{25,1},{2,10},{10... | collective-permute-start | bytes 1179656 | tf_op jit(solution)/shard_map/ppermute | solution.py:97
  6.0 1.6 %collective-permute-start.9 = (bf16[128,1536]{1,0:T(8,128)(2,1)}, bf16[128,1536]{1,0:T(8,128)(2,1)}, u32[]{:S(2)}, u32[]{:S(2)}) collective-permute-start(bf16[128,1536]{1,0:T(8,128)(2,1)} %get-tuple-element.32), channel_id=1, source_target_pairs={{0,8},{8,16},{16,24},{24,0},{1,9},{9,17},{17,25},{25,1},{2,10},{10... | collective-permute-start | bytes 1179656 | tf_op jit(solution)/shard_map/ppermute | solution.py:97
  7.8 0.9 pad_maximum_fusion
  8.7 1.6 %collective-permute-start.8 = (bf16[128,1536]{1,0:T(8,128)(2,1)}, bf16[128,1536]{1,0:T(8,128)(2,1)}, u32[]{:S(2)}, u32[]{:S(2)}) collective-permute-start(bf16[128,1536]{1,0:T(8,128)(2,1)} %get-tuple-element.30), channel_id=1, source_target_pairs={{0,8},{8,16},{16,24},{24,0},{1,9},{9,17},{17,25},{25,1},{2,10},{10... | collective-permute-start | bytes 1179656 | tf_op jit(solution)/shard_map/ppermute | solution.py:97
  10.3 0.9 broadcast_compare_fusion
  11.2 1.0 constant_dynamic-update-slice_fusion.1
  12.8 0.8 copy.70
  13.7 0.8 copy.62
  15.1 2.0 %convolution_convert_fusion = bf16[3,128,128]{2,1,0:T(8,128)(2,1)} fusion(bf16[256,3,128]{2,0,1:T(8,128)(2,1)S(1)} %copy.71, bf16[256,3,128]{2,0,1:T(8,128)(2,1)} %copy.70, bf16[256,3,128]{0,2,1:T(8,128)(2,1)S(1)} %bitcast.56, bf16[256,3,128]{0,2,1:T(8,128)(2,1)} %bitcast.54), kind=kOutput, calls=%fused_computation.24 | convolution fusion | flops 51953664 | bytes 884736 | tf_op jit(solution)/shard_map/tha,thb->hab/dot_general | solution.py:113
  17.1 1.9 %collective-permute-start.1 = (bf16[3,128,128]{2,1,0:T(8,128)(2,1)}, bf16[3,128,128]{2,1,0:T(8,128)(2,1)S(1)}, u32[]{:S(2)}, u32[]{:S(2)}) collective-permute-start(bf16[3,128,128]{2,1,0:T(8,128)(2,1)} %convolution_convert_fusion), channel_id=1, source_target_pairs={{0,8},{8,16},{16,24},{1,9},{9,17},{17,25},{2,10},{10,18},{18,26},{... | collective-permute-start | bytes 294920 | tf_op jit(solution)/shard_map/ppermute | solution.py:92
  19.0 4.7 %collective-permute-start.2 = (bf16[3,128,128]{2,1,0:T(8,128)(2,1)}, bf16[3,128,128]{2,1,0:T(8,128)(2,1)S(1)}, u32[]{:S(2)}, u32[]{:S(2)}) collective-permute-start(bf16[3,128,128]{2,1,0:T(8,128)(2,1)} %convolution_convert_fusion), channel_id=1, source_target_pairs={{0,16},{8,24},{1,17},{9,25},{2,18},{10,26},{3,19},{11,27},{4,20},{... | collective-permute-start | bytes 294920 | tf_op jit(solution)/shard_map/ppermute | solution.py:92
  24.1 1.3 collective-permute-start.3
  25.4 3.0 %fusion.2 = f32[3,128,512]{2,1,0:T(8,128)} fusion(pred[512,512]{1,0:T(8,128)(4,1)S(1)} %copy-done.8, bf16[256,3,128]{2,0,1:T(8,128)(2,1)} %copy-done.9, bf16[256,3,128]{2,0,1:T(8,128)(2,1)} %copy.70, bf16[256,3,128]{2,0,1:T(8,128)(2,1)S(1)} %copy.67, bf16[256,3,128]{2,0,1:T(8,128)(2,1)S(1)} %copy.66, bf16[256,3,128]{0,2,1:T(8,128)(2,1)S(1)} %bitcast.57, ...), kind=kOutput, calls=%fused_computation.4 | convolution fusion | flops 406585344 | bytes 2228224 | tf_op jit(solution)/shard_map/hts,shd->thd/dot_general | solution.py:113
  28.5 5.9 %collective-permute-done.8 = bf16[128,1536]{1,0:T(8,128)(2,1)} collective-permute-done((bf16[128,1536]{1,0:T(8,128)(2,1)}, bf16[128,1536]{1,0:T(8,128)(2,1)}, u32[]{:S(2)}, u32[]{:S(2)}) %collective-permute-start.8) | collective-permute-done | bytes 393248 | tf_op jit(solution)/shard_map/ppermute | solution.py:97
  34.3 0.9 collective-permute-start.13
  35.2 5.0 %collective-permute-start.12 = (bf16[128,1536]{1,0:T(8,128)(2,1)}, bf16[128,1536]{1,0:T(8,128)(2,1)}, u32[]{:S(2)}, u32[]{:S(2)}) collective-permute-start(bf16[128,1536]{1,0:T(8,128)(2,1)} %collective-permute-done.9), channel_id=1, source_target_pairs={{0,8},{8,16},{16,24},{24,0},{1,9},{9,17},{17,25},{25,1},{2,10},{10... | collective-permute-start | bytes 1179656 | tf_op jit(solution)/shard_map/ppermute | solution.py:97
  40.2 2.8 %collective-permute-start.11 = (bf16[128,1536]{1,0:T(8,128)(2,1)}, bf16[128,1536]{1,0:T(8,128)(2,1)}, u32[]{:S(2)}, u32[]{:S(2)}) collective-permute-start(bf16[128,1536]{1,0:T(8,128)(2,1)} %collective-permute-done.8), channel_id=1, source_target_pairs={{0,8},{8,16},{16,24},{24,0},{1,9},{9,17},{17,25},{25,1},{2,10},{10... | collective-permute-start | bytes 1179656 | tf_op jit(solution)/shard_map/ppermute | solution.py:97
  43.0 1.6 %fusion.22 = (f32[512]{0:T(512)S(1)}, f32[3,128,512]{2,1,0:T(8,128)S(1)}) fusion(f32[3,128,512]{2,1,0:T(8,128)} %fusion.2, bf16[256,3,128]{2,0,1:T(8,128)(2,1)} %copy-done.6, bf16[256,3,128]{2,0,1:T(8,128)(2,1)S(1)} %copy.66, bf16[3,128,128]{2,1,0:T(8,128)(2,1)S(1)} %collective-permute-done.3.refs_7_, ...), kind=kOutput, calls=%fused_computation.27 | convolution fusion | flops 52198912 | bytes 2263040 | tf_op jit(solution)/shard_map/thd,hde->the/dot_general | solution.py:113
  44.7 0.8 copy-done.5
  45.5 1.2 copy.75
  46.6 1.2 broadcast_multiply_fusion.refs_4_.refs_3_
  48.1 1.4 %multiply_convert_fusion = bf16[512,384]{0,1:T(8,128)(2,1)S(1)} fusion(f32[384]{0:T(512)S(1)} %dynamic_slice.27, f32[512]{0:T(512)S(1)} %fusion.50, f32[3,128,512]{2,1,0:T(8,128)} %copy-done.5), kind=kLoop, calls=%fused_computation.28 | loop fusion | flops 589824 | bytes 1183232 | tf_op jit(solution)/shard_map/convert_element_type | solution.py:232
  49.5 2.5 %collective-permute-start.5 = (bf16[512,384]{0,1:T(8,128)(2,1)S(1)}, bf16[512,384]{0,1:T(8,128)(2,1)S(1)}, u32[]{:S(2)}, u32[]{:S(2)}) collective-permute-start(bf16[512,384]{0,1:T(8,128)(2,1)S(1)} %multiply_convert_fusion), channel_id=1, source_target_pairs={{0,3},{1,2},{2,1},{3,0},{4,7},{5,6},{6,5},{7,4},{8,11},{9,10},{10,... | collective-permute-start | bytes 1179656 | tf_op jit(solution)/shard_map/ppermute | solution.py:87
  52.6 1.2 constant_dynamic-update-slice_fusion
  56.0 1.6 %fusion.73 = f32[512,128]{1,0:T(8,128)S(1)} fusion(bf16[512,1536]{1,0:T(8,128)(2,1)S(1)} %constant_dynamic-update-slice_fusion, bf16[128,1536]{1,0:T(8,128)(2,1)} %collective-permute-done.9), kind=kOutput, calls=%fused_computation.110 | convolution fusion | flops 201326592 | bytes 2228224 | tf_op jit(solution)/shard_map/dot_general | solution.py:238
  57.6 1.6 %fusion.71 = f32[512,128]{1,0:T(8,128)S(1)} fusion(bf16[512,1536]{1,0:T(8,128)(2,1)S(1)} %constant_dynamic-update-slice_fusion, bf16[128,1536]{1,0:T(8,128)(2,1)} %collective-permute-done.8), kind=kOutput, calls=%fused_computation.108 | convolution fusion | flops 201326592 | bytes 2228224 | tf_op jit(solution)/shard_map/dot_general | solution.py:238
  59.1 0.6 collective-permute-start.7
  59.8 1.6 %fusion.74 = f32[512,128]{1,0:T(8,128)S(1)} fusion(bf16[512,1536]{1,0:T(8,128)(2,1)S(1)} %constant_dynamic-update-slice_fusion, bf16[128,1536]{1,0:T(8,128)(2,1)} %collective-permute-done.13), kind=kOutput, calls=%fused_computation.111 | convolution fusion | flops 201326592 | bytes 2228224 | tf_op jit(solution)/shard_map/dot_general | solution.py:238
  61.4 1.6 %fusion.72 = f32[512,128]{1,0:T(8,128)S(1)} fusion(bf16[512,1536]{1,0:T(8,128)(2,1)S(1)} %constant_dynamic-update-slice_fusion, bf16[128,1536]{1,0:T(8,128)(2,1)} %collective-permute-done.12), kind=kOutput, calls=%fused_computation.109 | convolution fusion | flops 201326592 | bytes 2228224 | tf_op jit(solution)/shard_map/dot_general | solution.py:238
  63.0 1.4 %collective-permute-done.11 = bf16[128,1536]{1,0:T(8,128)(2,1)} collective-permute-done((bf16[128,1536]{1,0:T(8,128)(2,1)}, bf16[128,1536]{1,0:T(8,128)(2,1)}, u32[]{:S(2)}, u32[]{:S(2)}) %collective-permute-start.11) | collective-permute-done | bytes 393248 | tf_op jit(solution)/shard_map/ppermute | solution.py:97
  64.4 3.6 %collective-permute-start.15 = (bf16[128,1536]{1,0:T(8,128)(2,1)}, bf16[128,1536]{1,0:T(8,128)(2,1)S(1)}, u32[]{:S(2)}, u32[]{:S(2)}) collective-permute-start(bf16[128,1536]{1,0:T(8,128)(2,1)} %collective-permute-done.12), channel_id=1, source_target_pairs={{0,8},{8,16},{16,24},{24,0},{1,9},{9,17},{17,25},{25,1},{2,10},{10... | collective-permute-start | bytes 1179656 | tf_op jit(solution)/shard_map/ppermute | solution.py:97
  68.0 1.6 %fusion.70 = f32[512,128]{1,0:T(8,128)S(1)} fusion(bf16[512,1536]{1,0:T(8,128)(2,1)S(1)} %constant_dynamic-update-slice_fusion, bf16[128,1536]{1,0:T(8,128)(2,1)} %collective-permute-done.11), kind=kOutput, calls=%fused_computation.107 | convolution fusion | flops 201326592 | bytes 2228224 | tf_op jit(solution)/shard_map/dot_general | solution.py:238
  69.6 2.7 %collective-permute-start.14 = (bf16[128,1536]{1,0:T(8,128)(2,1)}, bf16[128,1536]{1,0:T(8,128)(2,1)S(1)}, u32[]{:S(2)}, u32[]{:S(2)}) collective-permute-start(bf16[128,1536]{1,0:T(8,128)(2,1)} %collective-permute-done.11), channel_id=1, source_target_pairs={{0,8},{8,16},{16,24},{24,0},{1,9},{9,17},{17,25},{25,1},{2,10},{10... | collective-permute-start | bytes 1179656 | tf_op jit(solution)/shard_map/ppermute | solution.py:97
  72.3 2.2 %fusion.3 = f32[512,1536]{1,0:T(8,128)S(1)} fusion(bf16[128,1536]{1,0:T(8,128)(2,1)S(1)} %collective-permute-done.10, bf16[128,1536]{1,0:T(8,128)(2,1)} %collective-permute-done.9, bf16[128,1536]{1,0:T(8,128)(2,1)} %collective-permute-done.8, bf16[512,384]{0,1:T(8,128)(2,1)S(1)} %collective-permute-done.5, bf16[512,384]{0,1:T(8,128)(2,1)S(1)} %collective-permute-done.6, ...), kind=kOutput, calls=%fused_computation.6 | convolution fusion | flops 608108544 | bytes 5898243 | tf_op jit(solution)/shard_map/dot_general | solution.py:265
  74.5 2.3 %fusion.9 = f32[512,1536]{1,0:T(8,128)S(1)} fusion(bf16[128,1536]{1,0:T(8,128)(2,1)} %collective-permute-done.13, bf16[128,1536]{1,0:T(8,128)(2,1)} %collective-permute-done.12, bf16[128,1536]{1,0:T(8,128)(2,1)} %collective-permute-done.11, bf16[512,384]{0,1:T(8,128)(2,1)S(1)} %collective-permute-done.5, bf16[512,384]{0,1:T(8,128)(2,1)S(1)} %collective-permute-done.6, ...), kind=kOutput, calls=%fused_computation.12 | convolution fusion | flops 608108544 | bytes 5898243 | tf_op jit(solution)/shard_map/dot_general | solution.py:265
  76.8 0.6 select_convert_fusion.3
  77.4 1.6 %collective-permute-start.25 = (bf16[512,128]{1,0:T(8,128)(2,1)S(1)}, bf16[512,128]{1,0:T(8,128)(2,1)S(1)}, u32[]{:S(2)}, u32[]{:S(2)}) collective-permute-start(bf16[512,128]{1,0:T(8,128)(2,1)S(1)} %get-tuple-element.33), channel_id=1, source_target_pairs={{0,1},{1,0},{2,3},{3,2},{4,5},{5,4},{6,7},{7,6},{8,9},{9,8},{10,11... | collective-permute-start | bytes 393224 | tf_op jit(solution)/shard_map/ppermute | solution.py:87
  79.0 1.5 %collective-permute-start.26 = (bf16[512,128]{1,0:T(8,128)(2,1)S(1)}, bf16[512,128]{1,0:T(8,128)(2,1)S(1)}, u32[]{:S(2)}, u32[]{:S(2)}) collective-permute-start(bf16[512,128]{1,0:T(8,128)(2,1)S(1)} %get-tuple-element.35), channel_id=1, source_target_pairs={{0,2},{1,3},{2,0},{3,1},{4,6},{5,7},{6,4},{7,5},{8,10},{9,11},{10,... | collective-permute-start | bytes 393224 | tf_op jit(solution)/shard_map/ppermute | solution.py:87
  81.0 2.9 %collective-permute-done.15 = bf16[128,1536]{1,0:T(8,128)(2,1)S(1)} collective-permute-done((bf16[128,1536]{1,0:T(8,128)(2,1)}, bf16[128,1536]{1,0:T(8,128)(2,1)S(1)}, u32[]{:S(2)}, u32[]{:S(2)}) %collective-permute-start.15) | collective-permute-done | bytes 393248 | tf_op jit(solution)/shard_map/ppermute | solution.py:97
  84.4 1.5 %collective-permute-start.22 = (bf16[512,128]{1,0:T(8,128)(2,1)S(1)}, bf16[512,128]{1,0:T(8,128)(2,1)S(1)}, u32[]{:S(2)}, u32[]{:S(2)}) collective-permute-start(bf16[512,128]{1,0:T(8,128)(2,1)S(1)} %get-tuple-element.36), channel_id=1, source_target_pairs={{0,1},{1,0},{2,3},{3,2},{4,5},{5,4},{6,7},{7,6},{8,9},{9,8},{10,11... | collective-permute-start | bytes 393224 | tf_op jit(solution)/shard_map/ppermute | solution.py:87
  86.0 4.1 %collective-permute-done.14 = bf16[128,1536]{1,0:T(8,128)(2,1)S(1)} collective-permute-done((bf16[128,1536]{1,0:T(8,128)(2,1)}, bf16[128,1536]{1,0:T(8,128)(2,1)S(1)}, u32[]{:S(2)}, u32[]{:S(2)}) %collective-permute-start.14) | collective-permute-done | bytes 393248 | tf_op jit(solution)/shard_map/ppermute | solution.py:97
  90.1 1.1 fusion.15
  91.2 1.1 fusion.1.refs_0_
  92.5 0.6 select_convert_fusion.9
  93.1 1.6 %collective-permute-start.23 = (bf16[512,128]{1,0:T(8,128)(2,1)S(1)}, bf16[512,128]{1,0:T(8,128)(2,1)S(1)}, u32[]{:S(2)}, u32[]{:S(2)}) collective-permute-start(bf16[512,128]{1,0:T(8,128)(2,1)S(1)} %get-tuple-element.38), channel_id=1, source_target_pairs={{0,2},{1,3},{2,0},{3,1},{4,6},{5,7},{6,4},{7,5},{8,10},{9,11},{10,... | collective-permute-start | bytes 393224 | tf_op jit(solution)/shard_map/ppermute | solution.py:87
  94.7 1.4 %collective-permute-start.24 = (bf16[512,128]{1,0:T(8,128)(2,1)S(1)}, bf16[512,128]{1,0:T(8,128)(2,1)S(1)}, u32[]{:S(2)}, u32[]{:S(2)}) collective-permute-start(bf16[512,128]{1,0:T(8,128)(2,1)S(1)} %get-tuple-element.37), channel_id=1, source_target_pairs={{0,3},{1,2},{2,1},{3,0},{4,7},{5,6},{6,5},{7,4},{8,11},{9,10},{10,... | collective-permute-start | bytes 393224 | tf_op jit(solution)/shard_map/ppermute | solution.py:87
  96.8 1.6 %collective-permute-start.20 = (bf16[512,128]{1,0:T(8,128)(2,1)S(1)}, bf16[512,128]{1,0:T(8,128)(2,1)S(1)}, u32[]{:S(2)}, u32[]{:S(2)}) collective-permute-start(bf16[512,128]{1,0:T(8,128)(2,1)S(1)} %get-tuple-element.41), channel_id=1, source_target_pairs={{0,2},{1,3},{2,0},{3,1},{4,6},{5,7},{6,4},{7,5},{8,10},{9,11},{10,... | collective-permute-start | bytes 393224 | tf_op jit(solution)/shard_map/ppermute | solution.py:87
  98.4 3.9 %collective-permute-done.23 = bf16[512,128]{1,0:T(8,128)(2,1)S(1)} collective-permute-done((bf16[512,128]{1,0:T(8,128)(2,1)S(1)}, bf16[512,128]{1,0:T(8,128)(2,1)S(1)}, u32[]{:S(2)}, u32[]{:S(2)}) %collective-permute-start.23) | collective-permute-done | bytes 131104 | tf_op jit(solution)/shard_map/ppermute | solution.py:87
  102.3 2.5 %collective-permute-start.21 = (bf16[512,128]{1,0:T(8,128)(2,1)S(1)}, bf16[512,128]{1,0:T(8,128)(2,1)S(1)}, u32[]{:S(2)}, u32[]{:S(2)}) collective-permute-start(bf16[512,128]{1,0:T(8,128)(2,1)S(1)} %get-tuple-element.40), channel_id=1, source_target_pairs={{0,3},{1,2},{2,1},{3,0},{4,7},{5,6},{6,5},{7,4},{8,11},{9,10},{10,... | collective-permute-start | bytes 393224 | tf_op jit(solution)/shard_map/ppermute | solution.py:87
  104.9 3.3 %collective-permute-done.21 = bf16[512,128]{1,0:T(8,128)(2,1)S(1)} collective-permute-done((bf16[512,128]{1,0:T(8,128)(2,1)S(1)}, bf16[512,128]{1,0:T(8,128)(2,1)S(1)}, u32[]{:S(2)}, u32[]{:S(2)}) %collective-permute-start.21) | collective-permute-done | bytes 131104 | tf_op jit(solution)/shard_map/ppermute | solution.py:87
  108.3 1.2 scale_grad.1
  109.6 1.5 %collective-permute-done.28.refs_2_ = f32[512,1]{1,0:T(8,128)S(1)} collective-permute-done((f32[512,1]{1,0:T(8,128)S(1)}, f32[512,1]{1,0:T(8,128)S(1)}, u32[]{:S(2)}, u32[]{:S(2)}) %collective-permute-start.28) | collective-permute-done | bytes 2080 | tf_op jit(solution)/shard_map/ppermute | solution.py:83
  111.1 1.1 back_state.1
  112.2 3.0 %local_grads.1 = (bf16[256,384]{1,0:T(8,128)(2,1)S(1)}, bf16[256,384]{1,0:T(8,128)(2,1)S(1)}, f32[2,256,384]{2,1,0:T(8,128)S(1)}, f32[2,256,384]{2,1,0:T(8,128)S(1)}) custom-call(s32[3]{0:T(128)S(1)} %pad_add_fusion.place_ref, bf16[256,768]{1,0:T(8,128)(2,1)S(1)} %copy-done, bf16[256,768]{1,0:T(8,128)(2,1)S(1)} %copy-done.2, bf16[256,768]{1,0:T(8,128)(2,1)S(1)} %copy-done.1, ...), custom_call_target="tpu_custom_call" | custom-call | flops 1 | bytes 1 | tf_op jit(solution)/shard_map/local_grads/pallas_call | solution.py:135
  115.8 1.3 collective-permute-start.31
  117.1 1.3 collective-permute-start.32
  118.4 1.3 collective-permute-start.33
  119.7 1.7 %finish_early.1 = (bf16[256,1536]{1,0:T(8,128)(2,1)}, bf16[256,768]{1,0:T(8,128)(2,1)}, f32[8,128]{1,0:T(8,128)S(1)}) custom-call(s32[3]{0:T(128)S(1)} %pad_add_fusion.place_ref, f32[512,1536]{1,0:T(8,128)S(1)} %fusion.1.refs_0_, f32[256,1536]{1,0:T(8,128)S(1)} %collective-permute-done.17.refs_1_, bf16[256,384]{1,0:T(8,128)(2,1)S(1)} %get-tuple-element.20.refs_2_, ...), custom_call_target="tpu_custom_call" | custom-call | flops 1 | bytes 1 | tf_op jit(solution)/shard_map/finish_early/pallas_call | solution.py:135
  121.4 1.4 %collective-permute-done.31.refs_0_ = bf16[3,128,128]{2,1,0:T(8,128)(2,1)S(1)} collective-permute-done((bf16[3,128,128]{2,1,0:T(8,128)(2,1)S(1)}, bf16[3,128,128]{2,1,0:T(8,128)(2,1)S(1)}, u32[]{:S(2)}, u32[]{:S(2)}) %collective-permute-start.31) | collective-permute-done | bytes 98336 | tf_op jit(solution)/shard_map/ppermute | solution.py:92
  122.8 8.1 %collective-permute-done.32.refs_1_ = bf16[3,128,128]{2,1,0:T(8,128)(2,1)S(1)} collective-permute-done((bf16[3,128,128]{2,1,0:T(8,128)(2,1)S(1)}, bf16[3,128,128]{2,1,0:T(8,128)(2,1)S(1)}, u32[]{:S(2)}, u32[]{:S(2)}) %collective-permute-start.32) | collective-permute-done | bytes 98336 | tf_op jit(solution)/shard_map/ppermute | solution.py:92
  130.9 0.6 sum_later.1.refs_4_
  131.6 1.3 collective-permute-done.34.refs_5_
  132.9 1.8 %far_grads.1 = (bf16[256,768]{1,0:T(8,128)(2,1)}, bf16[256,768]{1,0:T(8,128)(2,1)}) custom-call(s32[3]{0:T(128)S(1)} %pad_add_fusion.place_ref, bf16[256,768]{1,0:T(8,128)(2,1)S(1)} %copy-done.2, bf16[256,768]{1,0:T(8,128)(2,1)S(1)} %copy-done.1, f32[2,256,384]{2,1,0:T(8,128)S(1)} %get-tuple-element.24.refs_2_, ...), custom_call_target="tpu_custom_call" | custom-call | flops 1 | bytes 1 | tf_op jit(solution)/shard_map/far_grads/pallas_call | solution.py:135
  (87 shorter events, 7.5 us)
Async XLA Ops:
  0.6 7.0 %copy-start.1 = (bf16[256,768]{1,0:T(8,128)(2,1)S(1)}, bf16[256,768]{1,0:T(8,128)(2,1)}, u32[]{:S(2)}) copy-start(bf16[256,768]{1,0:T(8,128)(2,1)} %refs_1_.3) | copy-start | bytes 1179652
  0.6 7.0 %copy-start = (bf16[256,768]{1,0:T(8,128)(2,1)S(1)}, bf16[256,768]{1,0:T(8,128)(2,1)}, u32[]{:S(2)}) copy-start(bf16[256,768]{1,0:T(8,128)(2,1)} %refs_0_.2) | copy-start | bytes 1179652
  0.7 7.0 %copy-start.2 = (bf16[256,768]{1,0:T(8,128)(2,1)S(1)}, bf16[256,768]{1,0:T(8,128)(2,1)}, u32[]{:S(2)}) copy-start(bf16[256,768]{1,0:T(8,128)(2,1)} %refs_0_.3) | copy-start | bytes 1179652
  3.0 21.1 %collective-permute-start.10 = (bf16[128,1536]{1,0:T(8,128)(2,1)}, bf16[128,1536]{1,0:T(8,128)(2,1)S(1)}, u32[]{:S(2)}, u32[]{:S(2)}) collective-permute-start(bf16[128,1536]{1,0:T(8,128)(2,1)} %get-tuple-element.31), channel_id=1, source_target_pairs={{0,8},{8,16},{16,24},{24,0},{1,9},{9,17},{17,25},{25,1},{2,10},{10... | collective-permute-start | bytes 1179656 | tf_op jit(solution)/shard_map/ppermute | solution.py:97
  6.0 22.4 %collective-permute-start.9 = (bf16[128,1536]{1,0:T(8,128)(2,1)}, bf16[128,1536]{1,0:T(8,128)(2,1)}, u32[]{:S(2)}, u32[]{:S(2)}) collective-permute-start(bf16[128,1536]{1,0:T(8,128)(2,1)} %get-tuple-element.32), channel_id=1, source_target_pairs={{0,8},{8,16},{16,24},{24,0},{1,9},{9,17},{17,25},{25,1},{2,10},{10... | collective-permute-start | bytes 1179656 | tf_op jit(solution)/shard_map/ppermute | solution.py:97
  7.7 3.5 %copy-start.7 = (bf16[256,1536]{1,0:T(8,128)(2,1)S(1)}, bf16[256,1536]{1,0:T(8,128)(2,1)}, u32[]{:S(2)}) copy-start(bf16[256,1536]{1,0:T(8,128)(2,1)} %param.11) | copy-start | bytes 2359300
  8.7 5.9 %collective-permute-start = (bf16[3,256,384]{2,1,0:T(8,128)(2,1)}, bf16[3,256,384]{2,1,0:T(8,128)(2,1)S(1)}, u32[]{:S(2)}, u32[]{:S(2)}) collective-permute-start(bf16[3,256,384]{2,1,0:T(8,128)(2,1)} %pad_maximum_fusion), channel_id=1, source_target_pairs={{0,4},{4,0},{1,5},{5,1},{2,6},{6,2},{3,7},{7,3},{8,12},{12,8},{9,1... | collective-permute-start | bytes 1769480 | tf_op jit(solution)/shard_map/ppermute | solution.py:83
  8.7 25.6 %collective-permute-start.8 = (bf16[128,1536]{1,0:T(8,128)(2,1)}, bf16[128,1536]{1,0:T(8,128)(2,1)}, u32[]{:S(2)}, u32[]{:S(2)}) collective-permute-start(bf16[128,1536]{1,0:T(8,128)(2,1)} %get-tuple-element.30), channel_id=1, source_target_pairs={{0,8},{8,16},{16,24},{24,0},{1,9},{9,17},{17,25},{25,1},{2,10},{10... | collective-permute-start | bytes 1179656 | tf_op jit(solution)/shard_map/ppermute | solution.py:97
  11.2 3.3 %copy-start.10 = (f32[768]{0:T(1024)S(1)}, f32[768]{0:T(1024)}, u32[]{:S(2)}) copy-start(f32[768]{0:T(1024)} %param.9) | copy-start | bytes 9220
  14.8 10.6 %copy-start.8 = (pred[512,512]{1,0:T(8,128)(4,1)S(1)}, pred[512,512]{1,0:T(8,128)(4,1)}, u32[]{:S(2)}) copy-start(pred[512,512]{1,0:T(8,128)(4,1)} %broadcast_compare_fusion) | copy-start | bytes 786436
  15.0 8.8 %copy-start.9 = (bf16[256,3,128]{2,0,1:T(8,128)(2,1)}, bf16[256,3,128]{2,0,1:T(8,128)(2,1)S(1)}, u32[]{:S(2)}) copy-start(bf16[256,3,128]{2,0,1:T(8,128)(2,1)S(1)} %copy.71) | copy-start | bytes 589828
  17.1 18.1 %collective-permute-start.1 = (bf16[3,128,128]{2,1,0:T(8,128)(2,1)}, bf16[3,128,128]{2,1,0:T(8,128)(2,1)S(1)}, u32[]{:S(2)}, u32[]{:S(2)}) collective-permute-start(bf16[3,128,128]{2,1,0:T(8,128)(2,1)} %convolution_convert_fusion), channel_id=1, source_target_pairs={{0,8},{8,16},{16,24},{1,9},{9,17},{17,25},{2,10},{10,18},{18,26},{... | collective-permute-start | bytes 294920 | tf_op jit(solution)/shard_map/ppermute | solution.py:92
  19.0 21.2 %collective-permute-start.2 = (bf16[3,128,128]{2,1,0:T(8,128)(2,1)}, bf16[3,128,128]{2,1,0:T(8,128)(2,1)S(1)}, u32[]{:S(2)}, u32[]{:S(2)}) collective-permute-start(bf16[3,128,128]{2,1,0:T(8,128)(2,1)} %convolution_convert_fusion), channel_id=1, source_target_pairs={{0,16},{8,24},{1,17},{9,25},{2,18},{10,26},{3,19},{11,27},{4,20},{... | collective-permute-start | bytes 294920 | tf_op jit(solution)/shard_map/ppermute | solution.py:92
  24.1 4.4 %copy-start.6 = (bf16[256,3,128]{2,0,1:T(8,128)(2,1)}, bf16[256,3,128]{2,0,1:T(8,128)(2,1)S(1)}, u32[]{:S(2)}) copy-start(bf16[256,3,128]{2,0,1:T(8,128)(2,1)S(1)} %copy.67) | copy-start | bytes 589828
  24.1 18.9 %collective-permute-start.3 = (bf16[3,128,128]{2,1,0:T(8,128)(2,1)}, bf16[3,128,128]{2,1,0:T(8,128)(2,1)S(1)}, u32[]{:S(2)}, u32[]{:S(2)}) collective-permute-start(bf16[3,128,128]{2,1,0:T(8,128)(2,1)} %convolution_convert_fusion), channel_id=1, source_target_pairs={{0,24},{1,25},{2,26},{3,27},{4,28},{5,29},{6,30},{7,31}} | collective-permute-start | bytes 294920 | tf_op jit(solution)/shard_map/ppermute | solution.py:92
  28.4 23.6 %collective-permute-start.18 = (bf16[256,1536]{1,0:T(8,128)(2,1)}, bf16[256,1536]{1,0:T(8,128)(2,1)}, u32[]{:S(2)}, u32[]{:S(2)}) collective-permute-start(bf16[256,1536]{1,0:T(8,128)(2,1)} %param.11), channel_id=1, source_target_pairs={{0,4},{4,0},{1,5},{5,1},{2,6},{6,2},{3,7},{7,3},{8,12},{12,8},{9,1... | collective-permute-start | bytes 2359304 | tf_op jit(solution)/shard_map/ppermute | solution.py:83
  34.3 24.8 %collective-permute-start.13 = (bf16[128,1536]{1,0:T(8,128)(2,1)S(1)}, bf16[128,1536]{1,0:T(8,128)(2,1)}, u32[]{:S(2)}, u32[]{:S(2)}) collective-permute-start(bf16[128,1536]{1,0:T(8,128)(2,1)S(1)} %collective-permute-done.10), channel_id=1, source_target_pairs={{0,8},{8,16},{16,24},{24,0},{1,9},{9,17},{17,25},{25,1},{2,10},{10... | collective-permute-start | bytes 1179656 | tf_op jit(solution)/shard_map/ppermute | solution.py:97
  35.2 26.1 %collective-permute-start.12 = (bf16[128,1536]{1,0:T(8,128)(2,1)}, bf16[128,1536]{1,0:T(8,128)(2,1)}, u32[]{:S(2)}, u32[]{:S(2)}) collective-permute-start(bf16[128,1536]{1,0:T(8,128)(2,1)} %collective-permute-done.9), channel_id=1, source_target_pairs={{0,8},{8,16},{16,24},{24,0},{1,9},{9,17},{17,25},{25,1},{2,10},{10... | collective-permute-start | bytes 1179656 | tf_op jit(solution)/shard_map/ppermute | solution.py:97
  40.2 24.2 %collective-permute-start.11 = (bf16[128,1536]{1,0:T(8,128)(2,1)}, bf16[128,1536]{1,0:T(8,128)(2,1)}, u32[]{:S(2)}, u32[]{:S(2)}) collective-permute-start(bf16[128,1536]{1,0:T(8,128)(2,1)} %collective-permute-done.8), channel_id=1, source_target_pairs={{0,8},{8,16},{16,24},{24,0},{1,9},{9,17},{17,25},{25,1},{2,10},{10... | collective-permute-start | bytes 1179656 | tf_op jit(solution)/shard_map/ppermute | solution.py:97
  44.6 0.9 copy-start.5
  44.6 3.2 %collective-permute-start.4 = (f32[512]{0:T(512)S(1)}, f32[512]{0:T(512)S(1)}, u32[]{:S(2)}, u32[]{:S(2)}) collective-permute-start(f32[512]{0:T(512)S(1)} %get-tuple-element.53), channel_id=1, source_target_pairs={{0,4},{4,0},{1,5},{5,1},{2,6},{6,2},{3,7},{7,3},{8,12},{12,8},{9,1... | collective-permute-start | bytes 6152 | tf_op jit(solution)/shard_map/ppermute | solution.py:83
  48.0 4.5 %copy-start.3 = (bf16[512,1536]{1,0:T(8,128)(2,1)S(1)}, bf16[512,1536]{1,0:T(8,128)(2,1)}, u32[]{:S(2)}) copy-start(bf16[512,1536]{1,0:T(8,128)(2,1)} %constant_dynamic-update-slice_fusion.1) | copy-start | bytes 4718596
  48.0 5.7 %copy-start.4 = (bf16[384,1536]{1,0:T(8,128)(2,1)S(1)}, bf16[384,1536]{1,0:T(8,128)(2,1)}, u32[]{:S(2)}) copy-start(bf16[384,1536]{1,0:T(8,128)(2,1)} %param.10) | copy-start | bytes 3538948
  49.5 20.0 %collective-permute-start.5 = (bf16[512,384]{0,1:T(8,128)(2,1)S(1)}, bf16[512,384]{0,1:T(8,128)(2,1)S(1)}, u32[]{:S(2)}, u32[]{:S(2)}) collective-permute-start(bf16[512,384]{0,1:T(8,128)(2,1)S(1)} %multiply_convert_fusion), channel_id=1, source_target_pairs={{0,3},{1,2},{2,1},{3,0},{4,7},{5,6},{6,5},{7,4},{8,11},{9,10},{10,... | collective-permute-start | bytes 1179656 | tf_op jit(solution)/shard_map/ppermute | solution.py:87
  52.0 20.3 %collective-permute-start.6 = (bf16[512,384]{0,1:T(8,128)(2,1)S(1)}, bf16[512,384]{0,1:T(8,128)(2,1)S(1)}, u32[]{:S(2)}, u32[]{:S(2)}) collective-permute-start(bf16[512,384]{0,1:T(8,128)(2,1)S(1)} %multiply_convert_fusion), channel_id=1, source_target_pairs={{0,2},{1,3},{2,0},{3,1},{4,6},{5,7},{6,4},{7,5},{8,10},{9,11},{10,... | collective-permute-start | bytes 1179656 | tf_op jit(solution)/shard_map/ppermute | solution.py:87
  59.1 13.2 %collective-permute-start.7 = (bf16[512,384]{0,1:T(8,128)(2,1)S(1)}, bf16[512,384]{0,1:T(8,128)(2,1)S(1)}, u32[]{:S(2)}, u32[]{:S(2)}) collective-permute-start(bf16[512,384]{0,1:T(8,128)(2,1)S(1)} %multiply_convert_fusion), channel_id=1, source_target_pairs={{0,1},{1,0},{2,3},{3,2},{4,5},{5,4},{6,7},{7,6},{8,9},{9,8},{10,11... | collective-permute-start | bytes 1179656 | tf_op jit(solution)/shard_map/ppermute | solution.py:87
  61.3 15.5 %collective-permute-start.16 = (bf16[128,1536]{1,0:T(8,128)(2,1)}, bf16[128,1536]{1,0:T(8,128)(2,1)S(1)}, u32[]{:S(2)}, u32[]{:S(2)}) collective-permute-start(bf16[128,1536]{1,0:T(8,128)(2,1)} %collective-permute-done.13), channel_id=1, source_target_pairs={{0,8},{8,16},{16,24},{24,0},{1,9},{9,17},{17,25},{25,1},{2,10},{10... | collective-permute-start | bytes 1179656 | tf_op jit(solution)/shard_map/ppermute | solution.py:97
  64.4 19.5 %collective-permute-start.15 = (bf16[128,1536]{1,0:T(8,128)(2,1)}, bf16[128,1536]{1,0:T(8,128)(2,1)S(1)}, u32[]{:S(2)}, u32[]{:S(2)}) collective-permute-start(bf16[128,1536]{1,0:T(8,128)(2,1)} %collective-permute-done.12), channel_id=1, source_target_pairs={{0,8},{8,16},{16,24},{24,0},{1,9},{9,17},{17,25},{25,1},{2,10},{10... | collective-permute-start | bytes 1179656 | tf_op jit(solution)/shard_map/ppermute | solution.py:97
  69.6 20.5 %collective-permute-start.14 = (bf16[128,1536]{1,0:T(8,128)(2,1)}, bf16[128,1536]{1,0:T(8,128)(2,1)S(1)}, u32[]{:S(2)}, u32[]{:S(2)}) collective-permute-start(bf16[128,1536]{1,0:T(8,128)(2,1)} %collective-permute-done.11), channel_id=1, source_target_pairs={{0,8},{8,16},{16,24},{24,0},{1,9},{9,17},{17,25},{25,1},{2,10},{10... | collective-permute-start | bytes 1179656 | tf_op jit(solution)/shard_map/ppermute | solution.py:97
  77.4 15.7 %collective-permute-start.25 = (bf16[512,128]{1,0:T(8,128)(2,1)S(1)}, bf16[512,128]{1,0:T(8,128)(2,1)S(1)}, u32[]{:S(2)}, u32[]{:S(2)}) collective-permute-start(bf16[512,128]{1,0:T(8,128)(2,1)S(1)} %get-tuple-element.33), channel_id=1, source_target_pairs={{0,1},{1,0},{2,3},{3,2},{4,5},{5,4},{6,7},{7,6},{8,9},{9,8},{10,11... | collective-permute-start | bytes 393224 | tf_op jit(solution)/shard_map/ppermute | solution.py:87
  79.0 15.8 %collective-permute-start.26 = (bf16[512,128]{1,0:T(8,128)(2,1)S(1)}, bf16[512,128]{1,0:T(8,128)(2,1)S(1)}, u32[]{:S(2)}, u32[]{:S(2)}) collective-permute-start(bf16[512,128]{1,0:T(8,128)(2,1)S(1)} %get-tuple-element.35), channel_id=1, source_target_pairs={{0,2},{1,3},{2,0},{3,1},{4,6},{5,7},{6,4},{7,5},{8,10},{9,11},{10,... | collective-permute-start | bytes 393224 | tf_op jit(solution)/shard_map/ppermute | solution.py:87
  80.5 15.7 %collective-permute-start.27 = (bf16[512,128]{1,0:T(8,128)(2,1)S(1)}, bf16[512,128]{1,0:T(8,128)(2,1)S(1)}, u32[]{:S(2)}, u32[]{:S(2)}) collective-permute-start(bf16[512,128]{1,0:T(8,128)(2,1)S(1)} %get-tuple-element.34), channel_id=1, source_target_pairs={{0,3},{1,2},{2,1},{3,0},{4,7},{5,6},{6,5},{7,4},{8,11},{9,10},{10,... | collective-permute-start | bytes 393224 | tf_op jit(solution)/shard_map/ppermute | solution.py:87
  84.4 12.3 %collective-permute-start.22 = (bf16[512,128]{1,0:T(8,128)(2,1)S(1)}, bf16[512,128]{1,0:T(8,128)(2,1)S(1)}, u32[]{:S(2)}, u32[]{:S(2)}) collective-permute-start(bf16[512,128]{1,0:T(8,128)(2,1)S(1)} %get-tuple-element.36), channel_id=1, source_target_pairs={{0,1},{1,0},{2,3},{3,2},{4,5},{5,4},{6,7},{7,6},{8,9},{9,8},{10,11... | collective-permute-start | bytes 393224 | tf_op jit(solution)/shard_map/ppermute | solution.py:87
  92.5 27.2 %collective-permute-start.17 = (f32[256,1536]{1,0:T(8,128)S(1)}, f32[256,1536]{1,0:T(8,128)S(1)}, u32[]{:S(2)}, u32[]{:S(2)}) collective-permute-start(f32[256,1536]{1,0:T(8,128)S(1)} %slice.40), channel_id=1, source_target_pairs={{0,4},{4,0},{1,5},{5,1},{2,6},{6,2},{3,7},{7,3},{8,12},{12,8},{9,1... | collective-permute-start | bytes 4718600 | tf_op jit(solution)/shard_map/ppermute | solution.py:83
  93.1 9.2 %collective-permute-start.23 = (bf16[512,128]{1,0:T(8,128)(2,1)S(1)}, bf16[512,128]{1,0:T(8,128)(2,1)S(1)}, u32[]{:S(2)}, u32[]{:S(2)}) collective-permute-start(bf16[512,128]{1,0:T(8,128)(2,1)S(1)} %get-tuple-element.38), channel_id=1, source_target_pairs={{0,2},{1,3},{2,0},{3,1},{4,6},{5,7},{6,4},{7,5},{8,10},{9,11},{10,... | collective-permute-start | bytes 393224 | tf_op jit(solution)/shard_map/ppermute | solution.py:87
  94.7 10.0 %collective-permute-start.24 = (bf16[512,128]{1,0:T(8,128)(2,1)S(1)}, bf16[512,128]{1,0:T(8,128)(2,1)S(1)}, u32[]{:S(2)}, u32[]{:S(2)}) collective-permute-start(bf16[512,128]{1,0:T(8,128)(2,1)S(1)} %get-tuple-element.37), channel_id=1, source_target_pairs={{0,3},{1,2},{2,1},{3,0},{4,7},{5,6},{6,5},{7,4},{8,11},{9,10},{10,... | collective-permute-start | bytes 393224 | tf_op jit(solution)/shard_map/ppermute | solution.py:87
  96.2 8.7 %collective-permute-start.19 = (bf16[512,128]{1,0:T(8,128)(2,1)S(1)}, bf16[512,128]{1,0:T(8,128)(2,1)S(1)}, u32[]{:S(2)}, u32[]{:S(2)}) collective-permute-start(bf16[512,128]{1,0:T(8,128)(2,1)S(1)} %get-tuple-element.39), channel_id=1, source_target_pairs={{0,1},{1,0},{2,3},{3,2},{4,5},{5,4},{6,7},{7,6},{8,9},{9,8},{10,11... | collective-permute-start | bytes 393224 | tf_op jit(solution)/shard_map/ppermute | solution.py:87
  96.8 8.1 %collective-permute-start.20 = (bf16[512,128]{1,0:T(8,128)(2,1)S(1)}, bf16[512,128]{1,0:T(8,128)(2,1)S(1)}, u32[]{:S(2)}, u32[]{:S(2)}) collective-permute-start(bf16[512,128]{1,0:T(8,128)(2,1)S(1)} %get-tuple-element.41), channel_id=1, source_target_pairs={{0,2},{1,3},{2,0},{3,1},{4,6},{5,7},{6,4},{7,5},{8,10},{9,11},{10,... | collective-permute-start | bytes 393224 | tf_op jit(solution)/shard_map/ppermute | solution.py:87
  102.3 5.9 %collective-permute-start.21 = (bf16[512,128]{1,0:T(8,128)(2,1)S(1)}, bf16[512,128]{1,0:T(8,128)(2,1)S(1)}, u32[]{:S(2)}, u32[]{:S(2)}) collective-permute-start(bf16[512,128]{1,0:T(8,128)(2,1)S(1)} %get-tuple-element.40), channel_id=1, source_target_pairs={{0,3},{1,2},{2,1},{3,0},{4,7},{5,6},{6,5},{7,4},{8,11},{9,10},{10,... | collective-permute-start | bytes 393224 | tf_op jit(solution)/shard_map/ppermute | solution.py:87
  109.5 1.6 %collective-permute-start.28 = (f32[512,1]{1,0:T(8,128)S(1)}, f32[512,1]{1,0:T(8,128)S(1)}, u32[]{:S(2)}, u32[]{:S(2)}) collective-permute-start(f32[512,1]{1,0:T(8,128)S(1)} %get-tuple-element.18.refs_1_), channel_id=1, source_target_pairs={{0,4},{4,0},{1,5},{5,1},{2,6},{6,2},{3,7},{7,3},{8,12},{12,8},{9,1... | collective-permute-start | bytes 6152 | tf_op jit(solution)/shard_map/ppermute | solution.py:83
  115.2 16.4 %collective-permute-start.30 = (f32[2,256,384]{2,1,0:T(8,128)S(1)}, f32[2,256,384]{2,1,0:T(8,128)S(1)}, u32[]{:S(2)}, u32[]{:S(2)}) collective-permute-start(f32[2,256,384]{2,1,0:T(8,128)S(1)} %get-tuple-element.25), channel_id=1, source_target_pairs={{0,4},{4,0},{1,5},{5,1},{2,6},{6,2},{3,7},{7,3},{8,12},{12,8},{9,1... | collective-permute-start | bytes 2359304 | tf_op jit(solution)/shard_map/ppermute | solution.py:83
  115.4 2.9 %collective-permute-start.29 = (bf16[256,384]{1,0:T(8,128)(2,1)S(1)}, bf16[256,384]{1,0:T(8,128)(2,1)S(1)}, u32[]{:S(2)}, u32[]{:S(2)}) collective-permute-start(bf16[256,384]{1,0:T(8,128)(2,1)S(1)} %get-tuple-element.21), channel_id=1, source_target_pairs={{0,4},{4,0},{1,5},{5,1},{2,6},{6,2},{3,7},{7,3},{8,12},{12,8},{9,1... | collective-permute-start | bytes 589832 | tf_op jit(solution)/shard_map/ppermute | solution.py:83
  115.8 7.0 %collective-permute-start.31 = (bf16[3,128,128]{2,1,0:T(8,128)(2,1)S(1)}, bf16[3,128,128]{2,1,0:T(8,128)(2,1)S(1)}, u32[]{:S(2)}, u32[]{:S(2)}) collective-permute-start(bf16[3,128,128]{2,1,0:T(8,128)(2,1)S(1)} %get-tuple-element.26), channel_id=1, source_target_pairs={{8,0},{16,8},{24,16},{9,1},{17,9},{25,17},{10,2},{18,10},{26,18},{... | collective-permute-start | bytes 294920 | tf_op jit(solution)/shard_map/ppermute | solution.py:92
  117.1 13.9 %collective-permute-start.32 = (bf16[3,128,128]{2,1,0:T(8,128)(2,1)S(1)}, bf16[3,128,128]{2,1,0:T(8,128)(2,1)S(1)}, u32[]{:S(2)}, u32[]{:S(2)}) collective-permute-start(bf16[3,128,128]{2,1,0:T(8,128)(2,1)S(1)} %get-tuple-element.26), channel_id=1, source_target_pairs={{16,0},{24,8},{17,1},{25,9},{18,2},{26,10},{19,3},{27,11},{20,4},{... | collective-permute-start | bytes 294920 | tf_op jit(solution)/shard_map/ppermute | solution.py:92
  118.4 12.6 %collective-permute-start.33 = (bf16[3,128,128]{2,1,0:T(8,128)(2,1)S(1)}, bf16[3,128,128]{2,1,0:T(8,128)(2,1)S(1)}, u32[]{:S(2)}, u32[]{:S(2)}) collective-permute-start(bf16[3,128,128]{2,1,0:T(8,128)(2,1)S(1)} %get-tuple-element.26), channel_id=1, source_target_pairs={{24,0},{25,1},{26,2},{27,3},{28,4},{29,5},{30,6},{31,7}} | collective-permute-start | bytes 294920 | tf_op jit(solution)/shard_map/ppermute | solution.py:92
  131.5 1.4 %collective-permute-start.34 = (bf16[3,128,128]{2,1,0:T(8,128)(2,1)S(1)}, bf16[3,128,128]{2,1,0:T(8,128)(2,1)S(1)}, u32[]{:S(2)}, u32[]{:S(2)}) collective-permute-start(bf16[3,128,128]{2,1,0:T(8,128)(2,1)S(1)} %sum_later.1.refs_4_), channel_id=1, source_target_pairs={{0,4},{4,0},{1,5},{5,1},{2,6},{6,2},{3,7},{7,3},{8,12},{12,8},{9,1... | collective-permute-start | bytes 294920 | tf_op jit(solution)/shard_map/ppermute | solution.py:83

commit v3 on v2

--- a/solution.py
+++ b/solution.py
@@ -138,7 +138,7 @@
         out_shape=[jax.ShapeDtypeStruct(shape, dtype) for shape, dtype in outs],
         in_specs=[pl.BlockSpec(memory_space=pltpu.SMEM)] + in_specs + [anywhere] * n_after,
         out_specs=[block_of(shape) if store else whole for shape, _ in outs],
-        cost_estimate=pl.CostEstimate(flops=1, bytes_accessed=1, transcendentals=0),
+        cost_estimate=pl.CostEstimate(flops=15 * 10**9 if name == "local_grads" else 1, bytes_accessed=1, transcendentals=0),
         compiler_params=pltpu.CompilerParams(vmem_limit_bytes=40 * 2**20),
     )(place, *ins, *after)
 
@@ -353,7 +353,7 @@
     )
 
     def sum_later(s, *refs):
-        *parts, _, total = refs
+        *parts, total = refs
         for h in range(heads):
             total[h] = total_of(parts, h)
 
@@ -362,10 +362,10 @@
         "sum_later",
         [((heads, DH, DH), bf16)],
         place,
-        [*suffix, token],
-    )
-
-    def far_grads(s, k, v, kv_own, kv_got, later, later_got, key_grad, value_grad):
+        suffix,
+    )
+
+    def far_grads(s, k, v, kv_own, kv_got, later, later_got, token, key_grad, value_grad):
         for local, state, which in ((kv_own, later, s[1]), (kv_got, later_got, 1 - s[1])):
             for h in range(heads):
                 cols = slice(h * DH, (h + 1) * DH)
@@ -380,7 +380,7 @@
         "far_grads",
         [((tok, width), bf16)] * 2,
         place,
-        [key_input, value_input, kv_own, kv_got, later, row_swap(later)],
+        [key_input, value_input, kv_own, kv_got, later, row_swap(later), token],
         store=True,
     )
     return (projected, query_grad, key_grad, value_grad)

time: 135 us -> 133 us (0.985)
  waiting for transfers between devices: 33.9 us -> 31.6 us
    ppermute x8, waiting for transfers between devices: 2.82 us -> 0.02 us  [row_swap(): return lax.ppermute(x, 'row', [(0, 1), (1, 0)])]
    ppermute x6, waiting for transfers between devices: 9.56 us -> 11.4 us  [seq_shift(): lax.ppermute(x, 'seq', [(i, i + step) for i in range(count) if 0 <= i + s...]
    ppermute x12, waiting for transfers between devices: 7.22 us -> 5.84 us  [col_flip(): lax.ppermute(x, 'col', [(i, i ^ bits) for i in range(lax.axis_size('col'))])]
  transfers between devices with their start and end apart: 35 -> 35, of which waited for: 10 -> 9; matrix products, arithmetic and copies ran while one was open for 27% -> 27% of each run, Pallas kernels for 6% -> 5%
where the time goes in v3:
time: 133 us; the launch traced here: 132 us
  starting transfers between devices  49.8 us (37%)
  waiting for transfers between devices  31.6 us (24%)
  matrix products  25 us (19%)
  local copies, waits for them, and re-layouts  9.95 us (7%)
  Pallas kernels  9.39 us (7%)
  other arithmetic  4.77 us (4%)
    ppermute x9, starting transfers between devices, seq_rotate(): return lax.ppermute(x, 'seq', [(i, (i + 1) % count) for i in range(count)])  21.3 us
    ppermute x12, starting transfers between devices, col_flip(): lax.ppermute(x, 'col', [(i, i ^ bits) for i in range(lax.axis_size('col'))])  15.3 us
    ppermute x9, waiting for transfers between devices, seq_rotate(): return lax.ppermute(x, 'seq', [(i, (i + 1) % count) for i in range(count)])  14.3 us
    ppermute x6, starting transfers between devices, seq_shift(): lax.ppermute(x, 'seq', [(i, i + step) for i in range(count) if 0 <= i + s...  11.8 us
    dot_general x12, matrix products, head_split(): lax.dot_general(grads, w, (((1,), (1,)), ((), ())), preferred_element_typ...  11.7 us
    ppermute x6, waiting for transfers between devices, seq_shift(): lax.ppermute(x, 'seq', [(i, i + step) for i in range(count) if 0 <= i + s...  11.4 us
    pallas_call x6, Pallas kernels, call(): pl.pallas_call(kernel, name=name, out_shape=[jax.ShapeDtypeStruct(shape,...  9.39 us
    dot_general x4, matrix products, head_split(): jnp.dot(features((z - s) % n_seq), weight, preferred_element_type=f32)  6.74 us
  transfers between devices with their start and end apart: 35, of which 9 were waited for; matrix products, arithmetic and copies ran while one was open for 27% of the time, Pallas kernels for 5%

profile of v3, /device:TPU:0, one launch (start us, length us, event | category | flops | bytes accessed | tf_op | source)
XLA Modules:
  0.0 131.9 jit_solution(17671428224784848175)
XLA Ops:
  0.7 2.4 %fusion.67 = (bf16[128,1536]{1,0:T(8,128)(2,1)}, bf16[128,1536]{1,0:T(8,128)(2,1)}, bf16[128,1536]{1,0:T(8,128)(2,1)}) fusion(bf16[384,1536]{1,0:T(8,128)(2,1)} %param.10), kind=kLoop, calls=%fused_computation.104 | loop fusion | bytes 2359296 | tf_op jit(solution)/shard_map/slice | solution.py:195
  3.0 3.0 %collective-permute-start.10 = (bf16[128,1536]{1,0:T(8,128)(2,1)}, bf16[128,1536]{1,0:T(8,128)(2,1)S(1)}, u32[]{:S(2)}, u32[]{:S(2)}) collective-permute-start(bf16[128,1536]{1,0:T(8,128)(2,1)} %get-tuple-element.31), channel_id=1, source_target_pairs={{0,8},{8,16},{16,24},{24,0},{1,9},{9,17},{17,25},{25,1},{2,10},{10... | collective-permute-start | bytes 1179656 | tf_op jit(solution)/shard_map/ppermute | solution.py:97
  6.0 1.6 %collective-permute-start.9 = (bf16[128,1536]{1,0:T(8,128)(2,1)}, bf16[128,1536]{1,0:T(8,128)(2,1)}, u32[]{:S(2)}, u32[]{:S(2)}) collective-permute-start(bf16[128,1536]{1,0:T(8,128)(2,1)} %get-tuple-element.32), channel_id=1, source_target_pairs={{0,8},{8,16},{16,24},{24,0},{1,9},{9,17},{17,25},{25,1},{2,10},{10... | collective-permute-start | bytes 1179656 | tf_op jit(solution)/shard_map/ppermute | solution.py:97
  7.8 0.9 pad_maximum_fusion
  8.7 1.6 %collective-permute-start.8 = (bf16[128,1536]{1,0:T(8,128)(2,1)}, bf16[128,1536]{1,0:T(8,128)(2,1)}, u32[]{:S(2)}, u32[]{:S(2)}) collective-permute-start(bf16[128,1536]{1,0:T(8,128)(2,1)} %get-tuple-element.30), channel_id=1, source_target_pairs={{0,8},{8,16},{16,24},{24,0},{1,9},{9,17},{17,25},{25,1},{2,10},{10... | collective-permute-start | bytes 1179656 | tf_op jit(solution)/shard_map/ppermute | solution.py:97
  10.3 0.9 broadcast_compare_fusion
  11.2 1.0 constant_dynamic-update-slice_fusion.1
  12.8 0.8 copy.70
  13.7 0.8 copy.62
  15.1 2.0 %convolution_convert_fusion = bf16[3,128,128]{2,1,0:T(8,128)(2,1)} fusion(bf16[256,3,128]{2,0,1:T(8,128)(2,1)S(1)} %copy.71, bf16[256,3,128]{2,0,1:T(8,128)(2,1)} %copy.70, bf16[256,3,128]{0,2,1:T(8,128)(2,1)S(1)} %bitcast.56, bf16[256,3,128]{0,2,1:T(8,128)(2,1)} %bitcast.54), kind=kOutput, calls=%fused_computation.24 | convolution fusion | flops 51953664 | bytes 884736 | tf_op jit(solution)/shard_map/tha,thb->hab/dot_general | solution.py:113
  17.1 1.9 %collective-permute-start.1 = (bf16[3,128,128]{2,1,0:T(8,128)(2,1)}, bf16[3,128,128]{2,1,0:T(8,128)(2,1)S(1)}, u32[]{:S(2)}, u32[]{:S(2)}) collective-permute-start(bf16[3,128,128]{2,1,0:T(8,128)(2,1)} %convolution_convert_fusion), channel_id=1, source_target_pairs={{0,8},{8,16},{16,24},{1,9},{9,17},{17,25},{2,10},{10,18},{18,26},{... | collective-permute-start | bytes 294920 | tf_op jit(solution)/shard_map/ppermute | solution.py:92
  19.0 4.7 %collective-permute-start.2 = (bf16[3,128,128]{2,1,0:T(8,128)(2,1)}, bf16[3,128,128]{2,1,0:T(8,128)(2,1)S(1)}, u32[]{:S(2)}, u32[]{:S(2)}) collective-permute-start(bf16[3,128,128]{2,1,0:T(8,128)(2,1)} %convolution_convert_fusion), channel_id=1, source_target_pairs={{0,16},{8,24},{1,17},{9,25},{2,18},{10,26},{3,19},{11,27},{4,20},{... | collective-permute-start | bytes 294920 | tf_op jit(solution)/shard_map/ppermute | solution.py:92
  24.1 1.3 collective-permute-start.3
  25.4 3.0 %fusion.2 = f32[3,128,512]{2,1,0:T(8,128)} fusion(pred[512,512]{1,0:T(8,128)(4,1)S(1)} %copy-done.8, bf16[256,3,128]{2,0,1:T(8,128)(2,1)} %copy-done.9, bf16[256,3,128]{2,0,1:T(8,128)(2,1)} %copy.70, bf16[256,3,128]{2,0,1:T(8,128)(2,1)S(1)} %copy.67, bf16[256,3,128]{2,0,1:T(8,128)(2,1)S(1)} %copy.66, bf16[256,3,128]{0,2,1:T(8,128)(2,1)S(1)} %bitcast.57, ...), kind=kOutput, calls=%fused_computation.4 | convolution fusion | flops 406585344 | bytes 2228224 | tf_op jit(solution)/shard_map/hts,shd->thd/dot_general | solution.py:113
  28.5 5.9 %collective-permute-done.8 = bf16[128,1536]{1,0:T(8,128)(2,1)} collective-permute-done((bf16[128,1536]{1,0:T(8,128)(2,1)}, bf16[128,1536]{1,0:T(8,128)(2,1)}, u32[]{:S(2)}, u32[]{:S(2)}) %collective-permute-start.8) | collective-permute-done | bytes 393248 | tf_op jit(solution)/shard_map/ppermute | solution.py:97
  34.3 0.9 collective-permute-start.13
  35.2 5.0 %collective-permute-start.12 = (bf16[128,1536]{1,0:T(8,128)(2,1)}, bf16[128,1536]{1,0:T(8,128)(2,1)}, u32[]{:S(2)}, u32[]{:S(2)}) collective-permute-start(bf16[128,1536]{1,0:T(8,128)(2,1)} %collective-permute-done.9), channel_id=1, source_target_pairs={{0,8},{8,16},{16,24},{24,0},{1,9},{9,17},{17,25},{25,1},{2,10},{10... | collective-permute-start | bytes 1179656 | tf_op jit(solution)/shard_map/ppermute | solution.py:97
  40.2 2.8 %collective-permute-start.11 = (bf16[128,1536]{1,0:T(8,128)(2,1)}, bf16[128,1536]{1,0:T(8,128)(2,1)}, u32[]{:S(2)}, u32[]{:S(2)}) collective-permute-start(bf16[128,1536]{1,0:T(8,128)(2,1)} %collective-permute-done.8), channel_id=1, source_target_pairs={{0,8},{8,16},{16,24},{24,0},{1,9},{9,17},{17,25},{25,1},{2,10},{10... | collective-permute-start | bytes 1179656 | tf_op jit(solution)/shard_map/ppermute | solution.py:97
  43.0 1.6 %fusion.22 = (f32[512]{0:T(512)S(1)}, f32[3,128,512]{2,1,0:T(8,128)S(1)}) fusion(f32[3,128,512]{2,1,0:T(8,128)} %fusion.2, bf16[256,3,128]{2,0,1:T(8,128)(2,1)} %copy-done.6, bf16[256,3,128]{2,0,1:T(8,128)(2,1)S(1)} %copy.66, bf16[3,128,128]{2,1,0:T(8,128)(2,1)S(1)} %collective-permute-done.3.refs_7_, ...), kind=kOutput, calls=%fused_computation.27 | convolution fusion | flops 52198912 | bytes 2263040 | tf_op jit(solution)/shard_map/thd,hde->the/dot_general | solution.py:113
  44.7 0.8 copy-done.5
  45.5 1.2 copy.75
  46.6 1.2 broadcast_multiply_fusion.refs_4_.refs_3_
  48.1 1.4 %multiply_convert_fusion = bf16[512,384]{0,1:T(8,128)(2,1)S(1)} fusion(f32[384]{0:T(512)S(1)} %dynamic_slice.27, f32[512]{0:T(512)S(1)} %fusion.50, f32[3,128,512]{2,1,0:T(8,128)} %copy-done.5), kind=kLoop, calls=%fused_computation.28 | loop fusion | flops 589824 | bytes 1183232 | tf_op jit(solution)/shard_map/convert_element_type | solution.py:232
  49.5 2.5 %collective-permute-start.5 = (bf16[512,384]{0,1:T(8,128)(2,1)S(1)}, bf16[512,384]{0,1:T(8,128)(2,1)S(1)}, u32[]{:S(2)}, u32[]{:S(2)}) collective-permute-start(bf16[512,384]{0,1:T(8,128)(2,1)S(1)} %multiply_convert_fusion), channel_id=1, source_target_pairs={{0,3},{1,2},{2,1},{3,0},{4,7},{5,6},{6,5},{7,4},{8,11},{9,10},{10,... | collective-permute-start | bytes 1179656 | tf_op jit(solution)/shard_map/ppermute | solution.py:87
  52.6 1.2 constant_dynamic-update-slice_fusion
  56.0 1.6 %fusion.73 = f32[512,128]{1,0:T(8,128)S(1)} fusion(bf16[512,1536]{1,0:T(8,128)(2,1)S(1)} %constant_dynamic-update-slice_fusion, bf16[128,1536]{1,0:T(8,128)(2,1)} %collective-permute-done.9), kind=kOutput, calls=%fused_computation.110 | convolution fusion | flops 201326592 | bytes 2228224 | tf_op jit(solution)/shard_map/dot_general | solution.py:238
  57.6 1.6 %fusion.71 = f32[512,128]{1,0:T(8,128)S(1)} fusion(bf16[512,1536]{1,0:T(8,128)(2,1)S(1)} %constant_dynamic-update-slice_fusion, bf16[128,1536]{1,0:T(8,128)(2,1)} %collective-permute-done.8), kind=kOutput, calls=%fused_computation.108 | convolution fusion | flops 201326592 | bytes 2228224 | tf_op jit(solution)/shard_map/dot_general | solution.py:238
  59.1 0.6 collective-permute-start.7
  59.8 1.6 %fusion.74 = f32[512,128]{1,0:T(8,128)S(1)} fusion(bf16[512,1536]{1,0:T(8,128)(2,1)S(1)} %constant_dynamic-update-slice_fusion, bf16[128,1536]{1,0:T(8,128)(2,1)} %collective-permute-done.13), kind=kOutput, calls=%fused_computation.111 | convolution fusion | flops 201326592 | bytes 2228224 | tf_op jit(solution)/shard_map/dot_general | solution.py:238
  61.4 1.6 %fusion.72 = f32[512,128]{1,0:T(8,128)S(1)} fusion(bf16[512,1536]{1,0:T(8,128)(2,1)S(1)} %constant_dynamic-update-slice_fusion, bf16[128,1536]{1,0:T(8,128)(2,1)} %collective-permute-done.12), kind=kOutput, calls=%fused_computation.109 | convolution fusion | flops 201326592 | bytes 2228224 | tf_op jit(solution)/shard_map/dot_general | solution.py:238
  63.0 1.4 %collective-permute-done.11 = bf16[128,1536]{1,0:T(8,128)(2,1)} collective-permute-done((bf16[128,1536]{1,0:T(8,128)(2,1)}, bf16[128,1536]{1,0:T(8,128)(2,1)}, u32[]{:S(2)}, u32[]{:S(2)}) %collective-permute-start.11) | collective-permute-done | bytes 393248 | tf_op jit(solution)/shard_map/ppermute | solution.py:97
  64.4 3.6 %collective-permute-start.15 = (bf16[128,1536]{1,0:T(8,128)(2,1)}, bf16[128,1536]{1,0:T(8,128)(2,1)S(1)}, u32[]{:S(2)}, u32[]{:S(2)}) collective-permute-start(bf16[128,1536]{1,0:T(8,128)(2,1)} %collective-permute-done.12), channel_id=1, source_target_pairs={{0,8},{8,16},{16,24},{24,0},{1,9},{9,17},{17,25},{25,1},{2,10},{10... | collective-permute-start | bytes 1179656 | tf_op jit(solution)/shard_map/ppermute | solution.py:97
  68.0 1.6 %fusion.70 = f32[512,128]{1,0:T(8,128)S(1)} fusion(bf16[512,1536]{1,0:T(8,128)(2,1)S(1)} %constant_dynamic-update-slice_fusion, bf16[128,1536]{1,0:T(8,128)(2,1)} %collective-permute-done.11), kind=kOutput, calls=%fused_computation.107 | convolution fusion | flops 201326592 | bytes 2228224 | tf_op jit(solution)/shard_map/dot_general | solution.py:238
  69.6 2.7 %collective-permute-start.14 = (bf16[128,1536]{1,0:T(8,128)(2,1)}, bf16[128,1536]{1,0:T(8,128)(2,1)S(1)}, u32[]{:S(2)}, u32[]{:S(2)}) collective-permute-start(bf16[128,1536]{1,0:T(8,128)(2,1)} %collective-permute-done.11), channel_id=1, source_target_pairs={{0,8},{8,16},{16,24},{24,0},{1,9},{9,17},{17,25},{25,1},{2,10},{10... | collective-permute-start | bytes 1179656 | tf_op jit(solution)/shard_map/ppermute | solution.py:97
  72.3 2.2 %fusion.3 = f32[512,1536]{1,0:T(8,128)S(1)} fusion(bf16[128,1536]{1,0:T(8,128)(2,1)S(1)} %collective-permute-done.10, bf16[128,1536]{1,0:T(8,128)(2,1)} %collective-permute-done.9, bf16[128,1536]{1,0:T(8,128)(2,1)} %collective-permute-done.8, bf16[512,384]{0,1:T(8,128)(2,1)S(1)} %collective-permute-done.5, bf16[512,384]{0,1:T(8,128)(2,1)S(1)} %collective-permute-done.6, ...), kind=kOutput, calls=%fused_computation.6 | convolution fusion | flops 608108544 | bytes 5898243 | tf_op jit(solution)/shard_map/dot_general | solution.py:265
  74.5 2.3 %fusion.9 = f32[512,1536]{1,0:T(8,128)S(1)} fusion(bf16[128,1536]{1,0:T(8,128)(2,1)} %collective-permute-done.13, bf16[128,1536]{1,0:T(8,128)(2,1)} %collective-permute-done.12, bf16[128,1536]{1,0:T(8,128)(2,1)} %collective-permute-done.11, bf16[512,384]{0,1:T(8,128)(2,1)S(1)} %collective-permute-done.5, bf16[512,384]{0,1:T(8,128)(2,1)S(1)} %collective-permute-done.6, ...), kind=kOutput, calls=%fused_computation.12 | convolution fusion | flops 608108544 | bytes 5898243 | tf_op jit(solution)/shard_map/dot_general | solution.py:265
  76.8 0.6 select_convert_fusion.3
  77.4 1.6 %collective-permute-start.25 = (bf16[512,128]{1,0:T(8,128)(2,1)S(1)}, bf16[512,128]{1,0:T(8,128)(2,1)S(1)}, u32[]{:S(2)}, u32[]{:S(2)}) collective-permute-start(bf16[512,128]{1,0:T(8,128)(2,1)S(1)} %get-tuple-element.33), channel_id=1, source_target_pairs={{0,1},{1,0},{2,3},{3,2},{4,5},{5,4},{6,7},{7,6},{8,9},{9,8},{10,11... | collective-permute-start | bytes 393224 | tf_op jit(solution)/shard_map/ppermute | solution.py:87
  79.0 1.5 %collective-permute-start.26 = (bf16[512,128]{1,0:T(8,128)(2,1)S(1)}, bf16[512,128]{1,0:T(8,128)(2,1)S(1)}, u32[]{:S(2)}, u32[]{:S(2)}) collective-permute-start(bf16[512,128]{1,0:T(8,128)(2,1)S(1)} %get-tuple-element.35), channel_id=1, source_target_pairs={{0,2},{1,3},{2,0},{3,1},{4,6},{5,7},{6,4},{7,5},{8,10},{9,11},{10,... | collective-permute-start | bytes 393224 | tf_op jit(solution)/shard_map/ppermute | solution.py:87
  81.0 2.9 %collective-permute-done.15 = bf16[128,1536]{1,0:T(8,128)(2,1)S(1)} collective-permute-done((bf16[128,1536]{1,0:T(8,128)(2,1)}, bf16[128,1536]{1,0:T(8,128)(2,1)S(1)}, u32[]{:S(2)}, u32[]{:S(2)}) %collective-permute-start.15) | collective-permute-done | bytes 393248 | tf_op jit(solution)/shard_map/ppermute | solution.py:97
  83.9 0.6 select_convert_fusion.6
  84.4 1.5 %collective-permute-start.22 = (bf16[512,128]{1,0:T(8,128)(2,1)S(1)}, bf16[512,128]{1,0:T(8,128)(2,1)S(1)}, u32[]{:S(2)}, u32[]{:S(2)}) collective-permute-start(bf16[512,128]{1,0:T(8,128)(2,1)S(1)} %get-tuple-element.36), channel_id=1, source_target_pairs={{0,1},{1,0},{2,3},{3,2},{4,5},{5,4},{6,7},{7,6},{8,9},{9,8},{10,11... | collective-permute-start | bytes 393224 | tf_op jit(solution)/shard_map/ppermute | solution.py:87
  86.0 4.1 %collective-permute-done.14 = bf16[128,1536]{1,0:T(8,128)(2,1)S(1)} collective-permute-done((bf16[128,1536]{1,0:T(8,128)(2,1)}, bf16[128,1536]{1,0:T(8,128)(2,1)S(1)}, u32[]{:S(2)}, u32[]{:S(2)}) %collective-permute-start.14) | collective-permute-done | bytes 393248 | tf_op jit(solution)/shard_map/ppermute | solution.py:97
  90.1 1.5 %collective-permute-start.23 = (bf16[512,128]{1,0:T(8,128)(2,1)S(1)}, bf16[512,128]{1,0:T(8,128)(2,1)S(1)}, u32[]{:S(2)}, u32[]{:S(2)}) collective-permute-start(bf16[512,128]{1,0:T(8,128)(2,1)S(1)} %get-tuple-element.38), channel_id=1, source_target_pairs={{0,2},{1,3},{2,0},{3,1},{4,6},{5,7},{6,4},{7,5},{8,10},{9,11},{10,... | collective-permute-start | bytes 393224 | tf_op jit(solution)/shard_map/ppermute | solution.py:87
  91.7 0.6 select_convert_fusion.9
  92.2 1.5 %collective-permute-start.24 = (bf16[512,128]{1,0:T(8,128)(2,1)S(1)}, bf16[512,128]{1,0:T(8,128)(2,1)S(1)}, u32[]{:S(2)}, u32[]{:S(2)}) collective-permute-start(bf16[512,128]{1,0:T(8,128)(2,1)S(1)} %get-tuple-element.37), channel_id=1, source_target_pairs={{0,3},{1,2},{2,1},{3,0},{4,7},{5,6},{6,5},{7,4},{8,11},{9,10},{10,... | collective-permute-start | bytes 393224 | tf_op jit(solution)/shard_map/ppermute | solution.py:87
  94.3 1.5 %collective-permute-start.20 = (bf16[512,128]{1,0:T(8,128)(2,1)S(1)}, bf16[512,128]{1,0:T(8,128)(2,1)S(1)}, u32[]{:S(2)}, u32[]{:S(2)}) collective-permute-start(bf16[512,128]{1,0:T(8,128)(2,1)S(1)} %get-tuple-element.41), channel_id=1, source_target_pairs={{0,2},{1,3},{2,0},{3,1},{4,6},{5,7},{6,4},{7,5},{8,10},{9,11},{10,... | collective-permute-start | bytes 393224 | tf_op jit(solution)/shard_map/ppermute | solution.py:87
  95.9 1.5 %collective-permute-start.21 = (bf16[512,128]{1,0:T(8,128)(2,1)S(1)}, bf16[512,128]{1,0:T(8,128)(2,1)S(1)}, u32[]{:S(2)}, u32[]{:S(2)}) collective-permute-start(bf16[512,128]{1,0:T(8,128)(2,1)S(1)} %get-tuple-element.40), channel_id=1, source_target_pairs={{0,3},{1,2},{2,1},{3,0},{4,7},{5,6},{6,5},{7,4},{8,11},{9,10},{10,... | collective-permute-start | bytes 393224 | tf_op jit(solution)/shard_map/ppermute | solution.py:87
  97.4 3.1 %collective-permute-done.23 = bf16[512,128]{1,0:T(8,128)(2,1)S(1)} collective-permute-done((bf16[512,128]{1,0:T(8,128)(2,1)S(1)}, bf16[512,128]{1,0:T(8,128)(2,1)S(1)}, u32[]{:S(2)}, u32[]{:S(2)}) %collective-permute-start.23) | collective-permute-done | bytes 131104 | tf_op jit(solution)/shard_map/ppermute | solution.py:87
  100.6 2.7 %collective-permute-done.20 = bf16[512,128]{1,0:T(8,128)(2,1)S(1)} collective-permute-done((bf16[512,128]{1,0:T(8,128)(2,1)S(1)}, bf16[512,128]{1,0:T(8,128)(2,1)S(1)}, u32[]{:S(2)}, u32[]{:S(2)}) %collective-permute-start.20) | collective-permute-done | bytes 131104 | tf_op jit(solution)/shard_map/ppermute | solution.py:87
  103.4 1.1 fusion.15
  104.5 1.2 scale_grad.1
  105.8 1.1 fusion.1.refs_0_
  107.6 1.1 back_state.1
  108.7 3.0 %local_grads.1 = (bf16[256,384]{1,0:T(8,128)(2,1)S(1)}, bf16[256,384]{1,0:T(8,128)(2,1)S(1)}, f32[2,256,384]{2,1,0:T(8,128)S(1)}, f32[2,256,384]{2,1,0:T(8,128)S(1)}) custom-call(s32[3]{0:T(128)S(1)} %pad_add_fusion.place_ref, bf16[256,768]{1,0:T(8,128)(2,1)S(1)} %copy-done.1, bf16[256,768]{1,0:T(8,128)(2,1)S(1)} %copy-done.2, bf16[256,768]{1,0:T(8,128)(2,1)S(1)} %copy-done, ...), custom_call_target="tpu_custom_call" | custom-call | flops 15000000512 | bytes 1 | tf_op jit(solution)/shard_map/local_grads/pallas_call | solution.py:135
  111.8 1.3 collective-permute-start.31
  113.1 1.3 collective-permute-start.32
  114.9 4.4 %collective-permute-done.31.refs_0_ = bf16[3,128,128]{2,1,0:T(8,128)(2,1)S(1)} collective-permute-done((bf16[3,128,128]{2,1,0:T(8,128)(2,1)S(1)}, bf16[3,128,128]{2,1,0:T(8,128)(2,1)S(1)}, u32[]{:S(2)}, u32[]{:S(2)}) %collective-permute-start.31) | collective-permute-done | bytes 98336 | tf_op jit(solution)/shard_map/ppermute | solution.py:92
  119.4 1.3 collective-permute-start.33
  120.7 4.7 %collective-permute-done.32.refs_1_ = bf16[3,128,128]{2,1,0:T(8,128)(2,1)S(1)} collective-permute-done((bf16[3,128,128]{2,1,0:T(8,128)(2,1)S(1)}, bf16[3,128,128]{2,1,0:T(8,128)(2,1)S(1)}, u32[]{:S(2)}, u32[]{:S(2)}) %collective-permute-start.32) | collective-permute-done | bytes 98336 | tf_op jit(solution)/shard_map/ppermute | solution.py:92
  125.4 2.3 %collective-permute-done.33.refs_2_ = bf16[3,128,128]{2,1,0:T(8,128)(2,1)S(1)} collective-permute-done((bf16[3,128,128]{2,1,0:T(8,128)(2,1)S(1)}, bf16[3,128,128]{2,1,0:T(8,128)(2,1)S(1)}, u32[]{:S(2)}, u32[]{:S(2)}) %collective-permute-start.33) | collective-permute-done | bytes 98336 | tf_op jit(solution)/shard_map/ppermute | solution.py:92
  127.7 0.6 sum_later.1.refs_4_
  128.3 1.7 %finish_early.1 = (bf16[256,1536]{1,0:T(8,128)(2,1)}, bf16[256,768]{1,0:T(8,128)(2,1)}, f32[8,128]{1,0:T(8,128)S(1)}) custom-call(s32[3]{0:T(128)S(1)} %pad_add_fusion.place_ref, f32[512,1536]{1,0:T(8,128)S(1)} %fusion.1.refs_0_, f32[256,1536]{1,0:T(8,128)S(1)} %collective-permute-done.17.refs_1_, bf16[256,384]{1,0:T(8,128)(2,1)S(1)} %get-tuple-element.20.refs_2_, ...), custom_call_target="tpu_custom_call" | custom-call | flops 1 | bytes 1 | tf_op jit(solution)/shard_map/finish_early/pallas_call | solution.py:135
  130.1 1.8 %far_grads.1 = (bf16[256,768]{1,0:T(8,128)(2,1)}, bf16[256,768]{1,0:T(8,128)(2,1)}) custom-call(s32[3]{0:T(128)S(1)} %pad_add_fusion.place_ref, bf16[256,768]{1,0:T(8,128)(2,1)S(1)} %copy-done.2, bf16[256,768]{1,0:T(8,128)(2,1)S(1)} %copy-done, f32[2,256,384]{2,1,0:T(8,128)S(1)} %get-tuple-element.24.refs_2_, ...), custom_call_target="tpu_custom_call" | custom-call | flops 1 | bytes 1 | tf_op jit(solution)/shard_map/far_grads/pallas_call | solution.py:135
  (87 shorter events, 7.5 us)
Async XLA Ops:
  0.6 7.0 %copy-start = (bf16[256,768]{1,0:T(8,128)(2,1)S(1)}, bf16[256,768]{1,0:T(8,128)(2,1)}, u32[]{:S(2)}) copy-start(bf16[256,768]{1,0:T(8,128)(2,1)} %refs_1_.3) | copy-start | bytes 1179652
  0.6 7.0 %copy-start.1 = (bf16[256,768]{1,0:T(8,128)(2,1)S(1)}, bf16[256,768]{1,0:T(8,128)(2,1)}, u32[]{:S(2)}) copy-start(bf16[256,768]{1,0:T(8,128)(2,1)} %refs_0_.2) | copy-start | bytes 1179652
  0.7 7.0 %copy-start.2 = (bf16[256,768]{1,0:T(8,128)(2,1)S(1)}, bf16[256,768]{1,0:T(8,128)(2,1)}, u32[]{:S(2)}) copy-start(bf16[256,768]{1,0:T(8,128)(2,1)} %refs_0_.3) | copy-start | bytes 1179652
  3.0 21.1 %collective-permute-start.10 = (bf16[128,1536]{1,0:T(8,128)(2,1)}, bf16[128,1536]{1,0:T(8,128)(2,1)S(1)}, u32[]{:S(2)}, u32[]{:S(2)}) collective-permute-start(bf16[128,1536]{1,0:T(8,128)(2,1)} %get-tuple-element.31), channel_id=1, source_target_pairs={{0,8},{8,16},{16,24},{24,0},{1,9},{9,17},{17,25},{25,1},{2,10},{10... | collective-permute-start | bytes 1179656 | tf_op jit(solution)/shard_map/ppermute | solution.py:97
  6.0 22.4 %collective-permute-start.9 = (bf16[128,1536]{1,0:T(8,128)(2,1)}, bf16[128,1536]{1,0:T(8,128)(2,1)}, u32[]{:S(2)}, u32[]{:S(2)}) collective-permute-start(bf16[128,1536]{1,0:T(8,128)(2,1)} %get-tuple-element.32), channel_id=1, source_target_pairs={{0,8},{8,16},{16,24},{24,0},{1,9},{9,17},{17,25},{25,1},{2,10},{10... | collective-permute-start | bytes 1179656 | tf_op jit(solution)/shard_map/ppermute | solution.py:97
  7.7 3.5 %copy-start.7 = (bf16[256,1536]{1,0:T(8,128)(2,1)S(1)}, bf16[256,1536]{1,0:T(8,128)(2,1)}, u32[]{:S(2)}) copy-start(bf16[256,1536]{1,0:T(8,128)(2,1)} %param.11) | copy-start | bytes 2359300
  8.7 5.9 %collective-permute-start = (bf16[3,256,384]{2,1,0:T(8,128)(2,1)}, bf16[3,256,384]{2,1,0:T(8,128)(2,1)S(1)}, u32[]{:S(2)}, u32[]{:S(2)}) collective-permute-start(bf16[3,256,384]{2,1,0:T(8,128)(2,1)} %pad_maximum_fusion), channel_id=1, source_target_pairs={{0,4},{4,0},{1,5},{5,1},{2,6},{6,2},{3,7},{7,3},{8,12},{12,8},{9,1... | collective-permute-start | bytes 1769480 | tf_op jit(solution)/shard_map/ppermute | solution.py:83
  8.7 25.6 %collective-permute-start.8 = (bf16[128,1536]{1,0:T(8,128)(2,1)}, bf16[128,1536]{1,0:T(8,128)(2,1)}, u32[]{:S(2)}, u32[]{:S(2)}) collective-permute-start(bf16[128,1536]{1,0:T(8,128)(2,1)} %get-tuple-element.30), channel_id=1, source_target_pairs={{0,8},{8,16},{16,24},{24,0},{1,9},{9,17},{17,25},{25,1},{2,10},{10... | collective-permute-start | bytes 1179656 | tf_op jit(solution)/shard_map/ppermute | solution.py:97
  11.2 3.3 %copy-start.10 = (f32[768]{0:T(1024)S(1)}, f32[768]{0:T(1024)}, u32[]{:S(2)}) copy-start(f32[768]{0:T(1024)} %param.9) | copy-start | bytes 9220
  14.8 10.6 %copy-start.8 = (pred[512,512]{1,0:T(8,128)(4,1)S(1)}, pred[512,512]{1,0:T(8,128)(4,1)}, u32[]{:S(2)}) copy-start(pred[512,512]{1,0:T(8,128)(4,1)} %broadcast_compare_fusion) | copy-start | bytes 786436
  15.0 8.8 %copy-start.9 = (bf16[256,3,128]{2,0,1:T(8,128)(2,1)}, bf16[256,3,128]{2,0,1:T(8,128)(2,1)S(1)}, u32[]{:S(2)}) copy-start(bf16[256,3,128]{2,0,1:T(8,128)(2,1)S(1)} %copy.71) | copy-start | bytes 589828
  17.1 18.1 %collective-permute-start.1 = (bf16[3,128,128]{2,1,0:T(8,128)(2,1)}, bf16[3,128,128]{2,1,0:T(8,128)(2,1)S(1)}, u32[]{:S(2)}, u32[]{:S(2)}) collective-permute-start(bf16[3,128,128]{2,1,0:T(8,128)(2,1)} %convolution_convert_fusion), channel_id=1, source_target_pairs={{0,8},{8,16},{16,24},{1,9},{9,17},{17,25},{2,10},{10,18},{18,26},{... | collective-permute-start | bytes 294920 | tf_op jit(solution)/shard_map/ppermute | solution.py:92
  19.0 21.2 %collective-permute-start.2 = (bf16[3,128,128]{2,1,0:T(8,128)(2,1)}, bf16[3,128,128]{2,1,0:T(8,128)(2,1)S(1)}, u32[]{:S(2)}, u32[]{:S(2)}) collective-permute-start(bf16[3,128,128]{2,1,0:T(8,128)(2,1)} %convolution_convert_fusion), channel_id=1, source_target_pairs={{0,16},{8,24},{1,17},{9,25},{2,18},{10,26},{3,19},{11,27},{4,20},{... | collective-permute-start | bytes 294920 | tf_op jit(solution)/shard_map/ppermute | solution.py:92
  24.1 4.4 %copy-start.6 = (bf16[256,3,128]{2,0,1:T(8,128)(2,1)}, bf16[256,3,128]{2,0,1:T(8,128)(2,1)S(1)}, u32[]{:S(2)}) copy-start(bf16[256,3,128]{2,0,1:T(8,128)(2,1)S(1)} %copy.67) | copy-start | bytes 589828
  24.1 18.9 %collective-permute-start.3 = (bf16[3,128,128]{2,1,0:T(8,128)(2,1)}, bf16[3,128,128]{2,1,0:T(8,128)(2,1)S(1)}, u32[]{:S(2)}, u32[]{:S(2)}) collective-permute-start(bf16[3,128,128]{2,1,0:T(8,128)(2,1)} %convolution_convert_fusion), channel_id=1, source_target_pairs={{0,24},{1,25},{2,26},{3,27},{4,28},{5,29},{6,30},{7,31}} | collective-permute-start | bytes 294920 | tf_op jit(solution)/shard_map/ppermute | solution.py:92
  28.4 23.6 %collective-permute-start.18 = (bf16[256,1536]{1,0:T(8,128)(2,1)}, bf16[256,1536]{1,0:T(8,128)(2,1)}, u32[]{:S(2)}, u32[]{:S(2)}) collective-permute-start(bf16[256,1536]{1,0:T(8,128)(2,1)} %param.11), channel_id=1, source_target_pairs={{0,4},{4,0},{1,5},{5,1},{2,6},{6,2},{3,7},{7,3},{8,12},{12,8},{9,1... | collective-permute-start | bytes 2359304 | tf_op jit(solution)/shard_map/ppermute | solution.py:83
  34.3 24.8 %collective-permute-start.13 = (bf16[128,1536]{1,0:T(8,128)(2,1)S(1)}, bf16[128,1536]{1,0:T(8,128)(2,1)}, u32[]{:S(2)}, u32[]{:S(2)}) collective-permute-start(bf16[128,1536]{1,0:T(8,128)(2,1)S(1)} %collective-permute-done.10), channel_id=1, source_target_pairs={{0,8},{8,16},{16,24},{24,0},{1,9},{9,17},{17,25},{25,1},{2,10},{10... | collective-permute-start | bytes 1179656 | tf_op jit(solution)/shard_map/ppermute | solution.py:97
  35.2 26.1 %collective-permute-start.12 = (bf16[128,1536]{1,0:T(8,128)(2,1)}, bf16[128,1536]{1,0:T(8,128)(2,1)}, u32[]{:S(2)}, u32[]{:S(2)}) collective-permute-start(bf16[128,1536]{1,0:T(8,128)(2,1)} %collective-permute-done.9), channel_id=1, source_target_pairs={{0,8},{8,16},{16,24},{24,0},{1,9},{9,17},{17,25},{25,1},{2,10},{10... | collective-permute-start | bytes 1179656 | tf_op jit(solution)/shard_map/ppermute | solution.py:97
  40.2 24.2 %collective-permute-start.11 = (bf16[128,1536]{1,0:T(8,128)(2,1)}, bf16[128,1536]{1,0:T(8,128)(2,1)}, u32[]{:S(2)}, u32[]{:S(2)}) collective-permute-start(bf16[128,1536]{1,0:T(8,128)(2,1)} %collective-permute-done.8), channel_id=1, source_target_pairs={{0,8},{8,16},{16,24},{24,0},{1,9},{9,17},{17,25},{25,1},{2,10},{10... | collective-permute-start | bytes 1179656 | tf_op jit(solution)/shard_map/ppermute | solution.py:97
  44.6 0.9 copy-start.5
  44.6 3.2 %collective-permute-start.4 = (f32[512]{0:T(512)S(1)}, f32[512]{0:T(512)S(1)}, u32[]{:S(2)}, u32[]{:S(2)}) collective-permute-start(f32[512]{0:T(512)S(1)} %get-tuple-element.53), channel_id=1, source_target_pairs={{0,4},{4,0},{1,5},{5,1},{2,6},{6,2},{3,7},{7,3},{8,12},{12,8},{9,1... | collective-permute-start | bytes 6152 | tf_op jit(solution)/shard_map/ppermute | solution.py:83
  48.0 4.5 %copy-start.3 = (bf16[512,1536]{1,0:T(8,128)(2,1)S(1)}, bf16[512,1536]{1,0:T(8,128)(2,1)}, u32[]{:S(2)}) copy-start(bf16[512,1536]{1,0:T(8,128)(2,1)} %constant_dynamic-update-slice_fusion.1) | copy-start | bytes 4718596
  48.0 5.7 %copy-start.4 = (bf16[384,1536]{1,0:T(8,128)(2,1)S(1)}, bf16[384,1536]{1,0:T(8,128)(2,1)}, u32[]{:S(2)}) copy-start(bf16[384,1536]{1,0:T(8,128)(2,1)} %param.10) | copy-start | bytes 3538948
  49.5 20.0 %collective-permute-start.5 = (bf16[512,384]{0,1:T(8,128)(2,1)S(1)}, bf16[512,384]{0,1:T(8,128)(2,1)S(1)}, u32[]{:S(2)}, u32[]{:S(2)}) collective-permute-start(bf16[512,384]{0,1:T(8,128)(2,1)S(1)} %multiply_convert_fusion), channel_id=1, source_target_pairs={{0,3},{1,2},{2,1},{3,0},{4,7},{5,6},{6,5},{7,4},{8,11},{9,10},{10,... | collective-permute-start | bytes 1179656 | tf_op jit(solution)/shard_map/ppermute | solution.py:87
  52.0 20.3 %collective-permute-start.6 = (bf16[512,384]{0,1:T(8,128)(2,1)S(1)}, bf16[512,384]{0,1:T(8,128)(2,1)S(1)}, u32[]{:S(2)}, u32[]{:S(2)}) collective-permute-start(bf16[512,384]{0,1:T(8,128)(2,1)S(1)} %multiply_convert_fusion), channel_id=1, source_target_pairs={{0,2},{1,3},{2,0},{3,1},{4,6},{5,7},{6,4},{7,5},{8,10},{9,11},{10,... | collective-permute-start | bytes 1179656 | tf_op jit(solution)/shard_map/ppermute | solution.py:87
  59.1 13.2 %collective-permute-start.7 = (bf16[512,384]{0,1:T(8,128)(2,1)S(1)}, bf16[512,384]{0,1:T(8,128)(2,1)S(1)}, u32[]{:S(2)}, u32[]{:S(2)}) collective-permute-start(bf16[512,384]{0,1:T(8,128)(2,1)S(1)} %multiply_convert_fusion), channel_id=1, source_target_pairs={{0,1},{1,0},{2,3},{3,2},{4,5},{5,4},{6,7},{7,6},{8,9},{9,8},{10,11... | collective-permute-start | bytes 1179656 | tf_op jit(solution)/shard_map/ppermute | solution.py:87
  61.3 15.5 %collective-permute-start.16 = (bf16[128,1536]{1,0:T(8,128)(2,1)}, bf16[128,1536]{1,0:T(8,128)(2,1)S(1)}, u32[]{:S(2)}, u32[]{:S(2)}) collective-permute-start(bf16[128,1536]{1,0:T(8,128)(2,1)} %collective-permute-done.13), channel_id=1, source_target_pairs={{0,8},{8,16},{16,24},{24,0},{1,9},{9,17},{17,25},{25,1},{2,10},{10... | collective-permute-start | bytes 1179656 | tf_op jit(solution)/shard_map/ppermute | solution.py:97
  64.4 19.5 %collective-permute-start.15 = (bf16[128,1536]{1,0:T(8,128)(2,1)}, bf16[128,1536]{1,0:T(8,128)(2,1)S(1)}, u32[]{:S(2)}, u32[]{:S(2)}) collective-permute-start(bf16[128,1536]{1,0:T(8,128)(2,1)} %collective-permute-done.12), channel_id=1, source_target_pairs={{0,8},{8,16},{16,24},{24,0},{1,9},{9,17},{17,25},{25,1},{2,10},{10... | collective-permute-start | bytes 1179656 | tf_op jit(solution)/shard_map/ppermute | solution.py:97
  69.6 20.5 %collective-permute-start.14 = (bf16[128,1536]{1,0:T(8,128)(2,1)}, bf16[128,1536]{1,0:T(8,128)(2,1)S(1)}, u32[]{:S(2)}, u32[]{:S(2)}) collective-permute-start(bf16[128,1536]{1,0:T(8,128)(2,1)} %collective-permute-done.11), channel_id=1, source_target_pairs={{0,8},{8,16},{16,24},{24,0},{1,9},{9,17},{17,25},{25,1},{2,10},{10... | collective-permute-start | bytes 1179656 | tf_op jit(solution)/shard_map/ppermute | solution.py:97
  77.4 14.8 %collective-permute-start.25 = (bf16[512,128]{1,0:T(8,128)(2,1)S(1)}, bf16[512,128]{1,0:T(8,128)(2,1)S(1)}, u32[]{:S(2)}, u32[]{:S(2)}) collective-permute-start(bf16[512,128]{1,0:T(8,128)(2,1)S(1)} %get-tuple-element.33), channel_id=1, source_target_pairs={{0,1},{1,0},{2,3},{3,2},{4,5},{5,4},{6,7},{7,6},{8,9},{9,8},{10,11... | collective-permute-start | bytes 393224 | tf_op jit(solution)/shard_map/ppermute | solution.py:87
  79.0 14.8 %collective-permute-start.26 = (bf16[512,128]{1,0:T(8,128)(2,1)S(1)}, bf16[512,128]{1,0:T(8,128)(2,1)S(1)}, u32[]{:S(2)}, u32[]{:S(2)}) collective-permute-start(bf16[512,128]{1,0:T(8,128)(2,1)S(1)} %get-tuple-element.35), channel_id=1, source_target_pairs={{0,2},{1,3},{2,0},{3,1},{4,6},{5,7},{6,4},{7,5},{8,10},{9,11},{10,... | collective-permute-start | bytes 393224 | tf_op jit(solution)/shard_map/ppermute | solution.py:87
  80.5 13.8 %collective-permute-start.27 = (bf16[512,128]{1,0:T(8,128)(2,1)S(1)}, bf16[512,128]{1,0:T(8,128)(2,1)S(1)}, u32[]{:S(2)}, u32[]{:S(2)}) collective-permute-start(bf16[512,128]{1,0:T(8,128)(2,1)S(1)} %get-tuple-element.34), channel_id=1, source_target_pairs={{0,3},{1,2},{2,1},{3,0},{4,7},{5,6},{6,5},{7,4},{8,11},{9,10},{10,... | collective-permute-start | bytes 393224 | tf_op jit(solution)/shard_map/ppermute | solution.py:87
  84.4 11.4 %collective-permute-start.22 = (bf16[512,128]{1,0:T(8,128)(2,1)S(1)}, bf16[512,128]{1,0:T(8,128)(2,1)S(1)}, u32[]{:S(2)}, u32[]{:S(2)}) collective-permute-start(bf16[512,128]{1,0:T(8,128)(2,1)S(1)} %get-tuple-element.36), channel_id=1, source_target_pairs={{0,1},{1,0},{2,3},{3,2},{4,5},{5,4},{6,7},{7,6},{8,9},{9,8},{10,11... | collective-permute-start | bytes 393224 | tf_op jit(solution)/shard_map/ppermute | solution.py:87
  90.1 10.3 %collective-permute-start.23 = (bf16[512,128]{1,0:T(8,128)(2,1)S(1)}, bf16[512,128]{1,0:T(8,128)(2,1)S(1)}, u32[]{:S(2)}, u32[]{:S(2)}) collective-permute-start(bf16[512,128]{1,0:T(8,128)(2,1)S(1)} %get-tuple-element.38), channel_id=1, source_target_pairs={{0,2},{1,3},{2,0},{3,1},{4,6},{5,7},{6,4},{7,5},{8,10},{9,11},{10,... | collective-permute-start | bytes 393224 | tf_op jit(solution)/shard_map/ppermute | solution.py:87
  92.2 8.2 %collective-permute-start.24 = (bf16[512,128]{1,0:T(8,128)(2,1)S(1)}, bf16[512,128]{1,0:T(8,128)(2,1)S(1)}, u32[]{:S(2)}, u32[]{:S(2)}) collective-permute-start(bf16[512,128]{1,0:T(8,128)(2,1)S(1)} %get-tuple-element.37), channel_id=1, source_target_pairs={{0,3},{1,2},{2,1},{3,0},{4,7},{5,6},{6,5},{7,4},{8,11},{9,10},{10,... | collective-permute-start | bytes 393224 | tf_op jit(solution)/shard_map/ppermute | solution.py:87
  93.7 6.8 %collective-permute-start.19 = (bf16[512,128]{1,0:T(8,128)(2,1)S(1)}, bf16[512,128]{1,0:T(8,128)(2,1)S(1)}, u32[]{:S(2)}, u32[]{:S(2)}) collective-permute-start(bf16[512,128]{1,0:T(8,128)(2,1)S(1)} %get-tuple-element.39), channel_id=1, source_target_pairs={{0,1},{1,0},{2,3},{3,2},{4,5},{5,4},{6,7},{7,6},{8,9},{9,8},{10,11... | collective-permute-start | bytes 393224 | tf_op jit(solution)/shard_map/ppermute | solution.py:87
  94.3 9.0 %collective-permute-start.20 = (bf16[512,128]{1,0:T(8,128)(2,1)S(1)}, bf16[512,128]{1,0:T(8,128)(2,1)S(1)}, u32[]{:S(2)}, u32[]{:S(2)}) collective-permute-start(bf16[512,128]{1,0:T(8,128)(2,1)S(1)} %get-tuple-element.41), channel_id=1, source_target_pairs={{0,2},{1,3},{2,0},{3,1},{4,6},{5,7},{6,4},{7,5},{8,10},{9,11},{10,... | collective-permute-start | bytes 393224 | tf_op jit(solution)/shard_map/ppermute | solution.py:87
  95.9 7.4 %collective-permute-start.21 = (bf16[512,128]{1,0:T(8,128)(2,1)S(1)}, bf16[512,128]{1,0:T(8,128)(2,1)S(1)}, u32[]{:S(2)}, u32[]{:S(2)}) collective-permute-start(bf16[512,128]{1,0:T(8,128)(2,1)S(1)} %get-tuple-element.40), channel_id=1, source_target_pairs={{0,3},{1,2},{2,1},{3,0},{4,7},{5,6},{6,5},{7,4},{8,11},{9,10},{10,... | collective-permute-start | bytes 393224 | tf_op jit(solution)/shard_map/ppermute | solution.py:87
  105.7 1.9 %collective-permute-start.28 = (f32[512,1]{1,0:T(8,128)S(1)}, f32[512,1]{1,0:T(8,128)S(1)}, u32[]{:S(2)}, u32[]{:S(2)}) collective-permute-start(f32[512,1]{1,0:T(8,128)S(1)} %get-tuple-element.18.refs_1_), channel_id=1, source_target_pairs={{0,4},{4,0},{1,5},{5,1},{2,6},{6,2},{3,7},{7,3},{8,12},{12,8},{9,1... | collective-permute-start | bytes 6152 | tf_op jit(solution)/shard_map/ppermute | solution.py:83
  107.1 21.3 %collective-permute-start.17 = (f32[256,1536]{1,0:T(8,128)S(1)}, f32[256,1536]{1,0:T(8,128)S(1)}, u32[]{:S(2)}, u32[]{:S(2)}) collective-permute-start(f32[256,1536]{1,0:T(8,128)S(1)} %slice.40), channel_id=1, source_target_pairs={{0,4},{4,0},{1,5},{5,1},{2,6},{6,2},{3,7},{7,3},{8,12},{12,8},{9,1... | collective-permute-start | bytes 4718600 | tf_op jit(solution)/shard_map/ppermute | solution.py:83
  111.7 18.4 %collective-permute-start.30 = (f32[2,256,384]{2,1,0:T(8,128)S(1)}, f32[2,256,384]{2,1,0:T(8,128)S(1)}, u32[]{:S(2)}, u32[]{:S(2)}) collective-permute-start(f32[2,256,384]{2,1,0:T(8,128)S(1)} %get-tuple-element.25), channel_id=1, source_target_pairs={{0,4},{4,0},{1,5},{5,1},{2,6},{6,2},{3,7},{7,3},{8,12},{12,8},{9,1... | collective-permute-start | bytes 2359304 | tf_op jit(solution)/shard_map/ppermute | solution.py:83
  111.8 7.5 %collective-permute-start.31 = (bf16[3,128,128]{2,1,0:T(8,128)(2,1)S(1)}, bf16[3,128,128]{2,1,0:T(8,128)(2,1)S(1)}, u32[]{:S(2)}, u32[]{:S(2)}) collective-permute-start(bf16[3,128,128]{2,1,0:T(8,128)(2,1)S(1)} %get-tuple-element.26), channel_id=1, source_target_pairs={{8,0},{16,8},{24,16},{9,1},{17,9},{25,17},{10,2},{18,10},{26,18},{... | collective-permute-start | bytes 294920 | tf_op jit(solution)/shard_map/ppermute | solution.py:92
  113.1 12.3 %collective-permute-start.32 = (bf16[3,128,128]{2,1,0:T(8,128)(2,1)S(1)}, bf16[3,128,128]{2,1,0:T(8,128)(2,1)S(1)}, u32[]{:S(2)}, u32[]{:S(2)}) collective-permute-start(bf16[3,128,128]{2,1,0:T(8,128)(2,1)S(1)} %get-tuple-element.26), channel_id=1, source_target_pairs={{16,0},{24,8},{17,1},{25,9},{18,2},{26,10},{19,3},{27,11},{20,4},{... | collective-permute-start | bytes 294920 | tf_op jit(solution)/shard_map/ppermute | solution.py:92
  114.4 13.9 %collective-permute-start.29 = (bf16[256,384]{1,0:T(8,128)(2,1)S(1)}, bf16[256,384]{1,0:T(8,128)(2,1)S(1)}, u32[]{:S(2)}, u32[]{:S(2)}) collective-permute-start(bf16[256,384]{1,0:T(8,128)(2,1)S(1)} %get-tuple-element.21), channel_id=1, source_target_pairs={{0,4},{4,0},{1,5},{5,1},{2,6},{6,2},{3,7},{7,3},{8,12},{12,8},{9,1... | collective-permute-start | bytes 589832 | tf_op jit(solution)/shard_map/ppermute | solution.py:83
  119.4 8.3 %collective-permute-start.33 = (bf16[3,128,128]{2,1,0:T(8,128)(2,1)S(1)}, bf16[3,128,128]{2,1,0:T(8,128)(2,1)S(1)}, u32[]{:S(2)}, u32[]{:S(2)}) collective-permute-start(bf16[3,128,128]{2,1,0:T(8,128)(2,1)S(1)} %get-tuple-element.26), channel_id=1, source_target_pairs={{24,0},{25,1},{26,2},{27,3},{28,4},{29,5},{30,6},{31,7}} | collective-permute-start | bytes 294920 | tf_op jit(solution)/shard_map/ppermute | solution.py:92
  128.2 1.8 %collective-permute-start.34 = (bf16[3,128,128]{2,1,0:T(8,128)(2,1)S(1)}, bf16[3,128,128]{2,1,0:T(8,128)(2,1)S(1)}, u32[]{:S(2)}, u32[]{:S(2)}) collective-permute-start(bf16[3,128,128]{2,1,0:T(8,128)(2,1)S(1)} %sum_later.1.refs_4_), channel_id=1, source_target_pairs={{0,4},{4,0},{1,5},{5,1},{2,6},{6,2},{3,7},{7,3},{8,12},{12,8},{9,1... | collective-permute-start | bytes 294920 | tf_op jit(solution)/shard_map/ppermute | solution.py:83

commit v4 on v3

--- a/solution.py
+++ b/solution.py
@@ -138,7 +138,7 @@
         out_shape=[jax.ShapeDtypeStruct(shape, dtype) for shape, dtype in outs],
         in_specs=[pl.BlockSpec(memory_space=pltpu.SMEM)] + in_specs + [anywhere] * n_after,
         out_specs=[block_of(shape) if store else whole for shape, _ in outs],
-        cost_estimate=pl.CostEstimate(flops=15 * 10**9 if name == "local_grads" else 1, bytes_accessed=1, transcendentals=0),
+        cost_estimate=pl.CostEstimate(flops=6 * 10**9 if name in ("local_grads", "back_state", "scale_grad") else 1, bytes_accessed=1, transcendentals=0),
         compiler_params=pltpu.CompilerParams(vmem_limit_bytes=40 * 2**20),
     )(place, *ins, *after)
 

time: 133 us -> 132 us (level)
  transfers between devices with their start and end apart: 35 -> 35, of which waited for: 9 -> 11; matrix products, arithmetic and copies ran while one was open for 27% -> 28% of each run, Pallas kernels for 5% -> 5%
where the time goes in v4:
time: 132 us; the launch traced here: 131 us
  starting transfers between devices  49.7 us (38%)
  waiting for transfers between devices  31.1 us (24%)
  matrix products  25 us (19%)
  local copies, waits for them, and re-layouts  9.95 us (8%)
  Pallas kernels  9.39 us (7%)
  other arithmetic  4.77 us (4%)
    ppermute x9, starting transfers between devices, seq_rotate(): return lax.ppermute(x, 'seq', [(i, (i + 1) % count) for i in range(count)])  21.3 us
    ppermute x12, starting transfers between devices, col_flip(): lax.ppermute(x, 'col', [(i, i ^ bits) for i in range(lax.axis_size('col'))])  15.3 us
    ppermute x9, waiting for transfers between devices, seq_rotate(): return lax.ppermute(x, 'seq', [(i, (i + 1) % count) for i in range(count)])  14.3 us
    ppermute x6, starting transfers between devices, seq_shift(): lax.ppermute(x, 'seq', [(i, i + step) for i in range(count) if 0 <= i + s...  11.8 us
    ppermute x6, waiting for transfers between devices, seq_shift(): lax.ppermute(x, 'seq', [(i, i + step) for i in range(count) if 0 <= i + s...  11.7 us
    dot_general x12, matrix products, head_split(): lax.dot_general(grads, w, (((1,), (1,)), ((), ())), preferred_element_typ...  11.7 us
    pallas_call x6, Pallas kernels, call(): pl.pallas_call(kernel, name=name, out_shape=[jax.ShapeDtypeStruct(shape,...  9.39 us
    dot_general x4, matrix products, head_split(): jnp.dot(features((z - s) % n_seq), weight, preferred_element_type=f32)  6.74 us
  transfers between devices with their start and end apart: 35, of which 11 were waited for; matrix products, arithmetic and copies ran while one was open for 28% of the time, Pallas kernels for 5%

profile of v4, /device:TPU:0, one launch (start us, length us, event | category | flops | bytes accessed | tf_op | source)
XLA Modules:
  0.0 131.3 jit_solution(4946581724329717817)
XLA Ops:
  0.7 2.4 %fusion.67 = (bf16[128,1536]{1,0:T(8,128)(2,1)}, bf16[128,1536]{1,0:T(8,128)(2,1)}, bf16[128,1536]{1,0:T(8,128)(2,1)}) fusion(bf16[384,1536]{1,0:T(8,128)(2,1)} %param.10), kind=kLoop, calls=%fused_computation.104 | loop fusion | bytes 2359296 | tf_op jit(solution)/shard_map/slice | solution.py:195
  3.0 3.0 %collective-permute-start.10 = (bf16[128,1536]{1,0:T(8,128)(2,1)}, bf16[128,1536]{1,0:T(8,128)(2,1)S(1)}, u32[]{:S(2)}, u32[]{:S(2)}) collective-permute-start(bf16[128,1536]{1,0:T(8,128)(2,1)} %get-tuple-element.31), channel_id=1, source_target_pairs={{0,8},{8,16},{16,24},{24,0},{1,9},{9,17},{17,25},{25,1},{2,10},{10... | collective-permute-start | bytes 1179656 | tf_op jit(solution)/shard_map/ppermute | solution.py:97
  6.0 1.6 %collective-permute-start.9 = (bf16[128,1536]{1,0:T(8,128)(2,1)}, bf16[128,1536]{1,0:T(8,128)(2,1)}, u32[]{:S(2)}, u32[]{:S(2)}) collective-permute-start(bf16[128,1536]{1,0:T(8,128)(2,1)} %get-tuple-element.32), channel_id=1, source_target_pairs={{0,8},{8,16},{16,24},{24,0},{1,9},{9,17},{17,25},{25,1},{2,10},{10... | collective-permute-start | bytes 1179656 | tf_op jit(solution)/shard_map/ppermute | solution.py:97
  7.8 0.9 pad_maximum_fusion
  8.7 1.6 %collective-permute-start.8 = (bf16[128,1536]{1,0:T(8,128)(2,1)}, bf16[128,1536]{1,0:T(8,128)(2,1)}, u32[]{:S(2)}, u32[]{:S(2)}) collective-permute-start(bf16[128,1536]{1,0:T(8,128)(2,1)} %get-tuple-element.30), channel_id=1, source_target_pairs={{0,8},{8,16},{16,24},{24,0},{1,9},{9,17},{17,25},{25,1},{2,10},{10... | collective-permute-start | bytes 1179656 | tf_op jit(solution)/shard_map/ppermute | solution.py:97
  10.3 0.9 broadcast_compare_fusion
  11.2 1.0 constant_dynamic-update-slice_fusion.1
  12.8 0.8 copy.70
  13.7 0.8 copy.62
  15.1 2.0 %convolution_convert_fusion = bf16[3,128,128]{2,1,0:T(8,128)(2,1)} fusion(bf16[256,3,128]{2,0,1:T(8,128)(2,1)S(1)} %copy.71, bf16[256,3,128]{2,0,1:T(8,128)(2,1)} %copy.70, bf16[256,3,128]{0,2,1:T(8,128)(2,1)S(1)} %bitcast.56, bf16[256,3,128]{0,2,1:T(8,128)(2,1)} %bitcast.54), kind=kOutput, calls=%fused_computation.24 | convolution fusion | flops 51953664 | bytes 884736 | tf_op jit(solution)/shard_map/tha,thb->hab/dot_general | solution.py:113
  17.1 1.9 %collective-permute-start.1 = (bf16[3,128,128]{2,1,0:T(8,128)(2,1)}, bf16[3,128,128]{2,1,0:T(8,128)(2,1)S(1)}, u32[]{:S(2)}, u32[]{:S(2)}) collective-permute-start(bf16[3,128,128]{2,1,0:T(8,128)(2,1)} %convolution_convert_fusion), channel_id=1, source_target_pairs={{0,8},{8,16},{16,24},{1,9},{9,17},{17,25},{2,10},{10,18},{18,26},{... | collective-permute-start | bytes 294920 | tf_op jit(solution)/shard_map/ppermute | solution.py:92
  19.0 4.7 %collective-permute-start.2 = (bf16[3,128,128]{2,1,0:T(8,128)(2,1)}, bf16[3,128,128]{2,1,0:T(8,128)(2,1)S(1)}, u32[]{:S(2)}, u32[]{:S(2)}) collective-permute-start(bf16[3,128,128]{2,1,0:T(8,128)(2,1)} %convolution_convert_fusion), channel_id=1, source_target_pairs={{0,16},{8,24},{1,17},{9,25},{2,18},{10,26},{3,19},{11,27},{4,20},{... | collective-permute-start | bytes 294920 | tf_op jit(solution)/shard_map/ppermute | solution.py:92
  24.1 1.3 collective-permute-start.3
  25.4 3.0 %fusion.2 = f32[3,128,512]{2,1,0:T(8,128)} fusion(pred[512,512]{1,0:T(8,128)(4,1)S(1)} %copy-done.8, bf16[256,3,128]{2,0,1:T(8,128)(2,1)} %copy-done.9, bf16[256,3,128]{2,0,1:T(8,128)(2,1)} %copy.70, bf16[256,3,128]{2,0,1:T(8,128)(2,1)S(1)} %copy.67, bf16[256,3,128]{2,0,1:T(8,128)(2,1)S(1)} %copy.66, bf16[256,3,128]{0,2,1:T(8,128)(2,1)S(1)} %bitcast.57, ...), kind=kOutput, calls=%fused_computation.4 | convolution fusion | flops 406585344 | bytes 2228224 | tf_op jit(solution)/shard_map/hts,shd->thd/dot_general | solution.py:113
  28.5 5.9 %collective-permute-done.8 = bf16[128,1536]{1,0:T(8,128)(2,1)} collective-permute-done((bf16[128,1536]{1,0:T(8,128)(2,1)}, bf16[128,1536]{1,0:T(8,128)(2,1)}, u32[]{:S(2)}, u32[]{:S(2)}) %collective-permute-start.8) | collective-permute-done | bytes 393248 | tf_op jit(solution)/shard_map/ppermute | solution.py:97
  34.3 0.9 collective-permute-start.13
  35.2 5.0 %collective-permute-start.12 = (bf16[128,1536]{1,0:T(8,128)(2,1)}, bf16[128,1536]{1,0:T(8,128)(2,1)}, u32[]{:S(2)}, u32[]{:S(2)}) collective-permute-start(bf16[128,1536]{1,0:T(8,128)(2,1)} %collective-permute-done.9), channel_id=1, source_target_pairs={{0,8},{8,16},{16,24},{24,0},{1,9},{9,17},{17,25},{25,1},{2,10},{10... | collective-permute-start | bytes 1179656 | tf_op jit(solution)/shard_map/ppermute | solution.py:97
  40.2 2.8 %collective-permute-start.11 = (bf16[128,1536]{1,0:T(8,128)(2,1)}, bf16[128,1536]{1,0:T(8,128)(2,1)}, u32[]{:S(2)}, u32[]{:S(2)}) collective-permute-start(bf16[128,1536]{1,0:T(8,128)(2,1)} %collective-permute-done.8), channel_id=1, source_target_pairs={{0,8},{8,16},{16,24},{24,0},{1,9},{9,17},{17,25},{25,1},{2,10},{10... | collective-permute-start | bytes 1179656 | tf_op jit(solution)/shard_map/ppermute | solution.py:97
  43.0 1.6 %fusion.22 = (f32[512]{0:T(512)S(1)}, f32[3,128,512]{2,1,0:T(8,128)S(1)}) fusion(f32[3,128,512]{2,1,0:T(8,128)} %fusion.2, bf16[256,3,128]{2,0,1:T(8,128)(2,1)} %copy-done.6, bf16[256,3,128]{2,0,1:T(8,128)(2,1)S(1)} %copy.66, bf16[3,128,128]{2,1,0:T(8,128)(2,1)S(1)} %collective-permute-done.3.refs_7_, ...), kind=kOutput, calls=%fused_computation.27 | convolution fusion | flops 52198912 | bytes 2263040 | tf_op jit(solution)/shard_map/thd,hde->the/dot_general | solution.py:113
  44.7 0.8 copy-done.5
  45.5 1.2 copy.75
  46.6 1.2 broadcast_multiply_fusion.refs_4_.refs_3_
  48.1 1.4 %multiply_convert_fusion = bf16[512,384]{0,1:T(8,128)(2,1)S(1)} fusion(f32[384]{0:T(512)S(1)} %dynamic_slice.27, f32[512]{0:T(512)S(1)} %fusion.50, f32[3,128,512]{2,1,0:T(8,128)} %copy-done.5), kind=kLoop, calls=%fused_computation.28 | loop fusion | flops 589824 | bytes 1183232 | tf_op jit(solution)/shard_map/convert_element_type | solution.py:232
  49.5 2.5 %collective-permute-start.5 = (bf16[512,384]{0,1:T(8,128)(2,1)S(1)}, bf16[512,384]{0,1:T(8,128)(2,1)S(1)}, u32[]{:S(2)}, u32[]{:S(2)}) collective-permute-start(bf16[512,384]{0,1:T(8,128)(2,1)S(1)} %multiply_convert_fusion), channel_id=1, source_target_pairs={{0,3},{1,2},{2,1},{3,0},{4,7},{5,6},{6,5},{7,4},{8,11},{9,10},{10,... | collective-permute-start | bytes 1179656 | tf_op jit(solution)/shard_map/ppermute | solution.py:87
  52.6 1.2 constant_dynamic-update-slice_fusion
  56.0 1.6 %fusion.73 = f32[512,128]{1,0:T(8,128)S(1)} fusion(bf16[512,1536]{1,0:T(8,128)(2,1)S(1)} %constant_dynamic-update-slice_fusion, bf16[128,1536]{1,0:T(8,128)(2,1)} %collective-permute-done.9), kind=kOutput, calls=%fused_computation.110 | convolution fusion | flops 201326592 | bytes 2228224 | tf_op jit(solution)/shard_map/dot_general | solution.py:238
  57.6 1.6 %fusion.71 = f32[512,128]{1,0:T(8,128)S(1)} fusion(bf16[512,1536]{1,0:T(8,128)(2,1)S(1)} %constant_dynamic-update-slice_fusion, bf16[128,1536]{1,0:T(8,128)(2,1)} %collective-permute-done.8), kind=kOutput, calls=%fused_computation.108 | convolution fusion | flops 201326592 | bytes 2228224 | tf_op jit(solution)/shard_map/dot_general | solution.py:238
  59.1 0.6 collective-permute-start.7
  59.8 1.6 %fusion.74 = f32[512,128]{1,0:T(8,128)S(1)} fusion(bf16[512,1536]{1,0:T(8,128)(2,1)S(1)} %constant_dynamic-update-slice_fusion, bf16[128,1536]{1,0:T(8,128)(2,1)} %collective-permute-done.13), kind=kOutput, calls=%fused_computation.111 | convolution fusion | flops 201326592 | bytes 2228224 | tf_op jit(solution)/shard_map/dot_general | solution.py:238
  61.4 1.6 %fusion.72 = f32[512,128]{1,0:T(8,128)S(1)} fusion(bf16[512,1536]{1,0:T(8,128)(2,1)S(1)} %constant_dynamic-update-slice_fusion, bf16[128,1536]{1,0:T(8,128)(2,1)} %collective-permute-done.12), kind=kOutput, calls=%fused_computation.109 | convolution fusion | flops 201326592 | bytes 2228224 | tf_op jit(solution)/shard_map/dot_general | solution.py:238
  63.0 1.4 %collective-permute-done.11 = bf16[128,1536]{1,0:T(8,128)(2,1)} collective-permute-done((bf16[128,1536]{1,0:T(8,128)(2,1)}, bf16[128,1536]{1,0:T(8,128)(2,1)}, u32[]{:S(2)}, u32[]{:S(2)}) %collective-permute-start.11) | collective-permute-done | bytes 393248 | tf_op jit(solution)/shard_map/ppermute | solution.py:97
  64.4 3.6 %collective-permute-start.15 = (bf16[128,1536]{1,0:T(8,128)(2,1)}, bf16[128,1536]{1,0:T(8,128)(2,1)S(1)}, u32[]{:S(2)}, u32[]{:S(2)}) collective-permute-start(bf16[128,1536]{1,0:T(8,128)(2,1)} %collective-permute-done.12), channel_id=1, source_target_pairs={{0,8},{8,16},{16,24},{24,0},{1,9},{9,17},{17,25},{25,1},{2,10},{10... | collective-permute-start | bytes 1179656 | tf_op jit(solution)/shard_map/ppermute | solution.py:97
  68.0 1.6 %fusion.70 = f32[512,128]{1,0:T(8,128)S(1)} fusion(bf16[512,1536]{1,0:T(8,128)(2,1)S(1)} %constant_dynamic-update-slice_fusion, bf16[128,1536]{1,0:T(8,128)(2,1)} %collective-permute-done.11), kind=kOutput, calls=%fused_computation.107 | convolution fusion | flops 201326592 | bytes 2228224 | tf_op jit(solution)/shard_map/dot_general | solution.py:238
  69.6 2.7 %collective-permute-start.14 = (bf16[128,1536]{1,0:T(8,128)(2,1)}, bf16[128,1536]{1,0:T(8,128)(2,1)S(1)}, u32[]{:S(2)}, u32[]{:S(2)}) collective-permute-start(bf16[128,1536]{1,0:T(8,128)(2,1)} %collective-permute-done.11), channel_id=1, source_target_pairs={{0,8},{8,16},{16,24},{24,0},{1,9},{9,17},{17,25},{25,1},{2,10},{10... | collective-permute-start | bytes 1179656 | tf_op jit(solution)/shard_map/ppermute | solution.py:97
  72.3 2.2 %fusion.3 = f32[512,1536]{1,0:T(8,128)S(1)} fusion(bf16[128,1536]{1,0:T(8,128)(2,1)S(1)} %collective-permute-done.10, bf16[128,1536]{1,0:T(8,128)(2,1)} %collective-permute-done.9, bf16[128,1536]{1,0:T(8,128)(2,1)} %collective-permute-done.8, bf16[512,384]{0,1:T(8,128)(2,1)S(1)} %collective-permute-done.5, bf16[512,384]{0,1:T(8,128)(2,1)S(1)} %collective-permute-done.6, ...), kind=kOutput, calls=%fused_computation.6 | convolution fusion | flops 608108544 | bytes 5898243 | tf_op jit(solution)/shard_map/dot_general | solution.py:265
  74.5 2.3 %fusion.9 = f32[512,1536]{1,0:T(8,128)S(1)} fusion(bf16[128,1536]{1,0:T(8,128)(2,1)} %collective-permute-done.13, bf16[128,1536]{1,0:T(8,128)(2,1)} %collective-permute-done.12, bf16[128,1536]{1,0:T(8,128)(2,1)} %collective-permute-done.11, bf16[512,384]{0,1:T(8,128)(2,1)S(1)} %collective-permute-done.5, bf16[512,384]{0,1:T(8,128)(2,1)S(1)} %collective-permute-done.6, ...), kind=kOutput, calls=%fused_computation.12 | convolution fusion | flops 608108544 | bytes 5898243 | tf_op jit(solution)/shard_map/dot_general | solution.py:265
  76.8 0.6 select_convert_fusion.3
  77.4 1.6 %collective-permute-start.25 = (bf16[512,128]{1,0:T(8,128)(2,1)S(1)}, bf16[512,128]{1,0:T(8,128)(2,1)S(1)}, u32[]{:S(2)}, u32[]{:S(2)}) collective-permute-start(bf16[512,128]{1,0:T(8,128)(2,1)S(1)} %get-tuple-element.33), channel_id=1, source_target_pairs={{0,1},{1,0},{2,3},{3,2},{4,5},{5,4},{6,7},{7,6},{8,9},{9,8},{10,11... | collective-permute-start | bytes 393224 | tf_op jit(solution)/shard_map/ppermute | solution.py:87
  79.0 1.5 %collective-permute-start.26 = (bf16[512,128]{1,0:T(8,128)(2,1)S(1)}, bf16[512,128]{1,0:T(8,128)(2,1)S(1)}, u32[]{:S(2)}, u32[]{:S(2)}) collective-permute-start(bf16[512,128]{1,0:T(8,128)(2,1)S(1)} %get-tuple-element.35), channel_id=1, source_target_pairs={{0,2},{1,3},{2,0},{3,1},{4,6},{5,7},{6,4},{7,5},{8,10},{9,11},{10,... | collective-permute-start | bytes 393224 | tf_op jit(solution)/shard_map/ppermute | solution.py:87
  81.0 2.9 %collective-permute-done.15 = bf16[128,1536]{1,0:T(8,128)(2,1)S(1)} collective-permute-done((bf16[128,1536]{1,0:T(8,128)(2,1)}, bf16[128,1536]{1,0:T(8,128)(2,1)S(1)}, u32[]{:S(2)}, u32[]{:S(2)}) %collective-permute-start.15) | collective-permute-done | bytes 393248 | tf_op jit(solution)/shard_map/ppermute | solution.py:97
  84.4 1.5 %collective-permute-start.22 = (bf16[512,128]{1,0:T(8,128)(2,1)S(1)}, bf16[512,128]{1,0:T(8,128)(2,1)S(1)}, u32[]{:S(2)}, u32[]{:S(2)}) collective-permute-start(bf16[512,128]{1,0:T(8,128)(2,1)S(1)} %get-tuple-element.36), channel_id=1, source_target_pairs={{0,1},{1,0},{2,3},{3,2},{4,5},{5,4},{6,7},{7,6},{8,9},{9,8},{10,11... | collective-permute-start | bytes 393224 | tf_op jit(solution)/shard_map/ppermute | solution.py:87
  86.0 4.1 %collective-permute-done.14 = bf16[128,1536]{1,0:T(8,128)(2,1)S(1)} collective-permute-done((bf16[128,1536]{1,0:T(8,128)(2,1)}, bf16[128,1536]{1,0:T(8,128)(2,1)S(1)}, u32[]{:S(2)}, u32[]{:S(2)}) %collective-permute-start.14) | collective-permute-done | bytes 393248 | tf_op jit(solution)/shard_map/ppermute | solution.py:97
  90.1 1.5 %collective-permute-start.23 = (bf16[512,128]{1,0:T(8,128)(2,1)S(1)}, bf16[512,128]{1,0:T(8,128)(2,1)S(1)}, u32[]{:S(2)}, u32[]{:S(2)}) collective-permute-start(bf16[512,128]{1,0:T(8,128)(2,1)S(1)} %get-tuple-element.38), channel_id=1, source_target_pairs={{0,2},{1,3},{2,0},{3,1},{4,6},{5,7},{6,4},{7,5},{8,10},{9,11},{10,... | collective-permute-start | bytes 393224 | tf_op jit(solution)/shard_map/ppermute | solution.py:87
  91.7 1.1 fusion.15
  92.7 0.6 select_convert_fusion.9
  93.3 1.5 %collective-permute-start.24 = (bf16[512,128]{1,0:T(8,128)(2,1)S(1)}, bf16[512,128]{1,0:T(8,128)(2,1)S(1)}, u32[]{:S(2)}, u32[]{:S(2)}) collective-permute-start(bf16[512,128]{1,0:T(8,128)(2,1)S(1)} %get-tuple-element.37), channel_id=1, source_target_pairs={{0,3},{1,2},{2,1},{3,0},{4,7},{5,6},{6,5},{7,4},{8,11},{9,10},{10,... | collective-permute-start | bytes 393224 | tf_op jit(solution)/shard_map/ppermute | solution.py:87
  95.4 1.5 %collective-permute-start.20 = (bf16[512,128]{1,0:T(8,128)(2,1)S(1)}, bf16[512,128]{1,0:T(8,128)(2,1)S(1)}, u32[]{:S(2)}, u32[]{:S(2)}) collective-permute-start(bf16[512,128]{1,0:T(8,128)(2,1)S(1)} %get-tuple-element.41), channel_id=1, source_target_pairs={{0,2},{1,3},{2,0},{3,1},{4,6},{5,7},{6,4},{7,5},{8,10},{9,11},{10,... | collective-permute-start | bytes 393224 | tf_op jit(solution)/shard_map/ppermute | solution.py:87
  97.0 1.5 %collective-permute-start.21 = (bf16[512,128]{1,0:T(8,128)(2,1)S(1)}, bf16[512,128]{1,0:T(8,128)(2,1)S(1)}, u32[]{:S(2)}, u32[]{:S(2)}) collective-permute-start(bf16[512,128]{1,0:T(8,128)(2,1)S(1)} %get-tuple-element.40), channel_id=1, source_target_pairs={{0,3},{1,2},{2,1},{3,0},{4,7},{5,6},{6,5},{7,4},{8,11},{9,10},{10,... | collective-permute-start | bytes 393224 | tf_op jit(solution)/shard_map/ppermute | solution.py:87
  98.5 0.9 collective-permute-done.23
  99.4 0.9 collective-permute-done.24
  100.6 2.9 %collective-permute-done.20 = bf16[512,128]{1,0:T(8,128)(2,1)S(1)} collective-permute-done((bf16[512,128]{1,0:T(8,128)(2,1)S(1)}, bf16[512,128]{1,0:T(8,128)(2,1)S(1)}, u32[]{:S(2)}, u32[]{:S(2)}) %collective-permute-start.20) | collective-permute-done | bytes 131104 | tf_op jit(solution)/shard_map/ppermute | solution.py:87
  103.6 1.2 scale_grad.1
  104.9 1.2 fusion.1.refs_0_
  106.8 1.1 back_state.1
  107.9 3.0 %local_grads.1 = (bf16[256,384]{1,0:T(8,128)(2,1)S(1)}, bf16[256,384]{1,0:T(8,128)(2,1)S(1)}, f32[2,256,384]{2,1,0:T(8,128)S(1)}, f32[2,256,384]{2,1,0:T(8,128)S(1)}) custom-call(s32[3]{0:T(128)S(1)} %pad_add_fusion.place_ref, bf16[256,768]{1,0:T(8,128)(2,1)S(1)} %copy-done.2, bf16[256,768]{1,0:T(8,128)(2,1)S(1)} %copy-done.1, bf16[256,768]{1,0:T(8,128)(2,1)S(1)} %copy-done, ...), custom_call_target="tpu_custom_call" | custom-call | flops 6000000000 | bytes 1 | tf_op jit(solution)/shard_map/local_grads/pallas_call | solution.py:135
  111.0 1.3 collective-permute-start.31
  112.3 1.3 collective-permute-start.32
  114.1 4.7 %collective-permute-done.31.refs_0_ = bf16[3,128,128]{2,1,0:T(8,128)(2,1)S(1)} collective-permute-done((bf16[3,128,128]{2,1,0:T(8,128)(2,1)S(1)}, bf16[3,128,128]{2,1,0:T(8,128)(2,1)S(1)}, u32[]{:S(2)}, u32[]{:S(2)}) %collective-permute-start.31) | collective-permute-done | bytes 98336 | tf_op jit(solution)/shard_map/ppermute | solution.py:92
  118.8 1.3 collective-permute-start.33
  120.1 4.7 %collective-permute-done.32.refs_1_ = bf16[3,128,128]{2,1,0:T(8,128)(2,1)S(1)} collective-permute-done((bf16[3,128,128]{2,1,0:T(8,128)(2,1)S(1)}, bf16[3,128,128]{2,1,0:T(8,128)(2,1)S(1)}, u32[]{:S(2)}, u32[]{:S(2)}) %collective-permute-start.32) | collective-permute-done | bytes 98336 | tf_op jit(solution)/shard_map/ppermute | solution.py:92
  124.8 2.3 %collective-permute-done.33.refs_2_ = bf16[3,128,128]{2,1,0:T(8,128)(2,1)S(1)} collective-permute-done((bf16[3,128,128]{2,1,0:T(8,128)(2,1)S(1)}, bf16[3,128,128]{2,1,0:T(8,128)(2,1)S(1)}, u32[]{:S(2)}, u32[]{:S(2)}) %collective-permute-start.33) | collective-permute-done | bytes 98336 | tf_op jit(solution)/shard_map/ppermute | solution.py:92
  127.1 0.6 sum_later.1.refs_4_
  127.8 1.7 %finish_early.1 = (bf16[256,1536]{1,0:T(8,128)(2,1)}, bf16[256,768]{1,0:T(8,128)(2,1)}, f32[8,128]{1,0:T(8,128)S(1)}) custom-call(s32[3]{0:T(128)S(1)} %pad_add_fusion.place_ref, f32[512,1536]{1,0:T(8,128)S(1)} %fusion.1.refs_0_, f32[256,1536]{1,0:T(8,128)S(1)} %collective-permute-done.17.refs_1_, bf16[256,384]{1,0:T(8,128)(2,1)S(1)} %get-tuple-element.20.refs_2_, ...), custom_call_target="tpu_custom_call" | custom-call | flops 1 | bytes 1 | tf_op jit(solution)/shard_map/finish_early/pallas_call | solution.py:135
  129.5 1.8 %far_grads.1 = (bf16[256,768]{1,0:T(8,128)(2,1)}, bf16[256,768]{1,0:T(8,128)(2,1)}) custom-call(s32[3]{0:T(128)S(1)} %pad_add_fusion.place_ref, bf16[256,768]{1,0:T(8,128)(2,1)S(1)} %copy-done.1, bf16[256,768]{1,0:T(8,128)(2,1)S(1)} %copy-done, f32[2,256,384]{2,1,0:T(8,128)S(1)} %get-tuple-element.24.refs_2_, ...), custom_call_target="tpu_custom_call" | custom-call | flops 1 | bytes 1 | tf_op jit(solution)/shard_map/far_grads/pallas_call | solution.py:135
  (87 shorter events, 8.3 us)
Async XLA Ops:
  0.6 7.0 %copy-start = (bf16[256,768]{1,0:T(8,128)(2,1)S(1)}, bf16[256,768]{1,0:T(8,128)(2,1)}, u32[]{:S(2)}) copy-start(bf16[256,768]{1,0:T(8,128)(2,1)} %refs_1_.3) | copy-start | bytes 1179652
  0.6 7.0 %copy-start.2 = (bf16[256,768]{1,0:T(8,128)(2,1)S(1)}, bf16[256,768]{1,0:T(8,128)(2,1)}, u32[]{:S(2)}) copy-start(bf16[256,768]{1,0:T(8,128)(2,1)} %refs_0_.2) | copy-start | bytes 1179652
  0.7 7.0 %copy-start.1 = (bf16[256,768]{1,0:T(8,128)(2,1)S(1)}, bf16[256,768]{1,0:T(8,128)(2,1)}, u32[]{:S(2)}) copy-start(bf16[256,768]{1,0:T(8,128)(2,1)} %refs_0_.3) | copy-start | bytes 1179652
  3.0 21.1 %collective-permute-start.10 = (bf16[128,1536]{1,0:T(8,128)(2,1)}, bf16[128,1536]{1,0:T(8,128)(2,1)S(1)}, u32[]{:S(2)}, u32[]{:S(2)}) collective-permute-start(bf16[128,1536]{1,0:T(8,128)(2,1)} %get-tuple-element.31), channel_id=1, source_target_pairs={{0,8},{8,16},{16,24},{24,0},{1,9},{9,17},{17,25},{25,1},{2,10},{10... | collective-permute-start | bytes 1179656 | tf_op jit(solution)/shard_map/ppermute | solution.py:97
  6.0 22.4 %collective-permute-start.9 = (bf16[128,1536]{1,0:T(8,128)(2,1)}, bf16[128,1536]{1,0:T(8,128)(2,1)}, u32[]{:S(2)}, u32[]{:S(2)}) collective-permute-start(bf16[128,1536]{1,0:T(8,128)(2,1)} %get-tuple-element.32), channel_id=1, source_target_pairs={{0,8},{8,16},{16,24},{24,0},{1,9},{9,17},{17,25},{25,1},{2,10},{10... | collective-permute-start | bytes 1179656 | tf_op jit(solution)/shard_map/ppermute | solution.py:97
  7.7 3.5 %copy-start.7 = (bf16[256,1536]{1,0:T(8,128)(2,1)S(1)}, bf16[256,1536]{1,0:T(8,128)(2,1)}, u32[]{:S(2)}) copy-start(bf16[256,1536]{1,0:T(8,128)(2,1)} %param.11) | copy-start | bytes 2359300
  8.7 5.9 %collective-permute-start = (bf16[3,256,384]{2,1,0:T(8,128)(2,1)}, bf16[3,256,384]{2,1,0:T(8,128)(2,1)S(1)}, u32[]{:S(2)}, u32[]{:S(2)}) collective-permute-start(bf16[3,256,384]{2,1,0:T(8,128)(2,1)} %pad_maximum_fusion), channel_id=1, source_target_pairs={{0,4},{4,0},{1,5},{5,1},{2,6},{6,2},{3,7},{7,3},{8,12},{12,8},{9,1... | collective-permute-start | bytes 1769480 | tf_op jit(solution)/shard_map/ppermute | solution.py:83
  8.7 25.6 %collective-permute-start.8 = (bf16[128,1536]{1,0:T(8,128)(2,1)}, bf16[128,1536]{1,0:T(8,128)(2,1)}, u32[]{:S(2)}, u32[]{:S(2)}) collective-permute-start(bf16[128,1536]{1,0:T(8,128)(2,1)} %get-tuple-element.30), channel_id=1, source_target_pairs={{0,8},{8,16},{16,24},{24,0},{1,9},{9,17},{17,25},{25,1},{2,10},{10... | collective-permute-start | bytes 1179656 | tf_op jit(solution)/shard_map/ppermute | solution.py:97
  11.2 3.3 %copy-start.10 = (f32[768]{0:T(1024)S(1)}, f32[768]{0:T(1024)}, u32[]{:S(2)}) copy-start(f32[768]{0:T(1024)} %param.9) | copy-start | bytes 9220
  14.8 10.6 %copy-start.8 = (pred[512,512]{1,0:T(8,128)(4,1)S(1)}, pred[512,512]{1,0:T(8,128)(4,1)}, u32[]{:S(2)}) copy-start(pred[512,512]{1,0:T(8,128)(4,1)} %broadcast_compare_fusion) | copy-start | bytes 786436
  15.0 8.8 %copy-start.9 = (bf16[256,3,128]{2,0,1:T(8,128)(2,1)}, bf16[256,3,128]{2,0,1:T(8,128)(2,1)S(1)}, u32[]{:S(2)}) copy-start(bf16[256,3,128]{2,0,1:T(8,128)(2,1)S(1)} %copy.71) | copy-start | bytes 589828
  17.1 18.1 %collective-permute-start.1 = (bf16[3,128,128]{2,1,0:T(8,128)(2,1)}, bf16[3,128,128]{2,1,0:T(8,128)(2,1)S(1)}, u32[]{:S(2)}, u32[]{:S(2)}) collective-permute-start(bf16[3,128,128]{2,1,0:T(8,128)(2,1)} %convolution_convert_fusion), channel_id=1, source_target_pairs={{0,8},{8,16},{16,24},{1,9},{9,17},{17,25},{2,10},{10,18},{18,26},{... | collective-permute-start | bytes 294920 | tf_op jit(solution)/shard_map/ppermute | solution.py:92
  19.0 21.2 %collective-permute-start.2 = (bf16[3,128,128]{2,1,0:T(8,128)(2,1)}, bf16[3,128,128]{2,1,0:T(8,128)(2,1)S(1)}, u32[]{:S(2)}, u32[]{:S(2)}) collective-permute-start(bf16[3,128,128]{2,1,0:T(8,128)(2,1)} %convolution_convert_fusion), channel_id=1, source_target_pairs={{0,16},{8,24},{1,17},{9,25},{2,18},{10,26},{3,19},{11,27},{4,20},{... | collective-permute-start | bytes 294920 | tf_op jit(solution)/shard_map/ppermute | solution.py:92
  24.1 4.4 %copy-start.6 = (bf16[256,3,128]{2,0,1:T(8,128)(2,1)}, bf16[256,3,128]{2,0,1:T(8,128)(2,1)S(1)}, u32[]{:S(2)}) copy-start(bf16[256,3,128]{2,0,1:T(8,128)(2,1)S(1)} %copy.67) | copy-start | bytes 589828
  24.1 18.9 %collective-permute-start.3 = (bf16[3,128,128]{2,1,0:T(8,128)(2,1)}, bf16[3,128,128]{2,1,0:T(8,128)(2,1)S(1)}, u32[]{:S(2)}, u32[]{:S(2)}) collective-permute-start(bf16[3,128,128]{2,1,0:T(8,128)(2,1)} %convolution_convert_fusion), channel_id=1, source_target_pairs={{0,24},{1,25},{2,26},{3,27},{4,28},{5,29},{6,30},{7,31}} | collective-permute-start | bytes 294920 | tf_op jit(solution)/shard_map/ppermute | solution.py:92
  28.4 23.6 %collective-permute-start.18 = (bf16[256,1536]{1,0:T(8,128)(2,1)}, bf16[256,1536]{1,0:T(8,128)(2,1)}, u32[]{:S(2)}, u32[]{:S(2)}) collective-permute-start(bf16[256,1536]{1,0:T(8,128)(2,1)} %param.11), channel_id=1, source_target_pairs={{0,4},{4,0},{1,5},{5,1},{2,6},{6,2},{3,7},{7,3},{8,12},{12,8},{9,1... | collective-permute-start | bytes 2359304 | tf_op jit(solution)/shard_map/ppermute | solution.py:83
  34.3 24.8 %collective-permute-start.13 = (bf16[128,1536]{1,0:T(8,128)(2,1)S(1)}, bf16[128,1536]{1,0:T(8,128)(2,1)}, u32[]{:S(2)}, u32[]{:S(2)}) collective-permute-start(bf16[128,1536]{1,0:T(8,128)(2,1)S(1)} %collective-permute-done.10), channel_id=1, source_target_pairs={{0,8},{8,16},{16,24},{24,0},{1,9},{9,17},{17,25},{25,1},{2,10},{10... | collective-permute-start | bytes 1179656 | tf_op jit(solution)/shard_map/ppermute | solution.py:97
  35.2 26.1 %collective-permute-start.12 = (bf16[128,1536]{1,0:T(8,128)(2,1)}, bf16[128,1536]{1,0:T(8,128)(2,1)}, u32[]{:S(2)}, u32[]{:S(2)}) collective-permute-start(bf16[128,1536]{1,0:T(8,128)(2,1)} %collective-permute-done.9), channel_id=1, source_target_pairs={{0,8},{8,16},{16,24},{24,0},{1,9},{9,17},{17,25},{25,1},{2,10},{10... | collective-permute-start | bytes 1179656 | tf_op jit(solution)/shard_map/ppermute | solution.py:97
  40.2 24.2 %collective-permute-start.11 = (bf16[128,1536]{1,0:T(8,128)(2,1)}, bf16[128,1536]{1,0:T(8,128)(2,1)}, u32[]{:S(2)}, u32[]{:S(2)}) collective-permute-start(bf16[128,1536]{1,0:T(8,128)(2,1)} %collective-permute-done.8), channel_id=1, source_target_pairs={{0,8},{8,16},{16,24},{24,0},{1,9},{9,17},{17,25},{25,1},{2,10},{10... | collective-permute-start | bytes 1179656 | tf_op jit(solution)/shard_map/ppermute | solution.py:97
  44.6 0.9 copy-start.5
  44.6 3.2 %collective-permute-start.4 = (f32[512]{0:T(512)S(1)}, f32[512]{0:T(512)S(1)}, u32[]{:S(2)}, u32[]{:S(2)}) collective-permute-start(f32[512]{0:T(512)S(1)} %get-tuple-element.53), channel_id=1, source_target_pairs={{0,4},{4,0},{1,5},{5,1},{2,6},{6,2},{3,7},{7,3},{8,12},{12,8},{9,1... | collective-permute-start | bytes 6152 | tf_op jit(solution)/shard_map/ppermute | solution.py:83
  48.0 4.5 %copy-start.3 = (bf16[512,1536]{1,0:T(8,128)(2,1)S(1)}, bf16[512,1536]{1,0:T(8,128)(2,1)}, u32[]{:S(2)}) copy-start(bf16[512,1536]{1,0:T(8,128)(2,1)} %constant_dynamic-update-slice_fusion.1) | copy-start | bytes 4718596
  48.0 5.7 %copy-start.4 = (bf16[384,1536]{1,0:T(8,128)(2,1)S(1)}, bf16[384,1536]{1,0:T(8,128)(2,1)}, u32[]{:S(2)}) copy-start(bf16[384,1536]{1,0:T(8,128)(2,1)} %param.10) | copy-start | bytes 3538948
  49.5 20.0 %collective-permute-start.5 = (bf16[512,384]{0,1:T(8,128)(2,1)S(1)}, bf16[512,384]{0,1:T(8,128)(2,1)S(1)}, u32[]{:S(2)}, u32[]{:S(2)}) collective-permute-start(bf16[512,384]{0,1:T(8,128)(2,1)S(1)} %multiply_convert_fusion), channel_id=1, source_target_pairs={{0,3},{1,2},{2,1},{3,0},{4,7},{5,6},{6,5},{7,4},{8,11},{9,10},{10,... | collective-permute-start | bytes 1179656 | tf_op jit(solution)/shard_map/ppermute | solution.py:87
  52.0 20.3 %collective-permute-start.6 = (bf16[512,384]{0,1:T(8,128)(2,1)S(1)}, bf16[512,384]{0,1:T(8,128)(2,1)S(1)}, u32[]{:S(2)}, u32[]{:S(2)}) collective-permute-start(bf16[512,384]{0,1:T(8,128)(2,1)S(1)} %multiply_convert_fusion), channel_id=1, source_target_pairs={{0,2},{1,3},{2,0},{3,1},{4,6},{5,7},{6,4},{7,5},{8,10},{9,11},{10,... | collective-permute-start | bytes 1179656 | tf_op jit(solution)/shard_map/ppermute | solution.py:87
  59.1 13.2 %collective-permute-start.7 = (bf16[512,384]{0,1:T(8,128)(2,1)S(1)}, bf16[512,384]{0,1:T(8,128)(2,1)S(1)}, u32[]{:S(2)}, u32[]{:S(2)}) collective-permute-start(bf16[512,384]{0,1:T(8,128)(2,1)S(1)} %multiply_convert_fusion), channel_id=1, source_target_pairs={{0,1},{1,0},{2,3},{3,2},{4,5},{5,4},{6,7},{7,6},{8,9},{9,8},{10,11... | collective-permute-start | bytes 1179656 | tf_op jit(solution)/shard_map/ppermute | solution.py:87
  61.3 15.5 %collective-permute-start.16 = (bf16[128,1536]{1,0:T(8,128)(2,1)}, bf16[128,1536]{1,0:T(8,128)(2,1)S(1)}, u32[]{:S(2)}, u32[]{:S(2)}) collective-permute-start(bf16[128,1536]{1,0:T(8,128)(2,1)} %collective-permute-done.13), channel_id=1, source_target_pairs={{0,8},{8,16},{16,24},{24,0},{1,9},{9,17},{17,25},{25,1},{2,10},{10... | collective-permute-start | bytes 1179656 | tf_op jit(solution)/shard_map/ppermute | solution.py:97
  64.4 19.5 %collective-permute-start.15 = (bf16[128,1536]{1,0:T(8,128)(2,1)}, bf16[128,1536]{1,0:T(8,128)(2,1)S(1)}, u32[]{:S(2)}, u32[]{:S(2)}) collective-permute-start(bf16[128,1536]{1,0:T(8,128)(2,1)} %collective-permute-done.12), channel_id=1, source_target_pairs={{0,8},{8,16},{16,24},{24,0},{1,9},{9,17},{17,25},{25,1},{2,10},{10... | collective-permute-start | bytes 1179656 | tf_op jit(solution)/shard_map/ppermute | solution.py:97
  69.6 20.5 %collective-permute-start.14 = (bf16[128,1536]{1,0:T(8,128)(2,1)}, bf16[128,1536]{1,0:T(8,128)(2,1)S(1)}, u32[]{:S(2)}, u32[]{:S(2)}) collective-permute-start(bf16[128,1536]{1,0:T(8,128)(2,1)} %collective-permute-done.11), channel_id=1, source_target_pairs={{0,8},{8,16},{16,24},{24,0},{1,9},{9,17},{17,25},{25,1},{2,10},{10... | collective-permute-start | bytes 1179656 | tf_op jit(solution)/shard_map/ppermute | solution.py:97
  77.4 15.9 %collective-permute-start.25 = (bf16[512,128]{1,0:T(8,128)(2,1)S(1)}, bf16[512,128]{1,0:T(8,128)(2,1)S(1)}, u32[]{:S(2)}, u32[]{:S(2)}) collective-permute-start(bf16[512,128]{1,0:T(8,128)(2,1)S(1)} %get-tuple-element.33), channel_id=1, source_target_pairs={{0,1},{1,0},{2,3},{3,2},{4,5},{5,4},{6,7},{7,6},{8,9},{9,8},{10,11... | collective-permute-start | bytes 393224 | tf_op jit(solution)/shard_map/ppermute | solution.py:87
  79.0 15.8 %collective-permute-start.26 = (bf16[512,128]{1,0:T(8,128)(2,1)S(1)}, bf16[512,128]{1,0:T(8,128)(2,1)S(1)}, u32[]{:S(2)}, u32[]{:S(2)}) collective-permute-start(bf16[512,128]{1,0:T(8,128)(2,1)S(1)} %get-tuple-element.35), channel_id=1, source_target_pairs={{0,2},{1,3},{2,0},{3,1},{4,6},{5,7},{6,4},{7,5},{8,10},{9,11},{10,... | collective-permute-start | bytes 393224 | tf_op jit(solution)/shard_map/ppermute | solution.py:87
  80.5 14.9 %collective-permute-start.27 = (bf16[512,128]{1,0:T(8,128)(2,1)S(1)}, bf16[512,128]{1,0:T(8,128)(2,1)S(1)}, u32[]{:S(2)}, u32[]{:S(2)}) collective-permute-start(bf16[512,128]{1,0:T(8,128)(2,1)S(1)} %get-tuple-element.34), channel_id=1, source_target_pairs={{0,3},{1,2},{2,1},{3,0},{4,7},{5,6},{6,5},{7,4},{8,11},{9,10},{10,... | collective-permute-start | bytes 393224 | tf_op jit(solution)/shard_map/ppermute | solution.py:87
  84.4 12.5 %collective-permute-start.22 = (bf16[512,128]{1,0:T(8,128)(2,1)S(1)}, bf16[512,128]{1,0:T(8,128)(2,1)S(1)}, u32[]{:S(2)}, u32[]{:S(2)}) collective-permute-start(bf16[512,128]{1,0:T(8,128)(2,1)S(1)} %get-tuple-element.36), channel_id=1, source_target_pairs={{0,1},{1,0},{2,3},{3,2},{4,5},{5,4},{6,7},{7,6},{8,9},{9,8},{10,11... | collective-permute-start | bytes 393224 | tf_op jit(solution)/shard_map/ppermute | solution.py:87
  90.1 9.3 %collective-permute-start.23 = (bf16[512,128]{1,0:T(8,128)(2,1)S(1)}, bf16[512,128]{1,0:T(8,128)(2,1)S(1)}, u32[]{:S(2)}, u32[]{:S(2)}) collective-permute-start(bf16[512,128]{1,0:T(8,128)(2,1)S(1)} %get-tuple-element.38), channel_id=1, source_target_pairs={{0,2},{1,3},{2,0},{3,1},{4,6},{5,7},{6,4},{7,5},{8,10},{9,11},{10,... | collective-permute-start | bytes 393224 | tf_op jit(solution)/shard_map/ppermute | solution.py:87
  93.3 7.0 %collective-permute-start.24 = (bf16[512,128]{1,0:T(8,128)(2,1)S(1)}, bf16[512,128]{1,0:T(8,128)(2,1)S(1)}, u32[]{:S(2)}, u32[]{:S(2)}) collective-permute-start(bf16[512,128]{1,0:T(8,128)(2,1)S(1)} %get-tuple-element.37), channel_id=1, source_target_pairs={{0,3},{1,2},{2,1},{3,0},{4,7},{5,6},{6,5},{7,4},{8,11},{9,10},{10,... | collective-permute-start | bytes 393224 | tf_op jit(solution)/shard_map/ppermute | solution.py:87
  94.8 5.8 %collective-permute-start.19 = (bf16[512,128]{1,0:T(8,128)(2,1)S(1)}, bf16[512,128]{1,0:T(8,128)(2,1)S(1)}, u32[]{:S(2)}, u32[]{:S(2)}) collective-permute-start(bf16[512,128]{1,0:T(8,128)(2,1)S(1)} %get-tuple-element.39), channel_id=1, source_target_pairs={{0,1},{1,0},{2,3},{3,2},{4,5},{5,4},{6,7},{7,6},{8,9},{9,8},{10,11... | collective-permute-start | bytes 393224 | tf_op jit(solution)/shard_map/ppermute | solution.py:87
  95.4 8.2 %collective-permute-start.20 = (bf16[512,128]{1,0:T(8,128)(2,1)S(1)}, bf16[512,128]{1,0:T(8,128)(2,1)S(1)}, u32[]{:S(2)}, u32[]{:S(2)}) collective-permute-start(bf16[512,128]{1,0:T(8,128)(2,1)S(1)} %get-tuple-element.41), channel_id=1, source_target_pairs={{0,2},{1,3},{2,0},{3,1},{4,6},{5,7},{6,4},{7,5},{8,10},{9,11},{10,... | collective-permute-start | bytes 393224 | tf_op jit(solution)/shard_map/ppermute | solution.py:87
  97.0 6.5 %collective-permute-start.21 = (bf16[512,128]{1,0:T(8,128)(2,1)S(1)}, bf16[512,128]{1,0:T(8,128)(2,1)S(1)}, u32[]{:S(2)}, u32[]{:S(2)}) collective-permute-start(bf16[512,128]{1,0:T(8,128)(2,1)S(1)} %get-tuple-element.40), channel_id=1, source_target_pairs={{0,3},{1,2},{2,1},{3,0},{4,7},{5,6},{6,5},{7,4},{8,11},{9,10},{10,... | collective-permute-start | bytes 393224 | tf_op jit(solution)/shard_map/ppermute | solution.py:87
  104.8 1.9 %collective-permute-start.28 = (f32[512,1]{1,0:T(8,128)S(1)}, f32[512,1]{1,0:T(8,128)S(1)}, u32[]{:S(2)}, u32[]{:S(2)}) collective-permute-start(f32[512,1]{1,0:T(8,128)S(1)} %get-tuple-element.18.refs_1_), channel_id=1, source_target_pairs={{0,4},{4,0},{1,5},{5,1},{2,6},{6,2},{3,7},{7,3},{8,12},{12,8},{9,1... | collective-permute-start | bytes 6152 | tf_op jit(solution)/shard_map/ppermute | solution.py:83
  106.2 21.6 %collective-permute-start.17 = (f32[256,1536]{1,0:T(8,128)S(1)}, f32[256,1536]{1,0:T(8,128)S(1)}, u32[]{:S(2)}, u32[]{:S(2)}) collective-permute-start(f32[256,1536]{1,0:T(8,128)S(1)} %slice.40), channel_id=1, source_target_pairs={{0,4},{4,0},{1,5},{5,1},{2,6},{6,2},{3,7},{7,3},{8,12},{12,8},{9,1... | collective-permute-start | bytes 4718600 | tf_op jit(solution)/shard_map/ppermute | solution.py:83
  110.8 18.7 %collective-permute-start.30 = (f32[2,256,384]{2,1,0:T(8,128)S(1)}, f32[2,256,384]{2,1,0:T(8,128)S(1)}, u32[]{:S(2)}, u32[]{:S(2)}) collective-permute-start(f32[2,256,384]{2,1,0:T(8,128)S(1)} %get-tuple-element.25), channel_id=1, source_target_pairs={{0,4},{4,0},{1,5},{5,1},{2,6},{6,2},{3,7},{7,3},{8,12},{12,8},{9,1... | collective-permute-start | bytes 2359304 | tf_op jit(solution)/shard_map/ppermute | solution.py:83
  111.0 7.8 %collective-permute-start.31 = (bf16[3,128,128]{2,1,0:T(8,128)(2,1)S(1)}, bf16[3,128,128]{2,1,0:T(8,128)(2,1)S(1)}, u32[]{:S(2)}, u32[]{:S(2)}) collective-permute-start(bf16[3,128,128]{2,1,0:T(8,128)(2,1)S(1)} %get-tuple-element.26), channel_id=1, source_target_pairs={{8,0},{16,8},{24,16},{9,1},{17,9},{25,17},{10,2},{18,10},{26,18},{... | collective-permute-start | bytes 294920 | tf_op jit(solution)/shard_map/ppermute | solution.py:92
  112.3 12.5 %collective-permute-start.32 = (bf16[3,128,128]{2,1,0:T(8,128)(2,1)S(1)}, bf16[3,128,128]{2,1,0:T(8,128)(2,1)S(1)}, u32[]{:S(2)}, u32[]{:S(2)}) collective-permute-start(bf16[3,128,128]{2,1,0:T(8,128)(2,1)S(1)} %get-tuple-element.26), channel_id=1, source_target_pairs={{16,0},{24,8},{17,1},{25,9},{18,2},{26,10},{19,3},{27,11},{20,4},{... | collective-permute-start | bytes 294920 | tf_op jit(solution)/shard_map/ppermute | solution.py:92
  113.6 14.2 %collective-permute-start.29 = (bf16[256,384]{1,0:T(8,128)(2,1)S(1)}, bf16[256,384]{1,0:T(8,128)(2,1)S(1)}, u32[]{:S(2)}, u32[]{:S(2)}) collective-permute-start(bf16[256,384]{1,0:T(8,128)(2,1)S(1)} %get-tuple-element.21), channel_id=1, source_target_pairs={{0,4},{4,0},{1,5},{5,1},{2,6},{6,2},{3,7},{7,3},{8,12},{12,8},{9,1... | collective-permute-start | bytes 589832 | tf_op jit(solution)/shard_map/ppermute | solution.py:83
  118.8 8.3 %collective-permute-start.33 = (bf16[3,128,128]{2,1,0:T(8,128)(2,1)S(1)}, bf16[3,128,128]{2,1,0:T(8,128)(2,1)S(1)}, u32[]{:S(2)}, u32[]{:S(2)}) collective-permute-start(bf16[3,128,128]{2,1,0:T(8,128)(2,1)S(1)} %get-tuple-element.26), channel_id=1, source_target_pairs={{24,0},{25,1},{26,2},{27,3},{28,4},{29,5},{30,6},{31,7}} | collective-permute-start | bytes 294920 | tf_op jit(solution)/shard_map/ppermute | solution.py:92
  127.7 1.8 %collective-permute-start.34 = (bf16[3,128,128]{2,1,0:T(8,128)(2,1)S(1)}, bf16[3,128,128]{2,1,0:T(8,128)(2,1)S(1)}, u32[]{:S(2)}, u32[]{:S(2)}) collective-permute-start(bf16[3,128,128]{2,1,0:T(8,128)(2,1)S(1)} %sum_later.1.refs_4_), channel_id=1, source_target_pairs={{0,4},{4,0},{1,5},{5,1},{2,6},{6,2},{3,7},{7,3},{8,12},{12,8},{9,1... | collective-permute-start | bytes 294920 | tf_op jit(solution)/shard_map/ppermute | solution.py:83
